TPU v7x, 32 devices: a whole 2x2x4 slice. The times are simulated.
32 devices in a mesh: groups: 2 (over y), section: 4 (over z), tp: 2 (over core), sp: 2 (over x).
Axes of the slice: x: 2, y: 2, z: 4, core: 2. Of those that a mesh axis runs over, the one named last changes fastest.
Arguments:
- hidden: bfloat16 [1024, 6144], P(('groups', 'sp', 'section'), 'tp'), parts along dimension 0, may hold values from -6 to 6
- modulation: float32 [2, 6144], P(None, 'tp'), may hold values from -2 to 2
- time_embed: float32 [12288], P(('groups', 'tp')), parts along dimension 0, may hold values from -2 to 2
- head_weight: bfloat16 [6144, 64], P('tp'), may hold values from -0.078125 to 0.078125
- head_bias: float32 [64], replicated, may hold values from -2 to 2
- noisy: bfloat16 [16, 16, 16, 16], P(('groups', 'sp'), None, 'section'), parts along dimension 0, may hold values from -6 to 6
- step_size: float32 [2], P('groups'), parts along dimension 0, may hold values from 0.2 to 0.6
- latent_mean: float32 [16], replicated, may hold values from -2 to 2
- latent_std: float32 [16], replicated, may hold values from 0.5 to 2
- in_weight: bfloat16 [27, 16, 512], P(None, None, 'tp'), may hold values from -0.3125 to 0.3125
- in_bias: float32 [512], P('tp'), may hold values from -2 to 2
- norm_gain: float32 [512], replicated, may hold values from 0.25 to 1.75
- conv_weight: bfloat16 [27, 512, 512], P(None, 'section', 'tp'), may hold values from -0.0546875 to 0.0546875
- conv_bias: float32 [512], P('tp'), may hold values from -2 to 2
Outputs:
- decoded: bfloat16 [16, 16, 16, 512], P(('groups', 'sp'), None, 'section', 'tp'), parts along dimension 0
There are 2 independent parts, one for each index of `groups`. A program takes and returns all parts, laid end to end along the dimension named above; an argument that names none is the same for every part. Nothing has to cross between parts.
All inputs are finite; a program needn't handle non-finite values.
Results may differ from a plain program's by a relative error of at most 0.006.
Values may be sent and summed in bfloat16 or wider, within the bound.
No kernel may reach another device: no remote copies, remote signals or barrier semaphores. Data moves between devices by JAX's collectives and lax.ppermute only.
A program may use at most 128 MiB of HBM per device.

v0:
```python
import jax
import jax.numpy as jnp
from jax import lax
from jax.sharding import PartitionSpec as P

D = 6144


def padded_2(value, sides, width):
    for axis, dim in sides:
        count, length = (lax.axis_size(axis), value.shape[dim])
        up = [(i, (i + 1) % count) for i in range(count - 1)]
        down = [(j, i) for i, j in up]
        last = lax.slice_in_dim(value, length - width, length, axis=dim)
        leading = lax.slice_in_dim(value, 0, width, axis=dim)
        before = lax.ppermute(last, axis, up)
        after = lax.ppermute(leading, axis, down)
        value = jnp.concatenate([before, value, after], axis=dim)
    return value


def passed_along(value, axis, by):
    count = lax.axis_size(axis)
    pairs = [(i, i + by) for i in range(count) if 0 <= i + by < count]
    return lax.ppermute(value, axis, pairs)


def conv_taps(padded, weight, frames, height, columns):
    channels = padded.shape[3]
    result = jnp.zeros((frames * height * columns, weight.shape[2]), jnp.float32)
    for offset_time in range(3):
        for offset_row in range(3):
            slab = padded[offset_time : offset_time + frames, offset_row : offset_row + height]
            window = jnp.concatenate(
                [slab[:, :, 0:columns], slab[:, :, 1 : columns + 1], slab[:, :, 2 : columns + 2]],
                axis=3,
            )
            first = 9 * offset_time + 3 * offset_row
            taps = weight[first : first + 3].reshape(3 * channels, weight.shape[2])
            result = result + jnp.dot(
                window.reshape(-1, 3 * channels), taps, preferred_element_type=jnp.float32
            )
    return result


def activate(source, gain_vector):
    values = source.astype(jnp.float32)
    squares = jnp.mean(values * values, axis=-1, keepdims=True)
    return jax.nn.silu(values * lax.rsqrt(squares + 1e-06) * gain_vector).astype(jnp.bfloat16)


def pad_rows(source):
    return jnp.pad(source, ((0, 0), (1, 1), (0, 0), (0, 0)))


def shards(
    hidden,
    modulation,
    time_embed,
    head_weight,
    head_bias,
    noisy,
    step_size,
    latent_mean,
    latent_std,
    in_weight,
    in_bias,
    norm_gain,
    conv_weight,
    conv_bias,
):
    frames, height, columns, lat_channels = noisy.shape
    sections = lax.axis_size("section")
    half_channels = in_weight.shape[2]
    values = hidden.astype(jnp.float32)
    row_sums, square_sums = lax.psum(
        (jnp.sum(values, axis=1), jnp.sum(values * values, axis=1)), "tp"
    )
    average = row_sums / D
    variance = square_sums / D - average * average
    shift_term = modulation[0] + time_embed
    scale_term = modulation[1] + time_embed
    modulated = (
        (values - average[:, None]) * lax.rsqrt(variance[:, None] + 1e-06) * (1.0 + scale_term)
        + shift_term
    ).astype(jnp.bfloat16)
    partial_sum = jnp.dot(modulated, head_weight, preferred_element_type=jnp.float32)
    velocity = (lax.psum(partial_sum, "tp") + head_bias).astype(jnp.bfloat16)
    band_rows = velocity.shape[0] * 2 // (columns * sections)
    outgoing = velocity.reshape(band_rows, sections, -1)
    arrived = lax.all_to_all(outgoing, "section", split_axis=1, concat_axis=0, tiled=True)
    latent_field = arrived.reshape(frames, height // 2, columns // 2, 2, 2, lat_channels)
    latent_field = jnp.transpose(latent_field, (0, 1, 3, 2, 4, 5)).reshape(
        frames, height, columns, lat_channels
    )
    latent = (
        (noisy.astype(jnp.float32) - step_size[0] * latent_field.astype(jnp.float32)) * latent_std
        + latent_mean
    ).astype(jnp.bfloat16)
    latent_wide = padded_2(latent, (("section", 2),), 2)
    earlier = passed_along(latent_wide, "sp", 1)
    stacked = pad_rows(jnp.concatenate([earlier, latent_wide], axis=0))
    extended = (conv_taps(stacked, in_weight, frames + 2, height, columns + 2) + in_bias).astype(
        jnp.bfloat16
    )
    extended = extended.reshape(frames + 2, height, columns + 2, half_channels)
    upblock_half = extended[2:, :, 1 : columns + 1]
    extended_full = lax.all_gather(extended, "tp", axis=3, tiled=True)
    normed = activate(extended_full, norm_gain)
    frame_index = lax.axis_index("sp") * frames - 2 + jnp.arange(frames + 2, dtype=jnp.int32)
    column_index = (
        lax.axis_index("section") * columns - 1 + jnp.arange(columns + 2, dtype=jnp.int32)
    )
    inside_cols = (column_index >= 0) & (column_index < columns * sections)
    inside = (frame_index >= 0)[:, None, None, None] & inside_cols[None, None, :, None]
    conv_input = pad_rows(jnp.where(inside, normed, jnp.zeros_like(normed)))
    full_weight = lax.all_gather(conv_weight, "section", axis=1, tiled=True)
    mixed = conv_taps(conv_input, full_weight, frames, height, columns)
    decoded = (
        upblock_half.astype(jnp.float32).reshape(-1, half_channels) + mixed + conv_bias
    ).astype(jnp.bfloat16)
    return decoded.reshape(frames, height, columns, half_channels)


def solution(mesh):
    placed = (
        P(("groups", "sp", "section"), "tp"),
        P(None, "tp"),
        P(("groups", "tp")),
        P("tp", None),
        P(),
        P(("groups", "sp"), None, "section", None),
        P("groups"),
        P(),
        P(),
        P(None, None, "tp"),
        P("tp"),
        P(),
        P(None, "section", "tp"),
        P("tp"),
    )
    return jax.shard_map(
        shards,
        mesh=mesh,
        in_specs=placed,
        out_specs=P(("groups", "sp"), None, "section", "tp"),
        check_vma=False,
    )
```

profile of v0, /device:TPU:0, one launch (start us, length us, event | category | flops | bytes accessed | tf_op | source)
XLA Modules:
  0.0 158.0 jit_solution(14631500808163563009)
XLA Ops:
  7.8 2.6 %all-reduce.2 = (f32[64]{0:T(128)S(1)}, f32[64]{0:T(128)S(1)}) all-reduce(f32[64]{0:T(128)S(1)} %get-tuple-element.6, f32[64]{0:T(128)S(1)} %get-tuple-element.5), channel_id=1, replica_groups=mesh['groups'=2,'section'=4,'tp'=2,'sp'=2] {'tp'}, use_global_device_ids=true, to_apply=%region_3.0 | all-reduce | flops 128 | bytes 1024 | tf_op jit(solution)/shard_map/psum | solution.py:76
  10.8 3.6 %psum.23 = f32[64,64]{1,0:T(8,128)S(1)} all-reduce(f32[64,64]{1,0:T(8,128)S(1)} %fusion.19), channel_id=1, replica_groups=mesh['groups'=2,'section'=4,'tp'=2,'sp'=2] {'tp'}, use_global_device_ids=true, to_apply=%region_4.0 | all-reduce | flops 4096 | bytes 32768 | tf_op jit(solution)/shard_map/psum | solution.py:88
  15.1 6.0 %all-to-all-start = ((bf16[8,4,128]{2,0,1:T(8,128)(2,1)}), bf16[8,4,128]{2,0,1:T(8,128)(2,1)S(1)}, u32[]{:S(2)}, u32[]{:S(2)}) async-start(bf16[8,4,128]{2,0,1:T(8,128)(2,1)} %copy.17), calls=%async_computation | async-start | bytes 16384 | tf_op jit(solution)/shard_map/all_to_all | solution.py:91
  22.5 7.5 %all-to-all-done = bf16[8,4,128]{2,0,1:T(8,128)(2,1)S(1)} async-done(((bf16[8,4,128]{2,0,1:T(8,128)(2,1)}), bf16[8,4,128]{2,0,1:T(8,128)(2,1)S(1)}, u32[]{:S(2)}, u32[]{:S(2)}) %all-to-all-start) | async-done | bytes 8224 | tf_op jit(solution)/shard_map/all_to_all | solution.py:91
  30.4 1.3 collective-permute-start
  31.7 1.3 collective-permute-start.1
  33.9 4.4 %collective-permute-done.1 = bf16[4,16,2,16]{3,2,1,0:T(2,128)(2,1)S(1)} collective-permute-done((bf16[4,16,2,16]{3,2,1,0:T(2,128)(2,1)S(1)}, bf16[4,16,2,16]{3,2,1,0:T(2,128)(2,1)S(1)}, u32[]{:S(2)}, u32[]{:S(2)}) %collective-permute-start.1) | collective-permute-done | bytes 4128 | tf_op jit(solution)/shard_map/ppermute | solution.py:17
  38.5 3.4 %collective-permute-start.2 = (bf16[4,16,8,16]{3,2,1,0:T(8,128)(2,1)S(1)}, bf16[4,16,8,16]{3,2,1,0:T(8,128)(2,1)S(1)}, u32[]{:S(2)}, u32[]{:S(2)}) collective-permute-start(bf16[4,16,8,16]{3,2,1,0:T(8,128)(2,1)S(1)} %pad_maximum_fusion.18), channel_id=1, source_target_pairs={{0,1},{2,3},{4,5},{6,7},{8,9},{10,11},{12,13},{14,15},{16,17},{18,... | collective-permute-start | bytes 49160 | tf_op jit(solution)/shard_map/ppermute | solution.py:25
  42.5 1.9 %collective-permute-done.2 = bf16[4,16,8,16]{3,2,1,0:T(8,128)(2,1)S(1)} collective-permute-done((bf16[4,16,8,16]{3,2,1,0:T(8,128)(2,1)S(1)}, bf16[4,16,8,16]{3,2,1,0:T(8,128)(2,1)S(1)}, u32[]{:S(2)}, u32[]{:S(2)}) %collective-permute-start.2) | collective-permute-done | bytes 16416 | tf_op jit(solution)/shard_map/ppermute | solution.py:25
  44.8 1.0 pad_slice_fusion.2
  47.1 1.3 pad_slice_fusion.1
  48.3 1.1 pad_maximum_fusion.10
  50.2 2.2 %pad_maximum_fusion.12 = (bf16[6,16,6,48]{3,2,1,0:T(8,128)(2,1)}, bf16[6,16,6,48]{3,2,1,0:T(8,128)(2,1)S(1)}) fusion(bf16[6,16,6,16]{3,2,1,0:T(8,128)(2,1)S(1)} %get-tuple-element.53, bf16[6,16,6,16]{3,2,1,0:T(8,128)(2,1)S(1)} %get-tuple-element.52, bf16[6,16,6,16]{3,2,1,0:T(8,128)(2,1)S(1)} %get-tuple-element.51, ...), kind=kLoop, calls=%fused_computation.58 | loop fusion | flops 331776 | bytes 221184 | tf_op jit(solution)/shard_map/concatenate | solution.py:34
  52.4 1.7 %reshape.204 = bf16[576,48]{1,0:T(8,128)(2,1)} reshape(bf16[6,16,6,48]{3,2,1,0:T(8,128)(2,1)} %get-tuple-element.91) | data formatting | bytes 110592 | tf_op jit(solution)/shard_map/reshape | solution.py:41
  59.0 2.5 %all_gather.6 = bf16[6,16,6,512]{3,2,1,0:T(8,128)(2,1)S(1)} all-gather(bf16[6,16,6,256]{3,2,1,0:T(8,128)(2,1)S(1)} %reshape.216), channel_id=1, replica_groups=mesh['groups'=2,'section'=4,'tp'=2,'sp'=2] {'tp'}, dimensions={3}, use_global_device_ids=true | all-gather | bytes 884736 | tf_op jit(solution)/shard_map/all_gather | solution.py:108
  62.4 1.4 fusion.26
  64.3 2.3 %pad_slice_fusion.20 = (bf16[4,16,4,512]{3,2,1,0:T(4,128)(2,1)}, bf16[4,16,4,512]{3,2,1,0:T(4,128)(2,1)S(1)}, bf16[4,16,4,512]{3,2,1,0:T(4,128)(2,1)S(1)}, bf16[...) fusion(bf16[6,16,6,512]{3,2,1,0:T(8,128)(2,1)S(1)} %fusion.18), kind=kLoop, calls=%fused_computation.96 | loop fusion | bytes 3670016 | tf_op jit(solution)/shard_map/slice | solution.py:35
  67.2 1.5 pad_maximum_fusion.2
  68.6 1.1 reshape.223
  69.8 1.5 pad_maximum_fusion.3
  71.2 1.1 reshape.225
  72.4 2.5 %pad_slice_fusion.19 = (bf16[4,16,4,512]{3,2,1,0:T(4,128)(2,1)S(1)}, bf16[4,16,4,512]{3,2,1,0:T(4,128)(2,1)}, bf16[4,16,4,512]{3,2,1,0:T(4,128)(2,1)}, bf16[4,16...) fusion(bf16[6,16,6,512]{3,2,1,0:T(8,128)(2,1)S(1)} %fusion.18), kind=kLoop, calls=%fused_computation.95 | loop fusion | bytes 4456448 | tf_op jit(solution)/shard_map/slice | solution.py:35
  75.4 1.5 pad_maximum_fusion.4
  76.8 1.1 reshape.227
  77.9 1.5 pad_maximum_fusion.7
  79.4 1.1 reshape.233
  80.4 1.4 pad_maximum_fusion.5
  81.9 1.1 reshape.229
  82.9 1.4 pad_maximum_fusion.6
  84.4 1.1 reshape.231
  85.5 55.2 %all-gather.2.cloned.1.call-done = bf16[27,512,256]{2,1,0:T(8,128)(2,1)} async-done(((bf16[27,128,256]{2,1,0:T(8,128)(2,1)}), bf16[27,512,256]{2,1,0:T(8,128)(2,1)}) %all-gather.2.cloned.1.call-update) | async-done | bytes 7077904 | tf_op jit(solution)/shard_map/all_gather | solution.py:117
  140.7 3.8 %fusion.25 = (bf16[3,512,256]{2,1,0:T(8,128)(2,1)S(1)}, bf16[3,512,256]{2,1,0:T(8,128)(2,1)S(1)}, bf16[3,512,256]{2,1,0:T(8,128)(2,1)S(1)}, bf16[3,512,256]{2,1,...) fusion(bf16[27,512,256]{2,1,0:T(8,128)(2,1)} %all-gather.2.clon, ...), kind=kLoop, calls=%fused_computation.112 | loop fusion | bytes 14155776 | tf_op jit(solution)/shard_map/slice | solution.py:39
  (142 shorter events, 21.1 us)
Async XLA Ops:
  6.5 3.9 %copy-start = (bf16[3072,64]{0,1:T(8,128)(2,1)S(1)}, bf16[3072,64]{0,1:T(8,128)(2,1)}, u32[]{:S(2)}) copy-start(bf16[3072,64]{0,1:T(8,128)(2,1)} %param.17) | copy-start | bytes 1179652
  6.5 1.1 copy-start.18
  6.5 3.9 %copy-start.31 = (f32[3072]{0:T(1024)S(1)}, f32[3072]{0:T(1024)}, u32[]{:S(2)}) copy-start(f32[3072]{0:T(1024)} %param.16) | copy-start | bytes 36868
  6.5 7.9 %copy-start.36 = (f32[64]{0:T(128)S(1)}, f32[64]{0:T(128)}, u32[]{:S(2)}) copy-start(f32[64]{0:T(128)} %param.18) | copy-start | bytes 772
  6.5 14.6 %copy-start.19 = (bf16[27,16,256]{2,1,0:T(8,128)(2,1)S(1)}, bf16[27,16,256]{2,1,0:T(8,128)(2,1)}, u32[]{:S(2)}) copy-start(bf16[27,16,256]{2,1,0:T(8,128)(2,1)} %param.23) | copy-start | bytes 663556
  6.6 134.1 %all-gather.2.cloned.1.call-start = ((), (), s32[]{:S(2)}) async-start(), calls=%async_computation.1 | async-start | bytes 8847360 | tf_op jit(solution)/shard_map/all_gather | solution.py:117
  7.3 22.9 %copy-start.29 = (bf16[4,16,4,16]{3,2,1,0:T(4,128)(2,1)S(1)}, bf16[4,16,4,16]{3,2,1,0:T(4,128)(2,1)}, u32[]{:S(2)}) copy-start(bf16[4,16,4,16]{3,2,1,0:T(4,128)(2,1)} %param.19) | copy-start | bytes 24580
  7.3 22.9 %copy-start.37 = (f32[16]{0:T(128)S(1)}, f32[16]{0:T(128)}, u32[]{:S(2)}) copy-start(f32[16]{0:T(128)} %param.21) | copy-start | bytes 196
  7.3 23.0 %copy-start.38 = (f32[16]{0:T(128)S(1)}, f32[16]{0:T(128)}, u32[]{:S(2)}) copy-start(f32[16]{0:T(128)} %param.22) | copy-start | bytes 196
  15.1 14.9 %all-to-all-start = ((bf16[8,4,128]{2,0,1:T(8,128)(2,1)}), bf16[8,4,128]{2,0,1:T(8,128)(2,1)S(1)}, u32[]{:S(2)}, u32[]{:S(2)}) async-start(bf16[8,4,128]{2,0,1:T(8,128)(2,1)} %copy.17), calls=%async_computation | async-start | bytes 16384 | tf_op jit(solution)/shard_map/all_to_all | solution.py:91
  30.4 3.5 %collective-permute-start = (bf16[4,16,2,16]{3,2,1,0:T(2,128)(2,1)S(1)}, bf16[4,16,2,16]{3,2,1,0:T(2,128)(2,1)S(1)}, u32[]{:S(2)}, u32[]{:S(2)}) collective-permute-start(bf16[4,16,2,16]{3,2,1,0:T(2,128)(2,1)S(1)} %get-tuple-element.81), channel_id=1, source_target_pairs={{0,4},{4,8},{8,12},{1,5},{5,9},{9,13},{2,6},{6,10},{10,14},{3,7},{... | collective-permute-start | bytes 12296 | tf_op jit(solution)/shard_map/ppermute | solution.py:16
  31.7 6.6 %collective-permute-start.1 = (bf16[4,16,2,16]{3,2,1,0:T(2,128)(2,1)S(1)}, bf16[4,16,2,16]{3,2,1,0:T(2,128)(2,1)S(1)}, u32[]{:S(2)}, u32[]{:S(2)}) collective-permute-start(bf16[4,16,2,16]{3,2,1,0:T(2,128)(2,1)S(1)} %get-tuple-element.82), channel_id=1, source_target_pairs={{4,0},{8,4},{12,8},{5,1},{9,5},{13,9},{6,2},{10,6},{14,10},{7,3},{... | collective-permute-start | bytes 12296 | tf_op jit(solution)/shard_map/ppermute | solution.py:17
  38.5 5.9 %collective-permute-start.2 = (bf16[4,16,8,16]{3,2,1,0:T(8,128)(2,1)S(1)}, bf16[4,16,8,16]{3,2,1,0:T(8,128)(2,1)S(1)}, u32[]{:S(2)}, u32[]{:S(2)}) collective-permute-start(bf16[4,16,8,16]{3,2,1,0:T(8,128)(2,1)S(1)} %pad_maximum_fusion.18), channel_id=1, source_target_pairs={{0,1},{2,3},{4,5},{6,7},{8,9},{10,11},{12,13},{14,15},{16,17},{18,... | collective-permute-start | bytes 49160 | tf_op jit(solution)/shard_map/ppermute | solution.py:25
  49.4 4.6 %copy-start.11 = (bf16[6,16,6,16]{3,2,1,0:T(8,128)(2,1)S(1)}, bf16[6,16,6,16]{3,2,1,0:T(8,128)(2,1)}, u32[]{:S(2)}) copy-start(bf16[6,16,6,16]{3,2,1,0:T(8,128)(2,1)} %get-tuple-element.45) | copy-start | bytes 55300
  49.4 4.6 %copy-start.12 = (bf16[6,16,6,16]{3,2,1,0:T(8,128)(2,1)S(1)}, bf16[6,16,6,16]{3,2,1,0:T(8,128)(2,1)}, u32[]{:S(2)}) copy-start(bf16[6,16,6,16]{3,2,1,0:T(8,128)(2,1)} %get-tuple-element.55) | copy-start | bytes 55300
  49.4 4.6 %copy-start.13 = (bf16[6,16,6,16]{3,2,1,0:T(8,128)(2,1)S(1)}, bf16[6,16,6,16]{3,2,1,0:T(8,128)(2,1)}, u32[]{:S(2)}) copy-start(bf16[6,16,6,16]{3,2,1,0:T(8,128)(2,1)} %get-tuple-element.62) | copy-start | bytes 55300
  50.2 4.3 %copy-start.14 = (bf16[6,16,6,48]{3,2,1,0:T(8,128)(2,1)S(1)}, bf16[6,16,6,48]{3,2,1,0:T(8,128)(2,1)}, u32[]{:S(2)}) copy-start(bf16[6,16,6,48]{3,2,1,0:T(8,128)(2,1)} %get-tuple-element.94) | copy-start | bytes 165892
  50.2 4.4 %copy-start.10 = (bf16[6,16,6,16]{3,2,1,0:T(8,128)(2,1)S(1)}, bf16[6,16,6,16]{3,2,1,0:T(8,128)(2,1)}, u32[]{:S(2)}) copy-start(bf16[6,16,6,16]{3,2,1,0:T(8,128)(2,1)} %get-tuple-element.61) | copy-start | bytes 55300
  54.3 1.0 copy-start.15
  54.3 1.0 copy-start.20
  58.1 3.7 %copy-start.32 = (pred[6,6]{1,0:T(8,128)(4,1)S(1)}, pred[6,6]{1,0:T(8,128)(4,1)}, u32[]{:S(2)}) copy-start(pred[6,6]{1,0:T(8,128)(4,1)} %broadcast_and_fusion) | copy-start | bytes 112
  58.1 3.7 %copy-start.33 = (f32[512]{0:T(512)S(1)}, f32[512]{0:T(512)}, u32[]{:S(2)}) copy-start(f32[512]{0:T(512)} %param.25) | copy-start | bytes 6148
  64.3 2.3 %copy-start.8 = (bf16[4,16,4,512]{3,2,1,0:T(4,128)(2,1)S(1)}, bf16[4,16,4,512]{3,2,1,0:T(4,128)(2,1)}, u32[]{:S(2)}) copy-start(bf16[4,16,4,512]{3,2,1,0:T(4,128)(2,1)} %get-tuple-element.44) | copy-start | bytes 786436
  72.4 2.5 %copy-start.7 = (bf16[4,16,4,512]{3,2,1,0:T(4,128)(2,1)S(1)}, bf16[4,16,4,512]{3,2,1,0:T(4,128)(2,1)}, u32[]{:S(2)}) copy-start(bf16[4,16,4,512]{3,2,1,0:T(4,128)(2,1)} %get-tuple-element.18) | copy-start | bytes 786436
  144.4 1.1 copy-start.1
  145.2 1.2 copy-start.2
  146.0 1.2 copy-start.4
  146.8 1.2 copy-start.5
  147.5 1.2 copy-start.6
  148.3 1.2 copy-start.3
  149.1 1.0 copy-start.9
  149.1 1.0 copy-start.35
  (12 other events, 9.8 us)
Sparse Core Ops, SparseCore 0:
  8.9 131.6 all-gather.1
where the time goes:
time: 159 us; the launch traced here: 158 us
  waiting for transfers between devices  70.6 us (44%)
  local copies, waits for them, and re-layouts  30.1 us (19%)
  other arithmetic  16.3 us (10%)
  between operations  14.7 us (9%)
  starting transfers between devices  12 us (8%)
  blocking collectives  8.74 us (5%)
  matrix products  5.53 us (3%)
    all_gather x1, waiting for transfers between devices, shards(): full_weight = lax.all_gather(conv_weight, 'section', axis=1, tiled=True)  55.2 us
    concatenate x14, other arithmetic, conv_taps(): jnp.concatenate([slab[:, :, 0:columns], slab[:, :, 1:columns + 1], slab[:...  14.1 us
    reshape x18, local copies, waits for them, and re-layouts, conv_taps(): window.reshape(-1, 3 * channels)  10.7 us
    all_to_all x1, waiting for transfers between devices, shards(): lax.all_to_all(outgoing, 'section', split_axis=1, concat_axis=0, tiled=True)  7.51 us
    all_to_all x1, starting transfers between devices, shards(): lax.all_to_all(outgoing, 'section', split_axis=1, concat_axis=0, tiled=True)  6.02 us
    dot_general x18, matrix products, conv_taps(): jnp.dot(window.reshape(-1, 3 * channels), taps, preferred_element_type=jn...  5.17 us
    slice x4, local copies, waits for them, and re-layouts, conv_taps(): slab[:, :, 0:columns]  4.94 us
    slice x2, local copies, waits for them, and re-layouts, conv_taps(): taps = weight[first:first + 3].reshape(3 * channels, weight.shape[2])  4.44 us
  transfers between devices with their start and end apart: 5, of which 5 were waited for; matrix products, arithmetic and copies ran while one was open for 26% of the time, Pallas kernels for 0%

commit v1 on v0

--- a/solution.py
+++ b/solution.py
@@ -1,9 +1,13 @@
 import jax
 import jax.numpy as jnp
+import numpy as np
 from jax import lax
+from jax.experimental import pallas as pl
+from jax.experimental.pallas import tpu as pltpu
 from jax.sharding import PartitionSpec as P
 
-D = 6144
+F32 = jnp.float32
+BF16 = jnp.bfloat16
 
 
 def padded_2(value, sides, width):
@@ -53,31 +57,20 @@
     return jnp.pad(source, ((0, 0), (1, 1), (0, 0), (0, 0)))
 
 
-def shards(
-    hidden,
-    modulation,
-    time_embed,
-    head_weight,
-    head_bias,
-    noisy,
-    step_size,
-    latent_mean,
-    latent_std,
-    in_weight,
-    in_bias,
-    norm_gain,
-    conv_weight,
-    conv_bias,
+def general_shards(
+    hidden, modulation, time_embed, head_weight, head_bias, noisy, step_size,
+    latent_mean, latent_std, in_weight, in_bias, norm_gain, conv_weight, conv_bias,
 ):
     frames, height, columns, lat_channels = noisy.shape
     sections = lax.axis_size("section")
     half_channels = in_weight.shape[2]
+    features = hidden.shape[1] * lax.axis_size("tp")
     values = hidden.astype(jnp.float32)
     row_sums, square_sums = lax.psum(
         (jnp.sum(values, axis=1), jnp.sum(values * values, axis=1)), "tp"
     )
-    average = row_sums / D
-    variance = square_sums / D - average * average
+    average = row_sums / features
+    variance = square_sums / features - average * average
     shift_term = modulation[0] + time_embed
     scale_term = modulation[1] + time_embed
     modulated = (
@@ -120,6 +113,310 @@
         upblock_half.astype(jnp.float32).reshape(-1, half_channels) + mixed + conv_bias
     ).astype(jnp.bfloat16)
     return decoded.reshape(frames, height, columns, half_channels)
+
+
+def head_kernel(hidden, modulation, time_embed, weight, in_bias, out):
+    tokens = hidden.shape[0]
+    outs = weight.shape[1]
+    x = hidden[...].astype(F32)
+    embed = time_embed[...]
+    scale = 1.0 + (modulation[1:2, :] + embed)
+    shift = modulation[0:1, :] + embed
+    scaled = x * scale
+    high = scaled.astype(BF16)
+    low = (scaled - high.astype(F32)).astype(BF16)
+    row = lax.broadcasted_iota(jnp.int32, (16, x.shape[1]), 0)
+    scale_high = scale.astype(BF16).astype(F32)
+    shift_high = shift.astype(BF16).astype(F32)
+    extra = jnp.where(row == 0, scale_high, 0.0)
+    extra = jnp.where(row == 1, scale - scale_high, extra)
+    extra = jnp.where(row == 2, shift_high, extra)
+    extra = jnp.where(row == 3, shift - shift_high, extra).astype(BF16)
+    stacked = jnp.concatenate([high, low, extra], axis=0)
+    sums = jnp.dot(stacked, weight[...], preferred_element_type=F32)
+    out[0:tokens, 0:outs] = sums[0:tokens] + sums[tokens : 2 * tokens]
+    first = jnp.sum(x, axis=1, keepdims=True)
+    second = jnp.sum(x * x, axis=1, keepdims=True)
+    lane = lax.broadcasted_iota(jnp.int32, (tokens, outs), 1)
+    out[0:tokens, outs : 2 * outs] = jnp.where(lane == 0, first, second)
+    base = 2 * tokens
+    out[tokens : tokens + 1, 0:outs] = sums[base : base + 1] + sums[base + 1 : base + 2]
+    out[tokens : tokens + 1, outs : 2 * outs] = sums[base + 2 : base + 3] + sums[base + 3 : base + 4]
+    biases = in_bias.shape[0]
+    out[tokens + 1 : tokens + 1 + biases, :] = in_bias[...]
+    rest = out.shape[0] - tokens - 1 - biases
+    out[tokens + 1 + biases :, :] = jnp.zeros((rest, out.shape[1]), F32)
+
+
+def message_kernel(mine, other, bias, place, noisy, out, *, features, cells, channels):
+    tokens, outs = place.shape[0], bias.shape[1]
+    total = mine[...] + other[...]
+    average = total[0:tokens, outs : outs + 1] / features
+    variance = total[0:tokens, outs + 1 : outs + 2] / features - average * average
+    inverse = lax.rsqrt(variance + 1e-06)
+    scale_sum = total[tokens : tokens + 1, 0:outs]
+    shift_sum = total[tokens : tokens + 1, outs : 2 * outs]
+    velocity = inverse * (total[0:tokens, 0:outs] - average * scale_sum) + (shift_sum + bias[...])
+    velocity = velocity.astype(BF16)
+    spread = lax.dot_general(
+        velocity, place[...], (((0,), (0,)), ((), ())), preferred_element_type=F32
+    )
+    field = spread[0:channels, 0:cells]
+    for part in range(1, outs // channels):
+        field = field + spread[
+            part * channels : (part + 1) * channels, part * cells : (part + 1) * cells
+        ]
+    out[:, 0:cells] = field.astype(BF16)
+    out[:, cells:] = noisy[...]
+
+
+def latent_kernel(where, step, *refs, sections, cells):
+    messages, (std, mean, out, ordered) = refs[:sections], refs[sections:]
+    mine = where[0]
+    for k in range(sections):
+        ordered[mine ^ k] = messages[k][...].astype(F32)
+    tile = cells // sections
+    for frame in range(sections):
+        noisy = jnp.concatenate(
+            [
+                ordered[s, :, cells + frame * tile : cells + (frame + 1) * tile]
+                for s in range(sections)
+            ],
+            axis=1,
+        )
+        field = ordered[frame, :, 0:cells]
+        latent = (noisy - step[0] * field) * std[...] + mean[...]
+        out[:, frame * cells : (frame + 1) * cells] = latent.astype(BF16)
+
+
+def block_kernel(
+    where, earlier, latent, weight_mine, weight_other, sums_mine, sums_other, gain, conv_hbm,
+    *refs, frames, height, width, sections, tokens
+):
+    partials, (tile, rolled, blocks, normed, conv, arrived) = refs[:sections], refs[sections:]
+    mine, block, first_frame = where[0], where[1], where[2]
+    fetch = pltpu.make_async_copy(conv_hbm, conv, arrived)
+    fetch.start()
+    cells = height * width
+    lat = latent.shape[0]
+    lanes = 2 * frames * cells
+    columns = width // sections
+    half = weight_mine.shape[1]
+    deep = gain.shape[2]
+    per_half = half // deep
+    x = jnp.concatenate([earlier[...].astype(F32), latent[...].astype(F32)], axis=1)
+    position = lax.broadcasted_iota(jnp.int32, (1, lanes), 1)
+    at_row = position % height
+    at_column = (position // height) % width
+    for b in range(3):
+        for e in range(3):
+            offset = (e - 1) * height + (b - 1)
+            moved = x if offset == 0 else pltpu.roll(x, (-offset) % lanes, axis=1)
+            row, column = at_row + (b - 1), at_column + (e - 1)
+            inside = (row >= 0) & (row < height) & (column >= 0) & (column < width)
+            moved = jnp.where(inside, moved, 0.0)
+            first = (3 * b + e) * lat
+            rolled[first : first + lat, :] = moved.astype(BF16)
+    bias_rows = [
+        source[tokens + 1 + i : tokens + 2 + i, :]
+        for source in (sums_mine, sums_other)
+        for i in range(per_half)
+    ]
+    gain_row = gain[mine]
+    edge = lax.broadcasted_iota(jnp.int32, (cells, 1), 0) % height
+    zero_column = jnp.zeros((height, deep), BF16)
+    for frame in range(frames + 2):
+        stacked = jnp.concatenate(
+            [rolled[:, (frame + a) * cells : (frame + a + 1) * cells] for a in range(3)], axis=0
+        )
+        squares = jnp.zeros((cells, deep), F32)
+        for which, weight in enumerate((weight_mine, weight_other)):
+            product = lax.dot_general(
+                stacked, weight[...], (((0,), (0,)), ((), ())), preferred_element_type=F32
+            )
+            for i in range(per_half):
+                n = which * per_half + i
+                piece = (product[:, i * deep : (i + 1) * deep] + bias_rows[n]).astype(BF16)
+                blocks[n] = piece
+                wide = piece.astype(F32)
+                squares = squares + wide * wide
+        mean = jnp.sum(squares, axis=1, keepdims=True) / (2 * half)
+        inverse = lax.rsqrt(mean + 1e-06)
+        value = blocks[block].astype(F32) * inverse * gain_row
+        value = value / (1.0 + jnp.exp(-value))
+        if frame < 2:
+            value = jnp.where(first_frame + frame >= 0, value, 0.0)
+        above = jnp.where(edge == 0, 0.0, pltpu.roll(value, 1, axis=0))
+        below = jnp.where(edge == height - 1, 0.0, pltpu.roll(value, cells - 1, axis=0))
+        for b, shifted in enumerate((above, value, below)):
+            normed[b, frame, 1 : width + 1] = shifted.astype(BF16).reshape(width, height, deep)
+            normed[b, frame, 0] = zero_column
+            normed[b, frame, width + 1] = zero_column
+        if frame >= 2:
+            rows = pl.ds(pl.multiple_of(mine * (columns * height), columns * height), columns * height)
+            for i in range(per_half):
+                tile[frame - 2, :, i * deep : (i + 1) * deep] = blocks[i, rows, :]
+    fetch.wait()
+    size = frames * columns * height
+    for k in range(sections):
+        first_column = (mine ^ k) * columns
+        total = jnp.zeros((size, half), F32)
+        for a in range(3):
+            for b in range(3):
+                window = jnp.concatenate(
+                    [
+                        normed[b, a : a + frames, pl.ds(first_column + e, columns)].reshape(size, deep)
+                        for e in range(3)
+                    ],
+                    axis=1,
+                )
+                taps = conv[9 * a + 3 * b : 9 * a + 3 * b + 3].reshape(3 * deep, half)
+                total = total + jnp.dot(window, taps, preferred_element_type=F32)
+        partials[k][...] = total.astype(partials[k].dtype)
+
+
+def finish_kernel(tile, bias, order, *refs):
+    parts, out = refs[:-1], refs[-1]
+    rows = tile.shape[1]
+    for frame in range(tile.shape[0]):
+        total = tile[frame].astype(F32) + bias[...]
+        for part in parts:
+            total = total + part[frame * rows : (frame + 1) * rows, :].astype(F32)
+        placed = jnp.dot(order[...], total.astype(BF16), preferred_element_type=F32)
+        out[frame * rows : (frame + 1) * rows, :] = placed.astype(BF16)
+
+
+def vmem(count):
+    return [pl.BlockSpec(memory_space=pltpu.VMEM)] * count
+
+
+SMEM = pl.BlockSpec(memory_space=pltpu.SMEM)
+
+
+def call(kernel, shapes, in_specs, scratch=()):
+    single = not isinstance(shapes, (list, tuple))
+    specs = pl.BlockSpec(memory_space=pltpu.VMEM) if single else vmem(len(shapes))
+    return pl.pallas_call(
+        kernel, out_shape=shapes, in_specs=in_specs, out_specs=specs, scratch_shapes=list(scratch)
+    )
+
+
+def token_places(height, width):
+    cells = height * width
+    table = np.zeros((cells // 4, 4, cells), np.float32)
+    for i in range(height // 2):
+        for j in range(width // 2):
+            for p in range(2):
+                for q in range(2):
+                    cell = (2 * j + q) * height + 2 * i + p
+                    table[i * (width // 2) + j, 2 * p + q, cell] = 1.0
+    return table.reshape(cells // 4, 4 * cells)
+
+
+def row_order(height, columns):
+    table = np.zeros((height * columns, height * columns), np.float32)
+    for h in range(height):
+        for w in range(columns):
+            table[h * columns + w, w * height + h] = 1.0
+    return table
+
+
+def sectioned_shards(
+    hidden, modulation, time_embed, head_weight, head_bias, noisy, step_size,
+    latent_mean, latent_std, in_weight, in_bias, norm_gain, conv_weight, conv_bias,
+):
+    frames, height, columns, lat = noisy.shape
+    sections, halves = lax.axis_size("section"), lax.axis_size("tp")
+    width, half = columns * sections, in_weight.shape[2]
+    cells = height * width
+    tokens, local = hidden.shape
+    outs = head_weight.shape[1]
+    deep = conv_weight.shape[1]
+    per_half = half // deep
+    mine, side = lax.axis_index("section"), lax.axis_index("tp")
+    swap = [(i, i ^ 1) for i in range(halves)]
+    taps = in_weight.shape[0]
+
+    weight_mine = in_weight.reshape(taps * lat, half)
+    weight_other = lax.ppermute(weight_mine, "tp", swap)
+    noisy_rows = jnp.transpose(noisy, (3, 0, 2, 1)).reshape(lat, frames * columns * height)
+    sums = call(
+        head_kernel, jax.ShapeDtypeStruct((tokens + 8, 2 * outs), F32), vmem(5)
+    )(hidden, modulation, time_embed.reshape(1, local), head_weight, in_bias.reshape(per_half, deep))
+    sums_other = lax.ppermute(sums, "tp", swap)
+
+    place = jnp.asarray(token_places(height, width), BF16)
+    message = call(
+        lambda *refs: message_kernel(
+            *refs, features=local * halves, cells=cells, channels=lat
+        ),
+        jax.ShapeDtypeStruct((lat, 2 * cells), BF16), vmem(5),
+    )(sums, sums_other, head_bias.reshape(1, outs), place, noisy_rows)
+    messages = [message] + [
+        lax.ppermute(message, "section", [(i, i ^ k) for i in range(sections)])
+        for k in range(1, sections)
+    ]
+    block = jnp.where((mine // per_half) == side, 0, per_half) + mine % per_half
+    where = jnp.stack([mine, block, lax.axis_index("sp") * frames - 2]).astype(jnp.int32)
+    latent = call(
+        lambda *refs: latent_kernel(*refs, sections=sections, cells=cells),
+        jax.ShapeDtypeStruct((lat, frames * cells), BF16),
+        [SMEM, SMEM] + vmem(sections + 2),
+        [pltpu.VMEM((sections, lat, 2 * cells), F32)],
+    )(where, step_size, *messages, latent_std.reshape(lat, 1), latent_mean.reshape(lat, 1))
+    earlier = passed_along(latent, "sp", 1)
+
+    size = frames * columns * height
+    results = call(
+        lambda *refs: block_kernel(
+            *refs, frames=frames, height=height, width=width, sections=sections, tokens=tokens
+        ),
+        [jax.ShapeDtypeStruct((size, half), F32 if k == 0 else BF16) for k in range(sections)]
+        + [jax.ShapeDtypeStruct((frames, columns * height, half), BF16)],
+        [SMEM] + vmem(7) + [pl.BlockSpec(memory_space=pl.ANY)],
+        [
+            pltpu.VMEM((9 * lat, 2 * frames * cells), BF16),
+            pltpu.VMEM((sections, cells, deep), BF16),
+            pltpu.VMEM((3, frames + 2, width + 2, height, deep), BF16),
+            pltpu.VMEM(conv_weight.shape, BF16),
+            pltpu.SemaphoreType.DMA(()),
+        ],
+    )(
+        where, earlier, latent, weight_mine, weight_other, sums, sums_other,
+        norm_gain.reshape(sections, 1, deep), conv_weight,
+    )
+    partials, tile = results[:sections], results[sections]
+    received = {}
+    for k in (2, 1, 3) if sections == 4 else range(1, sections):
+        received[k] = lax.ppermute(partials[k], "section", [(i, i ^ k) for i in range(sections)])
+    order = jnp.asarray(row_order(height, columns), BF16)
+    decoded = call(
+        finish_kernel, jax.ShapeDtypeStruct((size, half), BF16), vmem(3 + sections)
+    )(
+        tile, conv_bias.reshape(1, half), order, partials[0],
+        *[received[k] for k in range(1, sections)],
+    )
+    return decoded.reshape(frames, height, columns, half)
+
+
+def sectioned(mesh):
+    def fits(hidden, noisy, in_weight, conv_weight):
+        frames, height, columns, _ = noisy.shape
+        sections = mesh.shape["section"]
+        cells = height * columns * sections
+        deep = conv_weight.shape[1]
+        return (
+            sections == frames
+            and sections & (sections - 1) == 0
+            and hidden.shape[0] * 4 == cells
+            and mesh.shape["tp"] == 2
+            and in_weight.shape[2] == 2 * deep
+            and 2 * in_weight.shape[2] == sections * deep
+            and deep % 128 == 0
+            and height % 16 == 0
+            and cells % 128 == 0
+        )
+    return fits
 
 
 def solution(mesh):
@@ -139,6 +436,12 @@
         P(None, "section", "tp"),
         P("tp"),
     )
+    fits = sectioned(mesh)
+
+    def shards(*args):
+        body = sectioned_shards if fits(args[0], args[5], args[9], args[12]) else general_shards
+        return body(*args)
+
     return jax.shard_map(
         shards,
         mesh=mesh,

time: 159 us -> 50.1 us (0.32)
  waiting for transfers between devices: 70.6 us -> 11.5 us
  local copies, waits for them, and re-layouts: 30.1 us -> 9.14 us
  other arithmetic: 16.3 us -> 0.56 us
  Pallas kernels: 0 us -> 14.1 us
  between operations: 14.7 us -> 0.72 us
  blocking collectives: 8.74 us -> 0 us
  matrix products: 5.53 us -> 0 us
  starting transfers between devices: 12 us -> 13.7 us
    all_gather x1 -> x0, waiting for transfers between devices: 55.2 us -> none  [shards(): full_weight = lax.all_gather(conv_weight, 'section', axis=1, tiled=True)]
    concatenate x16 -> x0, other arithmetic: 14.4 us -> none  [the longest x14 14.1 us: conv_taps(): jnp.concatenate([slab[:, :, 0:columns], slab[:, :, 1:columns + 1], slab[:...]
    pallas_call x0 -> x5, Pallas kernels: none -> 14.1 us  [the longest x1 6.23 us: sectioned_shards(): call(lambda *refs: block_kernel(*refs, frames=frames, height=height, widt...]
    slice x10 -> x0, local copies, waits for them, and re-layouts: 13.2 us -> none  [the longest x4 4.94 us: conv_taps(): slab[:, :, 0:columns]]
    reshape x23 -> x4, local copies, waits for them, and re-layouts: 13 us -> 3.67 us  [the longest x1 1.59 us: sectioned_shards(): return decoded.reshape(frames, height, columns, half)]
    ppermute x2 -> x8, starting transfers between devices: 2.58 us -> 10.3 us  [the longest x3 5.32 us: sectioned_shards(): lax.ppermute(message, 'section', [(i, i ^ k) for i in range(sections)])]
    all_to_all x1 -> x0, waiting for transfers between devices: 7.51 us -> none  [shards(): lax.all_to_all(outgoing, 'section', split_axis=1, concat_axis=0, tiled=True)]
    psum x2 -> x0, blocking collectives: 6.21 us -> none  [the longest x1 3.58 us: shards(): velocity = (lax.psum(partial_sum, 'tp') + head_bias).astype(jnp.bfloat16)]
  transfers between devices with their start and end apart: 5 -> 9, of which waited for: 5 -> 5; matrix products, arithmetic and copies ran while one was open for 26% -> 10% of each run, Pallas kernels for 0% -> 12%
where the time goes in v1:
time: 50.1 us; the launch traced here: 49.8 us
  Pallas kernels  14.1 us (28%)
  starting transfers between devices  13.7 us (27%)
  waiting for transfers between devices  11.5 us (23%)
  local copies, waits for them, and re-layouts  9.14 us (18%)
  between operations  0.72 us (1%)
  other arithmetic  0.56 us (1%)
    ppermute x3, waiting for transfers between devices, sectioned_shards(): lax.ppermute(partials[k], 'section', [(i, i ^ k) for i in range(sections)])  7.4 us
    pallas_call x1, Pallas kernels, sectioned_shards(): call(lambda *refs: block_kernel(*refs, frames=frames, height=height, widt...  6.23 us
    unnamed x25, local copies, waits for them, and re-layouts  5.34 us
    ppermute x3, starting transfers between devices, sectioned_shards(): lax.ppermute(message, 'section', [(i, i ^ k) for i in range(sections)])  5.32 us
    ppermute x3, starting transfers between devices, sectioned_shards(): lax.ppermute(partials[k], 'section', [(i, i ^ k) for i in range(sections)])  4.44 us
    ppermute x1, starting transfers between devices, passed_along(): return lax.ppermute(value, axis, pairs)  3.37 us
    pallas_call x1, Pallas kernels, sectioned_shards(): call(head_kernel, jax.ShapeDtypeStruct((tokens + 8, 2 * outs), F32), vmem...  2.42 us
    pallas_call x1, Pallas kernels, sectioned_shards(): call(finish_kernel, jax.ShapeDtypeStruct((size, half), BF16), vmem(3 + se...  2.05 us
  transfers between devices with their start and end apart: 9, of which 5 were waited for; matrix products, arithmetic and copies ran while one was open for 10% of the time, Pallas kernels for 12%

profile of v1, /device:TPU:0, one launch (start us, length us, event | category | flops | bytes accessed | tf_op | source)
XLA Modules:
  0.0 49.8 jit_solution(12330612211533128360)
XLA Ops:
  0.0 0.6 %collective-permute-start.5 = (bf16[432,256]{1,0:T(8,128)(2,1)}, bf16[432,256]{1,0:T(8,128)(2,1)S(1)}, u32[]{:S(2)}, u32[]{:S(2)}) collective-permute-start(bf16[432,256]{1,0:T(8,128)(2,1)} %bitcast.12), channel_id=1, source_target_pairs={{0,2},{2,0},{1,3},{3,1},{4,6},{6,4},{5,7},{7,5},{8,10},{10,8},{9,1... | collective-permute-start | bytes 663560 | tf_op jit(solution)/shard_map/ppermute | solution.py:341
  0.6 2.1 %copy.17.weight = bf16[3072,64]{1,0:T(8,128)(2,1)} copy(bf16[3072,64]{0,1:T(8,128)(2,1)} %param.19) | data formatting | bytes 786432 | tf_op args[3]
  2.7 2.4 %shard_map.154.refs_0_.refs_5_ = f32[72,128]{1,0:T(8,128)} custom-call(bf16[64,3072]{1,0:T(8,128)(2,1)} %hidden.1, f32[2,3072]{1,0:T(2,128)} %modulation.1, f32[1,3072]{1,0:T(1,128)} %bitcast.15, bf16[3072,64]{1,0:T(8,128)(2,1)} %copy.17.weight, f32[2,128]{1,0:T(2,128)} %bitcast.17), custom_call_target="tpu_custom_call" | custom-call | tf_op jit(solution)/shard_map/pallas_call | solution.py:343
  5.1 0.0 collective-permute-start
  5.2 0.1 copy.18
  5.3 0.7 %reshape.33.refs_4_ = bf16[16,256]{1,0:T(8,128)(2,1)} reshape(bf16[16,4,4,16]{3,2,1,0:T(4,128)(2,1)S(1)} %copy.18) | data formatting | bytes 16384 | tf_op jit(solution)/shard_map/reshape | solution.py:342
  6.0 0.6 %collective-permute-done.refs_1_.refs_6_ = f32[72,128]{1,0:T(8,128)S(1)} collective-permute-done((f32[72,128]{1,0:T(8,128)}, f32[72,128]{1,0:T(8,128)S(1)}, u32[]{:S(2)}, u32[]{:S(2)}) %collective-permute-start) | collective-permute-done | bytes 36896 | tf_op jit(solution)/shard_map/ppermute | solution.py:346
  6.6 0.6 %copy-done.1 = f32[72,128]{1,0:T(8,128)} copy-done((f32[72,128]{1,0:T(8,128)}, f32[72,128]{1,0:T(8,128)S(1)}, u32[]{:S(2)}) %copy-start.1) | copy-done | bytes 36888
  7.2 1.9 %shard_map.155.refs_2_ = bf16[16,512]{1,0:T(8,128)(2,1)} custom-call(f32[72,128]{1,0:T(8,128)} %shard_map.154.refs_0_.refs_5_, f32[72,128]{1,0:T(8,128)} %copy-done.1, f32[1,64]{1,0:T(1,128)} %bitcast.19, bf16[64,1024]{1,0:T(8,128)(2,1)} %constant.44.clone.refs_3_, bf16[16,256]{1,0:T(8,128)(2,1)} %reshape.33.refs_4_), custom_call_target="tpu_custom_call" | custom-call | tf_op jit(solution)/shard_map/pallas_call | solution.py:349
  9.1 4.7 %collective-permute-start.3 = (bf16[16,512]{1,0:T(8,128)(2,1)}, bf16[16,512]{1,0:T(8,128)(2,1)S(1)}, u32[]{:S(2)}, u32[]{:S(2)}) collective-permute-start(bf16[16,512]{1,0:T(8,128)(2,1)} %shard_map.155.refs_2_), channel_id=1, source_target_pairs={{0,12},{4,8},{8,4},{12,0},{1,13},{5,9},{9,5},{13,1},{2,14},{6,10},... | collective-permute-start | bytes 49160 | tf_op jit(solution)/shard_map/ppermute | solution.py:356
  13.8 0.6 %collective-permute-start.1 = (bf16[16,512]{1,0:T(8,128)(2,1)}, bf16[16,512]{1,0:T(8,128)(2,1)S(1)}, u32[]{:S(2)}, u32[]{:S(2)}) collective-permute-start(bf16[16,512]{1,0:T(8,128)(2,1)} %shard_map.155.refs_2_), channel_id=1, source_target_pairs={{0,4},{4,0},{8,12},{12,8},{1,5},{5,1},{9,13},{13,9},{2,6},{6,2},{1... | collective-permute-start | bytes 49160 | tf_op jit(solution)/shard_map/ppermute | solution.py:356
  14.4 0.6 %pad_add_fusion.refs_0_ = s32[3]{0:T(128)} fusion(s32[1]{0:T(128)} %bitcast.2, s32[1]{0:T(128)} %bitcast.1, s32[1]{0:T(128)} %bitcast), kind=kLoop, calls=%fused_computation | loop fusion | flops 6 | bytes 24 | tf_op jit(solution)/shard_map/stack | solution.py:360
  15.6 0.7 %copy.20.refs_7_ = f32[16,1]{1,0:T(8,128)} copy(f32[16,1]{0,1:T(1,128)S(1)} %bitcast.20) | data formatting | bytes 128 | tf_op jit(solution)/shard_map/reshape | solution.py:366
  16.3 0.7 %copy.19.refs_6_ = f32[16,1]{1,0:T(8,128)} copy(f32[16,1]{0,1:T(1,128)S(1)} %bitcast.21) | data formatting | bytes 128 | tf_op jit(solution)/shard_map/reshape | solution.py:366
  17.0 1.7 %collective-permute-done.2.refs_4_ = bf16[16,512]{1,0:T(8,128)(2,1)S(1)} collective-permute-done((bf16[16,512]{1,0:T(8,128)(2,1)}, bf16[16,512]{1,0:T(8,128)(2,1)S(1)}, u32[]{:S(2)}, u32[]{:S(2)}) %collective-permute-start.2) | collective-permute-done | bytes 16416 | tf_op jit(solution)/shard_map/ppermute | solution.py:356
  18.7 0.6 %copy-done.8 = bf16[16,512]{1,0:T(8,128)(2,1)} copy-done((bf16[16,512]{1,0:T(8,128)(2,1)}, bf16[16,512]{1,0:T(8,128)(2,1)S(1)}, u32[]{:S(2)}) %copy-start.8) | copy-done | bytes 16408
  19.3 0.6 %copy-done.9 = bf16[16,512]{1,0:T(8,128)(2,1)} copy-done((bf16[16,512]{1,0:T(8,128)(2,1)}, bf16[16,512]{1,0:T(8,128)(2,1)S(1)}, u32[]{:S(2)}) %copy-start.9) | copy-done | bytes 16408
  19.9 1.5 %shard_map.156.refs_2_ = bf16[16,1024]{1,0:T(8,128)(2,1)} custom-call(s32[3]{0:T(128)} %pad_add_fusion.refs_0_, f32[1]{0:T(128)S(6)} %copy.21.refs_1_, bf16[16,512]{1,0:T(8,128)(2,1)} %shard_map.155.refs_2_, bf16[16,512]{1,0:T(8,128)(2,1)} %copy-done.9, bf16[16,512]{1,0:T(8,128)(2,1)} %copy-done.8, bf16[16,512]{1,0:T(8,128)(2,1)} %copy-done.7, ...), custom_call_target="tpu_custom_call" | custom-call | tf_op jit(solution)/shard_map/pallas_call | solution.py:361
  21.4 3.4 %collective-permute-start.4 = (bf16[16,1024]{1,0:T(8,128)(2,1)}, bf16[16,1024]{1,0:T(8,128)(2,1)S(1)}, u32[]{:S(2)}, u32[]{:S(2)}) collective-permute-start(bf16[16,1024]{1,0:T(8,128)(2,1)} %shard_map.156.refs_2_), channel_id=1, source_target_pairs={{0,1},{2,3},{4,5},{6,7},{8,9},{10,11},{12,13},{14,15},{16,17},{18,... | collective-permute-start | bytes 98312 | tf_op jit(solution)/shard_map/ppermute | solution.py:29
  24.8 1.9 %collective-permute-done.4.refs_1_ = bf16[16,1024]{1,0:T(8,128)(2,1)S(1)} collective-permute-done((bf16[16,1024]{1,0:T(8,128)(2,1)}, bf16[16,1024]{1,0:T(8,128)(2,1)S(1)}, u32[]{:S(2)}, u32[]{:S(2)}) %collective-permute-start.4) | collective-permute-done | bytes 32800 | tf_op jit(solution)/shard_map/ppermute | solution.py:29
  26.7 0.6 %copy-done.6 = bf16[16,1024]{1,0:T(8,128)(2,1)} copy-done((bf16[16,1024]{1,0:T(8,128)(2,1)}, bf16[16,1024]{1,0:T(8,128)(2,1)S(1)}, u32[]{:S(2)}) %copy-start.6) | copy-done | bytes 32792
  27.3 0.1 copy-done
  27.4 6.2 %shard_map.157 = (f32[256,256]{1,0:T(8,128)}, bf16[256,256]{1,0:T(8,128)(2,1)}, bf16[256,256]{1,0:T(8,128)(2,1)}, bf16[256,256]{1,0:T(8,128)(2,1)}, bf16[4,64,256]{2,1,0:T(8,128)(2,1)}) custom-call(s32[3]{0:T(128)} %pad_add_fusion.refs_0_, bf16[16,1024]{1,0:T(8,128)(2,1)} %copy-done.6, bf16[16,1024]{1,0:T(8,128)(2,1)} %shard_map.156.refs_2_, ...), custom_call_target="tpu_custom_call" | custom-call | tf_op jit(solution)/shard_map/pallas_call | solution.py:370
  33.6 0.1 collective-permute-start.6
  33.7 2.7 %collective-permute-start.7 = (bf16[256,256]{1,0:T(8,128)(2,1)}, bf16[256,256]{1,0:T(8,128)(2,1)S(1)}, u32[]{:S(2)}, u32[]{:S(2)}) collective-permute-start(bf16[256,256]{1,0:T(8,128)(2,1)} %get-tuple-element.13), channel_id=1, source_target_pairs={{0,8},{4,12},{8,0},{12,4},{1,9},{5,13},{9,1},{13,5},{2,10},{6,14},... | collective-permute-start | bytes 393224 | tf_op jit(solution)/shard_map/ppermute | solution.py:391
  36.4 1.7 %collective-permute-start.8 = (bf16[256,256]{1,0:T(8,128)(2,1)}, bf16[256,256]{1,0:T(8,128)(2,1)S(1)}, u32[]{:S(2)}, u32[]{:S(2)}) collective-permute-start(bf16[256,256]{1,0:T(8,128)(2,1)} %get-tuple-element.14), channel_id=1, source_target_pairs={{0,12},{4,8},{8,4},{12,0},{1,13},{5,9},{9,5},{13,1},{2,14},{6,10},... | collective-permute-start | bytes 393224 | tf_op jit(solution)/shard_map/ppermute | solution.py:391
  38.0 2.3 %collective-permute-done.6.refs_1_ = bf16[256,256]{1,0:T(8,128)(2,1)S(1)} collective-permute-done((bf16[256,256]{1,0:T(8,128)(2,1)}, bf16[256,256]{1,0:T(8,128)(2,1)S(1)}, u32[]{:S(2)}, u32[]{:S(2)}) %collective-permute-start.6) | collective-permute-done | bytes 131104 | tf_op jit(solution)/shard_map/ppermute | solution.py:391
  40.3 5.1 %collective-permute-done.7.refs_2_ = bf16[256,256]{1,0:T(8,128)(2,1)S(1)} collective-permute-done((bf16[256,256]{1,0:T(8,128)(2,1)}, bf16[256,256]{1,0:T(8,128)(2,1)S(1)}, u32[]{:S(2)}, u32[]{:S(2)}) %collective-permute-start.7) | collective-permute-done | bytes 131104 | tf_op jit(solution)/shard_map/ppermute | solution.py:391
  45.5 0.6 %copy-done.3 = bf16[256,256]{1,0:T(8,128)(2,1)} copy-done((bf16[256,256]{1,0:T(8,128)(2,1)}, bf16[256,256]{1,0:T(8,128)(2,1)S(1)}, u32[]{:S(2)}) %copy-start.3) | copy-done | bytes 131096
  46.1 0.1 copy-done.4
  46.1 2.1 %shard_map.158 = bf16[256,256]{1,0:T(8,128)(2,1)} custom-call(bf16[4,64,256]{2,1,0:T(8,128)(2,1)} %get-tuple-element.10.tile, f32[1,256]{1,0:T(1,128)} %bitcast.18, bf16[64,64]{1,0:T(8,128)(2,1)} %constant.45.clone.order, f32[256,256]{1,0:T(8,128)} %get-tuple-element.11.refs_0_, bf16[256,256]{1,0:T(8,128)(2,1)} %copy-done.2, bf16[256,256]{1,0:T(8,128)(2,1)} %copy-done.3, ...), custom_call_target="tpu_custom_call" | custom-call | tf_op jit(solution)/shard_map/pallas_call | solution.py:393
  48.2 1.6 %reshape.39 = bf16[4,16,4,256]{3,2,1,0:T(4,128)(2,1)} reshape(bf16[256,256]{1,0:T(8,128)(2,1)} %shard_map.158) | data formatting | bytes 262144 | tf_op jit(solution)/shard_map/reshape | solution.py:399
  (22 shorter events, 0.0 us)
Async XLA Ops:
  0.0 5.2 %copy-start.5 = (bf16[4,16,4,16]{3,2,1,0:T(4,128)(2,1)S(1)}, bf16[4,16,4,16]{3,2,1,0:T(4,128)(2,1)}, u32[]{:S(2)}) copy-start(bf16[4,16,4,16]{3,2,1,0:T(4,128)(2,1)} %param.21) | copy-start | bytes 24580
  0.0 15.6 %copy-start.10 = (f32[16]{0:T(128)S(1)}, f32[16]{0:T(128)}, u32[]{:S(2)}) copy-start(f32[16]{0:T(128)} %param.23) | copy-start | bytes 196
  0.0 16.3 %copy-start.11 = (f32[16]{0:T(128)S(1)}, f32[16]{0:T(128)}, u32[]{:S(2)}) copy-start(f32[16]{0:T(128)} %param.24) | copy-start | bytes 196
  0.0 26.7 %collective-permute-start.5 = (bf16[432,256]{1,0:T(8,128)(2,1)}, bf16[432,256]{1,0:T(8,128)(2,1)S(1)}, u32[]{:S(2)}, u32[]{:S(2)}) collective-permute-start(bf16[432,256]{1,0:T(8,128)(2,1)} %bitcast.12), channel_id=1, source_target_pairs={{0,2},{2,0},{1,3},{3,1},{4,6},{6,4},{5,7},{7,5},{8,10},{10,8},{9,1... | collective-permute-start | bytes 663560 | tf_op jit(solution)/shard_map/ppermute | solution.py:341
  5.1 1.4 %collective-permute-start = (f32[72,128]{1,0:T(8,128)}, f32[72,128]{1,0:T(8,128)S(1)}, u32[]{:S(2)}, u32[]{:S(2)}) collective-permute-start(f32[72,128]{1,0:T(8,128)} %shard_map.154.refs_0_.refs_5_), channel_id=1, source_target_pairs={{0,2},{2,0},{1,3},{3,1},{4,6},{6,4},{5,7},{7,5},{8,10},{10,8},{9,1... | collective-permute-start | bytes 110600 | tf_op jit(solution)/shard_map/ppermute | solution.py:346
  6.6 0.6 %copy-start.1 = (f32[72,128]{1,0:T(8,128)}, f32[72,128]{1,0:T(8,128)S(1)}, u32[]{:S(2)}) copy-start(f32[72,128]{1,0:T(8,128)S(1)} %collective-permute-done.refs_1_.refs_6_) | copy-start | bytes 110596
  9.1 7.9 %collective-permute-start.3 = (bf16[16,512]{1,0:T(8,128)(2,1)}, bf16[16,512]{1,0:T(8,128)(2,1)S(1)}, u32[]{:S(2)}, u32[]{:S(2)}) collective-permute-start(bf16[16,512]{1,0:T(8,128)(2,1)} %shard_map.155.refs_2_), channel_id=1, source_target_pairs={{0,12},{4,8},{8,4},{12,0},{1,13},{5,9},{9,5},{13,1},{2,14},{6,10},... | collective-permute-start | bytes 49160 | tf_op jit(solution)/shard_map/ppermute | solution.py:356
  13.8 4.8 %collective-permute-start.2 = (bf16[16,512]{1,0:T(8,128)(2,1)}, bf16[16,512]{1,0:T(8,128)(2,1)S(1)}, u32[]{:S(2)}, u32[]{:S(2)}) collective-permute-start(bf16[16,512]{1,0:T(8,128)(2,1)} %shard_map.155.refs_2_), channel_id=1, source_target_pairs={{0,8},{4,12},{8,0},{12,4},{1,9},{5,13},{9,1},{13,5},{2,10},{6,14},... | collective-permute-start | bytes 49160 | tf_op jit(solution)/shard_map/ppermute | solution.py:356
  13.8 4.9 %collective-permute-start.1 = (bf16[16,512]{1,0:T(8,128)(2,1)}, bf16[16,512]{1,0:T(8,128)(2,1)S(1)}, u32[]{:S(2)}, u32[]{:S(2)}) collective-permute-start(bf16[16,512]{1,0:T(8,128)(2,1)} %shard_map.155.refs_2_), channel_id=1, source_target_pairs={{0,4},{4,0},{8,12},{12,8},{1,5},{5,1},{9,13},{13,9},{2,6},{6,2},{1... | collective-permute-start | bytes 49160 | tf_op jit(solution)/shard_map/ppermute | solution.py:356
  17.0 1.7 %copy-start.7 = (bf16[16,512]{1,0:T(8,128)(2,1)}, bf16[16,512]{1,0:T(8,128)(2,1)S(1)}, u32[]{:S(2)}) copy-start(bf16[16,512]{1,0:T(8,128)(2,1)S(1)} %collective-permute-done.3.refs_5_) | copy-start | bytes 49156
  18.7 0.6 %copy-start.8 = (bf16[16,512]{1,0:T(8,128)(2,1)}, bf16[16,512]{1,0:T(8,128)(2,1)S(1)}, u32[]{:S(2)}) copy-start(bf16[16,512]{1,0:T(8,128)(2,1)S(1)} %collective-permute-done.2.refs_4_) | copy-start | bytes 49156
  19.3 0.6 %copy-start.9 = (bf16[16,512]{1,0:T(8,128)(2,1)}, bf16[16,512]{1,0:T(8,128)(2,1)S(1)}, u32[]{:S(2)}) copy-start(bf16[16,512]{1,0:T(8,128)(2,1)S(1)} %collective-permute-done.1.refs_3_) | copy-start | bytes 49156
  21.4 5.3 %collective-permute-start.4 = (bf16[16,1024]{1,0:T(8,128)(2,1)}, bf16[16,1024]{1,0:T(8,128)(2,1)S(1)}, u32[]{:S(2)}, u32[]{:S(2)}) collective-permute-start(bf16[16,1024]{1,0:T(8,128)(2,1)} %shard_map.156.refs_2_), channel_id=1, source_target_pairs={{0,1},{2,3},{4,5},{6,7},{8,9},{10,11},{12,13},{14,15},{16,17},{18,... | collective-permute-start | bytes 98312 | tf_op jit(solution)/shard_map/ppermute | solution.py:29
  26.7 0.6 %copy-start.6 = (bf16[16,1024]{1,0:T(8,128)(2,1)}, bf16[16,1024]{1,0:T(8,128)(2,1)S(1)}, u32[]{:S(2)}) copy-start(bf16[16,1024]{1,0:T(8,128)(2,1)S(1)} %collective-permute-done.4.refs_1_) | copy-start | bytes 98308
  26.7 0.7 %copy-start = (bf16[432,256]{1,0:T(8,128)(2,1)}, bf16[432,256]{1,0:T(8,128)(2,1)S(1)}, u32[]{:S(2)}) copy-start(bf16[432,256]{1,0:T(8,128)(2,1)S(1)} %collective-permute-done.5.refs_4_) | copy-start | bytes 663556
  33.6 6.7 %collective-permute-start.6 = (bf16[256,256]{1,0:T(8,128)(2,1)}, bf16[256,256]{1,0:T(8,128)(2,1)S(1)}, u32[]{:S(2)}, u32[]{:S(2)}) collective-permute-start(bf16[256,256]{1,0:T(8,128)(2,1)} %get-tuple-element.12), channel_id=1, source_target_pairs={{0,4},{4,0},{8,12},{12,8},{1,5},{5,1},{9,13},{13,9},{2,6},{6,2},{1... | collective-permute-start | bytes 393224 | tf_op jit(solution)/shard_map/ppermute | solution.py:391
  33.7 11.8 %collective-permute-start.7 = (bf16[256,256]{1,0:T(8,128)(2,1)}, bf16[256,256]{1,0:T(8,128)(2,1)S(1)}, u32[]{:S(2)}, u32[]{:S(2)}) collective-permute-start(bf16[256,256]{1,0:T(8,128)(2,1)} %get-tuple-element.13), channel_id=1, source_target_pairs={{0,8},{4,12},{8,0},{12,4},{1,9},{5,13},{9,1},{13,5},{2,10},{6,14},... | collective-permute-start | bytes 393224 | tf_op jit(solution)/shard_map/ppermute | solution.py:391
  36.4 9.1 %collective-permute-start.8 = (bf16[256,256]{1,0:T(8,128)(2,1)}, bf16[256,256]{1,0:T(8,128)(2,1)S(1)}, u32[]{:S(2)}, u32[]{:S(2)}) collective-permute-start(bf16[256,256]{1,0:T(8,128)(2,1)} %get-tuple-element.14), channel_id=1, source_target_pairs={{0,12},{4,8},{8,4},{12,0},{1,13},{5,9},{9,5},{13,1},{2,14},{6,10},... | collective-permute-start | bytes 393224 | tf_op jit(solution)/shard_map/ppermute | solution.py:391
  40.3 5.1 %copy-start.2 = (bf16[256,256]{1,0:T(8,128)(2,1)}, bf16[256,256]{1,0:T(8,128)(2,1)S(1)}, u32[]{:S(2)}) copy-start(bf16[256,256]{1,0:T(8,128)(2,1)S(1)} %collective-permute-done.6.refs_1_) | copy-start | bytes 393220
  45.4 0.6 %copy-start.3 = (bf16[256,256]{1,0:T(8,128)(2,1)}, bf16[256,256]{1,0:T(8,128)(2,1)S(1)}, u32[]{:S(2)}) copy-start(bf16[256,256]{1,0:T(8,128)(2,1)S(1)} %collective-permute-done.7.refs_2_) | copy-start | bytes 393220
  45.5 0.7 %copy-start.4 = (bf16[256,256]{1,0:T(8,128)(2,1)}, bf16[256,256]{1,0:T(8,128)(2,1)S(1)}, u32[]{:S(2)}) copy-start(bf16[256,256]{1,0:T(8,128)(2,1)S(1)} %collective-permute-done.8.refs_3_) | copy-start | bytes 393220

commit v2 on v1

--- a/solution.py
+++ b/solution.py
@@ -115,28 +115,60 @@
     return decoded.reshape(frames, height, columns, half_channels)
 
 
-def head_kernel(hidden, modulation, time_embed, weight, in_bias, out):
-    tokens = hidden.shape[0]
-    outs = weight.shape[1]
-    x = hidden[...].astype(F32)
-    embed = time_embed[...]
-    scale = 1.0 + (modulation[1:2, :] + embed)
-    shift = modulation[0:1, :] + embed
-    scaled = x * scale
-    high = scaled.astype(BF16)
-    low = (scaled - high.astype(F32)).astype(BF16)
-    row = lax.broadcasted_iota(jnp.int32, (16, x.shape[1]), 0)
-    scale_high = scale.astype(BF16).astype(F32)
-    shift_high = shift.astype(BF16).astype(F32)
-    extra = jnp.where(row == 0, scale_high, 0.0)
-    extra = jnp.where(row == 1, scale - scale_high, extra)
-    extra = jnp.where(row == 2, shift_high, extra)
-    extra = jnp.where(row == 3, shift - shift_high, extra).astype(BF16)
-    stacked = jnp.concatenate([high, low, extra], axis=0)
-    sums = jnp.dot(stacked, weight[...], preferred_element_type=F32)
+def head_kernel(
+    hidden_hbm, modulation_hbm, embed_hbm, weight_hbm, bias_hbm, out,
+    hidden, modulation, time_embed, weight, in_bias, arrived, *, parts
+):
+    tokens, features = hidden.shape
+    outs = weight.shape[0]
+    wide = features // parts
+    small = [
+        pltpu.make_async_copy(source, target, arrived.at[i])
+        for i, (source, target) in enumerate(
+            ((modulation_hbm, modulation), (embed_hbm, time_embed), (bias_hbm, in_bias))
+        )
+    ]
+    large = []
+    for part in range(parts):
+        cut = pl.ds(part * wide, wide)
+        large.append(
+            [
+                pltpu.make_async_copy(
+                    source.at[:, cut], target.at[:, cut], arrived.at[3 + 2 * part + i]
+                )
+                for i, (source, target) in enumerate(((hidden_hbm, hidden), (weight_hbm, weight)))
+            ]
+        )
+    for copy in small + [copy for pair in large for copy in pair]:
+        copy.start()
+    for copy in small:
+        copy.wait()
+    sums, first, second = 0.0, 0.0, 0.0
+    row = lax.broadcasted_iota(jnp.int32, (16, wide), 0)
+    for part in range(parts):
+        for copy in large[part]:
+            copy.wait()
+        cut = slice(part * wide, (part + 1) * wide)
+        x = hidden[:, cut].astype(F32)
+        embed = time_embed[:, cut]
+        scale = 1.0 + (modulation[1:2, cut] + embed)
+        shift = modulation[0:1, cut] + embed
+        scaled = x * scale
+        high = scaled.astype(BF16)
+        low = (scaled - high.astype(F32)).astype(BF16)
+        scale_high = scale.astype(BF16).astype(F32)
+        shift_high = shift.astype(BF16).astype(F32)
+        extra = jnp.where(row == 0, scale_high, 0.0)
+        extra = jnp.where(row == 1, scale - scale_high, extra)
+        extra = jnp.where(row == 2, shift_high, extra)
+        extra = jnp.where(row == 3, shift - shift_high, extra).astype(BF16)
+        stacked = jnp.concatenate([high, low, extra], axis=0)
+        sums = sums + lax.dot_general(
+            stacked, weight[:, cut], (((1,), (1,)), ((), ())), preferred_element_type=F32
+        )
+        first = first + jnp.sum(x, axis=1, keepdims=True)
+        second = second + jnp.sum(x * x, axis=1, keepdims=True)
     out[0:tokens, 0:outs] = sums[0:tokens] + sums[tokens : 2 * tokens]
-    first = jnp.sum(x, axis=1, keepdims=True)
-    second = jnp.sum(x * x, axis=1, keepdims=True)
     lane = lax.broadcasted_iota(jnp.int32, (tokens, outs), 1)
     out[0:tokens, outs : 2 * outs] = jnp.where(lane == 0, first, second)
     base = 2 * tokens
@@ -146,6 +178,18 @@
     out[tokens + 1 : tokens + 1 + biases, :] = in_bias[...]
     rest = out.shape[0] - tokens - 1 - biases
     out[tokens + 1 + biases :, :] = jnp.zeros((rest, out.shape[1]), F32)
+
+
+def stage_kernel(_, *refs):
+    count = (len(refs) - 1) // 2
+    copies = [
+        pltpu.make_async_copy(source, target, refs[-1].at[i])
+        for i, (source, target) in enumerate(zip(refs[:count], refs[count:-1], strict=True))
+    ]
+    for copy in copies:
+        copy.start()
+    for copy in copies:
+        copy.wait()
 
 
 def message_kernel(mine, other, bias, place, noisy, out, *, features, cells, channels):
@@ -166,45 +210,65 @@
         field = field + spread[
             part * channels : (part + 1) * channels, part * cells : (part + 1) * cells
         ]
-    out[:, 0:cells] = field.astype(BF16)
-    out[:, cells:] = noisy[...]
-
-
-def latent_kernel(where, step, *refs, sections, cells):
-    messages, (std, mean, out, ordered) = refs[:sections], refs[sections:]
-    mine = where[0]
-    for k in range(sections):
-        ordered[mine ^ k] = messages[k][...].astype(F32)
+    for target in range(out.shape[0]):
+        out[target, :, 0:cells] = field.astype(BF16)
+        out[target, :, cells:] = noisy[...]
+
+
+def latents(messages, first, step, std, mean, sections, members, cells):
+    lat = std.shape[1]
+    diagonal = lax.broadcasted_iota(jnp.int32, (lat, lat), 0) == lax.broadcasted_iota(
+        jnp.int32, (lat, lat), 1
+    )
+    deviation = jnp.sum(jnp.where(diagonal, std[...], 0.0), axis=1, keepdims=True)
+    middle = jnp.sum(jnp.where(diagonal, mean[...], 0.0), axis=1, keepdims=True)
+    parts = [messages[first + s * members].astype(F32) for s in range(sections)]
     tile = cells // sections
+    frames = []
     for frame in range(sections):
-        noisy = jnp.concatenate(
-            [
-                ordered[s, :, cells + frame * tile : cells + (frame + 1) * tile]
-                for s in range(sections)
-            ],
-            axis=1,
-        )
-        field = ordered[frame, :, 0:cells]
-        latent = (noisy - step[0] * field) * std[...] + mean[...]
-        out[:, frame * cells : (frame + 1) * cells] = latent.astype(BF16)
-
-
-def block_kernel(
-    where, earlier, latent, weight_mine, weight_other, sums_mine, sums_other, gain, conv_hbm,
-    *refs, frames, height, width, sections, tokens
+        cut = slice(cells + frame * tile, cells + (frame + 1) * tile)
+        noisy = jnp.concatenate([part[:, cut] for part in parts], axis=1)
+        latent = (noisy - step * parts[frame][:, 0:cells]) * deviation + middle
+        frames.append(latent.astype(BF16).astype(F32))
+    return jnp.concatenate(frames, axis=1)
+
+
+def conv_tile(normed, conv, first_column, columns, frames):
+    height, deep = normed.shape[3:]
+    half = conv.shape[2]
+    size = frames * columns * height
+    total = jnp.zeros((size, half), F32)
+    for a in range(3):
+        for b in range(3):
+            window = jnp.concatenate(
+                [
+                    normed[b, a : a + frames, pl.ds(first_column + e, columns)].reshape(size, deep)
+                    for e in range(3)
+                ],
+                axis=1,
+            )
+            taps = conv[9 * a + 3 * b : 9 * a + 3 * b + 3].reshape(3 * deep, half)
+            total = total + jnp.dot(window, taps, preferred_element_type=F32)
+    return total
+
+
+def norm_kernel(
+    where, step, messages, std, mean, weight_mine, weight_other, sums_mine, sums_other, gain, conv,
+    partial, tile, normed, rolled, blocks, *, frames, height, width, tokens, k, sections, members
 ):
-    partials, (tile, rolled, blocks, normed, conv, arrived) = refs[:sections], refs[sections:]
-    mine, block, first_frame = where[0], where[1], where[2]
-    fetch = pltpu.make_async_copy(conv_hbm, conv, arrived)
-    fetch.start()
+    mine, block, member = where[0], where[1], where[2]
+    first_frame = member * frames - 2
     cells = height * width
-    lat = latent.shape[0]
+    lat = messages.shape[1]
     lanes = 2 * frames * cells
-    columns = width // sections
     half = weight_mine.shape[1]
     deep = gain.shape[2]
+    columns = tile.shape[1] // height
     per_half = half // deep
-    x = jnp.concatenate([earlier[...].astype(F32), latent[...].astype(F32)], axis=1)
+    rest = (step[0], std, mean, sections, members, cells)
+    earlier = latents(messages, jnp.maximum(member - 1, 0), *rest)
+    earlier = jnp.where(member > 0, earlier, 0.0)
+    x = jnp.concatenate([earlier, latents(messages, member, *rest)], axis=1)
     position = lax.broadcasted_iota(jnp.int32, (1, lanes), 1)
     at_row = position % height
     at_column = (position // height) % width
@@ -256,34 +320,24 @@
             rows = pl.ds(pl.multiple_of(mine * (columns * height), columns * height), columns * height)
             for i in range(per_half):
                 tile[frame - 2, :, i * deep : (i + 1) * deep] = blocks[i, rows, :]
-    fetch.wait()
-    size = frames * columns * height
-    for k in range(sections):
-        first_column = (mine ^ k) * columns
-        total = jnp.zeros((size, half), F32)
-        for a in range(3):
-            for b in range(3):
-                window = jnp.concatenate(
-                    [
-                        normed[b, a : a + frames, pl.ds(first_column + e, columns)].reshape(size, deep)
-                        for e in range(3)
-                    ],
-                    axis=1,
-                )
-                taps = conv[9 * a + 3 * b : 9 * a + 3 * b + 3].reshape(3 * deep, half)
-                total = total + jnp.dot(window, taps, preferred_element_type=F32)
-        partials[k][...] = total.astype(partials[k].dtype)
+    partial[...] = conv_tile(normed, conv, (mine ^ k) * columns, columns, frames).astype(BF16)
+
+
+def tile_kernel(where, normed, conv, partial, *, columns, frames, k):
+    partial[...] = conv_tile(normed, conv, (where[0] ^ k) * columns, columns, frames).astype(
+        partial.dtype
+    )
 
 
 def finish_kernel(tile, bias, order, *refs):
     parts, out = refs[:-1], refs[-1]
-    rows = tile.shape[1]
+    rows, (height, columns) = tile.shape[1], out.shape[1:3]
     for frame in range(tile.shape[0]):
         total = tile[frame].astype(F32) + bias[...]
         for part in parts:
             total = total + part[frame * rows : (frame + 1) * rows, :].astype(F32)
         placed = jnp.dot(order[...], total.astype(BF16), preferred_element_type=F32)
-        out[frame * rows : (frame + 1) * rows, :] = placed.astype(BF16)
+        out[frame] = placed.reshape(height, columns, -1).astype(BF16)
 
 
 def vmem(count):
@@ -291,14 +345,39 @@
 
 
 SMEM = pl.BlockSpec(memory_space=pltpu.SMEM)
-
-
-def call(kernel, shapes, in_specs, scratch=()):
+HBM = pl.BlockSpec(memory_space=pltpu.HBM)
+
+
+VMEM_LIMIT = 12 * 2**20
+
+
+def call(kernel, shapes, in_specs, scratch=(), last=False):
     single = not isinstance(shapes, (list, tuple))
     specs = pl.BlockSpec(memory_space=pltpu.VMEM) if single else vmem(len(shapes))
-    return pl.pallas_call(
-        kernel, out_shape=shapes, in_specs=in_specs, out_specs=specs, scratch_shapes=list(scratch)
-    )
+    if not last:
+        local = [pltpu.VMEM(s.shape, s.dtype) for s in ([shapes] if single else shapes)]
+        shapes = local[0] if single else local
+    run = pl.pallas_call(
+        kernel, out_shape=shapes, in_specs=in_specs, out_specs=specs, scratch_shapes=list(scratch),
+        compiler_params=pltpu.CompilerParams(vmem_limit_bytes=VMEM_LIMIT),
+    )
+
+    def constrained(*args):
+        return run(
+            *[
+                arg if spec is SMEM else pltpu.with_memory_space_constraint(arg, spec.memory_space)
+                for arg, spec in zip(args, in_specs, strict=True)
+            ]
+        )
+
+    return constrained
+
+
+def staged(after, *arrays):
+    return call(
+        stage_kernel, [jax.ShapeDtypeStruct(x.shape, x.dtype) for x in arrays],
+        vmem(1) + [HBM] * len(arrays), [pltpu.SemaphoreType.DMA((len(arrays),))],
+    )(after, *arrays)
 
 
 def token_places(height, width):
@@ -327,6 +406,7 @@
 ):
     frames, height, columns, lat = noisy.shape
     sections, halves = lax.axis_size("section"), lax.axis_size("tp")
+    members = lax.axis_size("sp")
     width, half = columns * sections, in_weight.shape[2]
     cells = height * width
     tokens, local = hidden.shape
@@ -337,70 +417,79 @@
     swap = [(i, i ^ 1) for i in range(halves)]
     taps = in_weight.shape[0]
 
-    weight_mine = in_weight.reshape(taps * lat, half)
+    noisy_rows = jnp.transpose(noisy, (3, 0, 2, 1)).reshape(lat, frames * columns * height)
+    parts = 3 if local % (3 * 128) == 0 else 1
+    head_in = (
+        hidden, modulation, time_embed.reshape(1, local), head_weight.T,
+        in_bias.reshape(per_half, deep),
+    )
+    sums = call(
+        lambda *refs: head_kernel(*refs, parts=parts),
+        jax.ShapeDtypeStruct((tokens + 8, 2 * outs), F32), [HBM] * 5,
+        [pltpu.VMEM(x.shape, x.dtype) for x in head_in]
+        + [pltpu.SemaphoreType.DMA((3 + 2 * parts,))],
+    )(*head_in)
+    sums_other = lax.ppermute(sums, "tp", swap)
+    place, head_bias, latent_std, latent_mean, conv, weight_mine, gain, order, conv_bias = staged(
+        sums, jnp.asarray(token_places(height, width), BF16), head_bias.reshape(1, outs),
+        latent_std.reshape(1, lat), latent_mean.reshape(1, lat),
+        conv_weight, in_weight.reshape(taps * lat, half),
+        norm_gain.reshape(sections, 1, deep), jnp.asarray(row_order(height, columns), BF16),
+        conv_bias.reshape(1, half),
+    )
     weight_other = lax.ppermute(weight_mine, "tp", swap)
-    noisy_rows = jnp.transpose(noisy, (3, 0, 2, 1)).reshape(lat, frames * columns * height)
-    sums = call(
-        head_kernel, jax.ShapeDtypeStruct((tokens + 8, 2 * outs), F32), vmem(5)
-    )(hidden, modulation, time_embed.reshape(1, local), head_weight, in_bias.reshape(per_half, deep))
-    sums_other = lax.ppermute(sums, "tp", swap)
-
-    place = jnp.asarray(token_places(height, width), BF16)
     message = call(
         lambda *refs: message_kernel(
             *refs, features=local * halves, cells=cells, channels=lat
         ),
-        jax.ShapeDtypeStruct((lat, 2 * cells), BF16), vmem(5),
-    )(sums, sums_other, head_bias.reshape(1, outs), place, noisy_rows)
-    messages = [message] + [
-        lax.ppermute(message, "section", [(i, i ^ k) for i in range(sections)])
-        for k in range(1, sections)
-    ]
+        jax.ShapeDtypeStruct((sections * members, lat, 2 * cells), BF16), vmem(5),
+    )(sums, sums_other, head_bias, place, noisy_rows)
+    messages = lax.all_to_all(message, ("section", "sp"), 0, 0)
     block = jnp.where((mine // per_half) == side, 0, per_half) + mine % per_half
-    where = jnp.stack([mine, block, lax.axis_index("sp") * frames - 2]).astype(jnp.int32)
-    latent = call(
-        lambda *refs: latent_kernel(*refs, sections=sections, cells=cells),
-        jax.ShapeDtypeStruct((lat, frames * cells), BF16),
-        [SMEM, SMEM] + vmem(sections + 2),
-        [pltpu.VMEM((sections, lat, 2 * cells), F32)],
-    )(where, step_size, *messages, latent_std.reshape(lat, 1), latent_mean.reshape(lat, 1))
-    earlier = passed_along(latent, "sp", 1)
+    where = jnp.stack([mine, block, lax.axis_index("sp")]).astype(jnp.int32)
 
     size = frames * columns * height
-    results = call(
-        lambda *refs: block_kernel(
-            *refs, frames=frames, height=height, width=width, sections=sections, tokens=tokens
+    sends = list(range(1, sections))
+    sends = sends[sections // 2 - 1 :] + sends[: sections // 2 - 1]
+    partials = {}
+    partials[sends[0]], tile, normed = call(
+        lambda *refs: norm_kernel(
+            *refs, frames=frames, height=height, width=width, tokens=tokens, k=sends[0],
+            sections=sections, members=members
         ),
-        [jax.ShapeDtypeStruct((size, half), F32 if k == 0 else BF16) for k in range(sections)]
-        + [jax.ShapeDtypeStruct((frames, columns * height, half), BF16)],
-        [SMEM] + vmem(7) + [pl.BlockSpec(memory_space=pl.ANY)],
+        [
+            jax.ShapeDtypeStruct((size, half), BF16),
+            jax.ShapeDtypeStruct((frames, columns * height, half), BF16),
+            jax.ShapeDtypeStruct((3, frames + 2, width + 2, height, deep), BF16),
+        ],
+        [SMEM, SMEM] + vmem(9),
         [
             pltpu.VMEM((9 * lat, 2 * frames * cells), BF16),
             pltpu.VMEM((sections, cells, deep), BF16),
-            pltpu.VMEM((3, frames + 2, width + 2, height, deep), BF16),
-            pltpu.VMEM(conv_weight.shape, BF16),
-            pltpu.SemaphoreType.DMA(()),
         ],
     )(
-        where, earlier, latent, weight_mine, weight_other, sums, sums_other,
-        norm_gain.reshape(sections, 1, deep), conv_weight,
-    )
-    partials, tile = results[:sections], results[sections]
+        where, step_size, messages, latent_std, latent_mean, weight_mine, weight_other, sums,
+        sums_other, gain, conv,
+    )
     received = {}
-    for k in (2, 1, 3) if sections == 4 else range(1, sections):
-        received[k] = lax.ppermute(partials[k], "section", [(i, i ^ k) for i in range(sections)])
-    order = jnp.asarray(row_order(height, columns), BF16)
-    decoded = call(
-        finish_kernel, jax.ShapeDtypeStruct((size, half), BF16), vmem(3 + sections)
-    )(
-        tile, conv_bias.reshape(1, half), order, partials[0],
-        *[received[k] for k in range(1, sections)],
-    )
-    return decoded.reshape(frames, height, columns, half)
+    for k in sends + [0]:
+        if k not in partials:
+            partials[k] = call(
+                lambda *refs: tile_kernel(*refs, columns=columns, frames=frames, k=k),
+                jax.ShapeDtypeStruct((size, half), BF16 if k else F32), [SMEM] + vmem(2),
+            )(where, normed, conv)
+        if k:
+            received[k] = lax.ppermute(
+                partials[k], "section", [(i, i ^ k) for i in range(sections)]
+            )
+    return call(
+        finish_kernel, jax.ShapeDtypeStruct((frames, height, columns, half), BF16),
+        vmem(3 + sections), last=True,
+    )(tile, conv_bias, order, partials[0], *[received[k] for k in sends])
 
 
 def sectioned(mesh):
-    def fits(hidden, noisy, in_weight, conv_weight):
+    def fits(hidden, head_weight, noisy, in_weight, conv_weight):
         frames, height, columns, _ = noisy.shape
         sections = mesh.shape["section"]
         cells = height * columns * sections
@@ -413,6 +502,7 @@
             and in_weight.shape[2] == 2 * deep
             and 2 * in_weight.shape[2] == sections * deep
             and deep % 128 == 0
+            and 2 * head_weight.shape[1] == deep
             and height % 16 == 0
             and cells % 128 == 0
         )
@@ -439,7 +529,7 @@
     fits = sectioned(mesh)
 
     def shards(*args):
-        body = sectioned_shards if fits(args[0], args[5], args[9], args[12]) else general_shards
+        body = sectioned_shards if fits(args[0], args[3], args[5], args[9], args[12]) else general_shards
         return body(*args)
 
     return jax.shard_map(

time: 50.1 us -> 41.4 us (0.83)
  local copies, waits for them, and re-layouts: 9.14 us -> 1.08 us
  waiting for transfers between devices: 11.5 us -> 13.7 us
  starting transfers between devices: 13.7 us -> 12 us
    ppermute x4 -> x0, starting transfers between devices: 8.69 us -> none  [the longest x3 5.32 us: sectioned_shards(): lax.ppermute(message, 'section', [(i, i ^ k) for i in range(sections)])]
    all_to_all x0 -> x1, starting transfers between devices: none -> 6.81 us  [sectioned_shards(): messages = lax.all_to_all(message, ('section', 'sp'), 0, 0)]
    all_to_all x0 -> x1, waiting for transfers between devices: none -> 6.16 us  [sectioned_shards(): messages = lax.all_to_all(message, ('section', 'sp'), 0, 0)]
    unnamed x25 -> x0, local copies, waits for them, and re-layouts: 5.34 us -> none
    ppermute x4 -> x0, waiting for transfers between devices: 3.6 us -> none  [the longest x1 1.89 us: passed_along(): return lax.ppermute(value, axis, pairs)]
    reshape x3 -> x0, local copies, waits for them, and re-layouts: 2.95 us -> none  [the longest x1 1.59 us: sectioned_shards(): return decoded.reshape(frames, height, columns, half)]
    transpose x1, local copies, waits for them, and re-layouts: 0.13 us -> 0.96 us  [sectioned_shards(): jnp.transpose(noisy, (3, 0, 2, 1)).reshape(lat, frames * columns * height)]
    reshape x1, local copies, waits for them, and re-layouts: 0.71 us -> 0.12 us  [sectioned_shards(): jnp.transpose(noisy, (3, 0, 2, 1)).reshape(lat, frames * columns * height)]
  transfers between devices with their start and end apart: 9 -> 6, of which waited for: 5 -> 5; matrix products, arithmetic and copies ran while one was open for 10% -> 3% of each run, Pallas kernels for 12% -> 7%
where the time goes in v2:
time: 41.4 us; the launch traced here: 41.1 us
  waiting for transfers between devices  13.7 us (33%)
  Pallas kernels  13.6 us (33%)
  starting transfers between devices  12 us (29%)
  local copies, waits for them, and re-layouts  1.08 us (3%)
  between operations  0.72 us (2%)
    pallas_call x8, Pallas kernels, constrained(): run(*[arg if spec is SMEM else pltpu.with_memory_space_constraint(arg, sp...  13.6 us
    ppermute x3, waiting for transfers between devices, sectioned_shards(): lax.ppermute(partials[k], 'section', [(i, i ^ k) for i in range(sections)])  6.97 us
    all_to_all x1, starting transfers between devices, sectioned_shards(): messages = lax.all_to_all(message, ('section', 'sp'), 0, 0)  6.81 us
    all_to_all x1, waiting for transfers between devices, sectioned_shards(): messages = lax.all_to_all(message, ('section', 'sp'), 0, 0)  6.16 us
    ppermute x3, starting transfers between devices, sectioned_shards(): lax.ppermute(partials[k], 'section', [(i, i ^ k) for i in range(sections)])  4.45 us
    transpose x1, local copies, waits for them, and re-layouts, sectioned_shards(): jnp.transpose(noisy, (3, 0, 2, 1)).reshape(lat, frames * columns * height)  0.96 us
  transfers between devices with their start and end apart: 6, of which 5 were waited for; matrix products, arithmetic and copies ran while one was open for 3% of the time, Pallas kernels for 7%

profile of v2, /device:TPU:0, one launch (start us, length us, event | category | flops | bytes accessed | tf_op | source)
XLA Modules:
  0.0 41.1 jit_solution(6437230030016486146)
XLA Ops:
  0.0 2.0 %shard_map.154._.refs_0_.refs_7_ = f32[72,128]{1,0:T(8,128)S(1)} custom-call(bf16[64,3072]{1,0:T(8,128)(2,1)} %refs_0_.2, f32[2,3072]{1,0:T(2,128)} %refs_1_.2, f32[1,3072]{1,0:T(1,128)} %bitcast.16, bf16[64,3072]{1,0:T(8,128)(2,1)} %bitcast.13, f32[2,128]{1,0:T(2,128)} %bitcast.19), custom_call_target="tpu_custom_call" | custom-call | tf_op jit(solution)/shard_map/pallas_call | solution.py:366
  2.0 0.6 %collective-permute-start = (f32[72,128]{1,0:T(8,128)S(1)}, f32[72,128]{1,0:T(8,128)S(1)}, u32[]{:S(2)}, u32[]{:S(2)}) collective-permute-start(f32[72,128]{1,0:T(8,128)S(1)} %shard_map.154._.refs_0_.refs_7_), channel_id=1, source_target_pairs={{0,2},{2,0},{1,3},{3,1},{4,6},{6,4},{5,7},{7,5},{8,10},{10,8},{9,1... | collective-permute-start | bytes 110600 | tf_op jit(solution)/shard_map/ppermute | solution.py:432
  2.6 1.0 %copy.17 = bf16[16,4,4,16]{3,2,1,0:T(4,128)(2,1)S(1)} copy(bf16[16,4,4,16]{0,2,3,1:T(4,128)(2,1)} %bitcast.15) | data formatting | bytes 16384 | tf_op jit(solution)/shard_map/transpose | solution.py:420
  3.5 0.1 reshape.35.refs_4_
  3.7 1.7 %shard_map.155 = (bf16[64,1024]{1,0:T(8,128)(2,1)S(1)}, f32[1,64]{1,0:T(1,128)S(1)}, f32[1,16]{1,0:T(1,128)S(1)}, f32[1,16]{1,0:T(1,128)S(1)}, bf16[27,128,256]{...) custom-call(f32[72,128]{1,0:T(8,128)S(1)} %shard_map.154._.refs_0_.r, ...), custom_call_target="tpu_custom_call" | custom-call | tf_op jit(solution)/shard_map/pallas_call | solution.py:366
  5.4 0.0 collective-permute-done.refs_1_.refs_8_
  5.4 1.0 %shard_map.156 = bf16[8,16,512]{2,1,0:T(8,128)(2,1)} custom-call(f32[72,128]{1,0:T(8,128)S(1)} %shard_map.154._.refs_0_.refs_7_, f32[72,128]{1,0:T(8,128)S(1)} %collective-permute-done.refs_1_.refs_8_, f32[1,64]{1,0:T(1,128)S(1)} %get-tuple-element.17.refs_2_, bf16[64,1024]{1,0:T(8,128)(2,1)S(1)} %get-tuple-element.18.refs_3_, ...), custom_call_target="tpu_custom_call" | custom-call | tf_op jit(solution)/shard_map/pallas_call | solution.py:366
  6.4 6.8 %all-to-all-start = ((bf16[8,16,512]{2,1,0:T(8,128)(2,1)}), bf16[8,16,512]{2,1,0:T(8,128)(2,1)S(1)}, u32[]{:S(2)}, u32[]{:S(2)}) async-start(bf16[8,16,512]{2,1,0:T(8,128)(2,1)} %shard_map.156), calls=%async_computation | async-start | bytes 262144 | tf_op jit(solution)/shard_map/all_to_all | solution.py:447
  13.2 0.2 collective-permute-start.1
  14.1 0.1 pad_add_fusion.refs_0_
  14.1 0.5 %collective-permute-done.1.refs_6_ = bf16[432,256]{1,0:T(8,128)(2,1)S(1)} collective-permute-done((bf16[432,256]{1,0:T(8,128)(2,1)S(1)}, bf16[432,256]{1,0:T(8,128)(2,1)S(1)}, u32[]{:S(2)}, u32[]{:S(2)}) %collective-permute-start.1) | collective-permute-done | bytes 221216 | tf_op jit(solution)/shard_map/ppermute | solution.py:440
  14.7 6.2 %all-to-all-done.refs_2_ = bf16[8,16,512]{2,1,0:T(8,128)(2,1)S(1)} async-done(((bf16[8,16,512]{2,1,0:T(8,128)(2,1)}), bf16[8,16,512]{2,1,0:T(8,128)(2,1)S(1)}, u32[]{:S(2)}, u32[]{:S(2)}) %all-to-all-start) | async-done | bytes 131104 | tf_op jit(solution)/shard_map/all_to_all | solution.py:447
  20.8 4.0 %shard_map.157 = (bf16[256,256]{1,0:T(8,128)(2,1)S(1)}, bf16[4,64,256]{2,1,0:T(8,128)(2,1)S(1)}, bf16[3,6,18,16,128]{4,3,2,1,0:T(8,128)(2,1)S(1)}) custom-call(s32[3]{0:T(128)S(1)} %pad_add_fusion.refs_0_, f32[1]{0:T(128)S(6)} %copy.18.refs_1_, bf16[8,16,512]{2,1,0:T(8,128)(2,1)S(1)} %all-to-all-done.refs_2_, f32[1,16]{1,0:T(1,128)S(1)} %get-tuple-element.19.refs_3_, ...), custom_call_target="tpu_custom_call" | custom-call | tf_op jit(solution)/shard_map/pallas_call | solution.py:366
  24.9 1.3 %shard_map.160 = bf16[256,256]{1,0:T(8,128)(2,1)S(1)} custom-call(s32[3]{0:T(128)S(1)} %pad_add_fusion.refs_0_, bf16[3,6,18,16,128]{4,3,2,1,0:T(8,128)(2,1)S(1)} %get-tuple-element.27.refs_1_, bf16[27,128,256]{2,1,0:T(8,128)(2,1)S(1)} %get-tuple-element.23.refs_10_.refs_2_), custom_call_target="tpu_custom_call" | custom-call | tf_op jit(solution)/shard_map/pallas_call | solution.py:366
  26.2 1.3 %shard_map.159 = bf16[256,256]{1,0:T(8,128)(2,1)S(1)} custom-call(s32[3]{0:T(128)S(1)} %pad_add_fusion.refs_0_, bf16[3,6,18,16,128]{4,3,2,1,0:T(8,128)(2,1)S(1)} %get-tuple-element.27.refs_1_, bf16[27,128,256]{2,1,0:T(8,128)(2,1)S(1)} %get-tuple-element.23.refs_10_.refs_2_), custom_call_target="tpu_custom_call" | custom-call | tf_op jit(solution)/shard_map/pallas_call | solution.py:366
  27.5 0.5 %collective-permute-start.3 = (bf16[256,256]{1,0:T(8,128)(2,1)S(1)}, bf16[256,256]{1,0:T(8,128)(2,1)S(1)}, u32[]{:S(2)}, u32[]{:S(2)}) collective-permute-start(bf16[256,256]{1,0:T(8,128)(2,1)S(1)} %shard_map.159), channel_id=1, source_target_pairs={{0,12},{4,8},{8,4},{12,0},{1,13},{5,9},{9,5},{13,1},{2,14},{6,10},... | collective-permute-start | bytes 393224 | tf_op jit(solution)/shard_map/ppermute | solution.py:482
  28.0 0.6 %collective-permute-start.4 = (bf16[256,256]{1,0:T(8,128)(2,1)S(1)}, bf16[256,256]{1,0:T(8,128)(2,1)S(1)}, u32[]{:S(2)}, u32[]{:S(2)}) collective-permute-start(bf16[256,256]{1,0:T(8,128)(2,1)S(1)} %shard_map.160), channel_id=1, source_target_pairs={{0,4},{4,0},{8,12},{12,8},{1,5},{5,1},{9,13},{13,9},{2,6},{6,2},{1... | collective-permute-start | bytes 393224 | tf_op jit(solution)/shard_map/ppermute | solution.py:482
  28.6 3.3 %collective-permute-start.2 = (bf16[256,256]{1,0:T(8,128)(2,1)S(1)}, bf16[256,256]{1,0:T(8,128)(2,1)S(1)}, u32[]{:S(2)}, u32[]{:S(2)}) collective-permute-start(bf16[256,256]{1,0:T(8,128)(2,1)S(1)} %get-tuple-element.28), channel_id=1, source_target_pairs={{0,8},{4,12},{8,0},{12,4},{1,9},{5,13},{9,1},{13,5},{2,10},{6,14},... | collective-permute-start | bytes 393224 | tf_op jit(solution)/shard_map/ppermute | solution.py:482
  32.0 1.3 %shard_map.158.refs_0_ = f32[256,256]{1,0:T(8,128)S(1)} custom-call(s32[3]{0:T(128)S(1)} %pad_add_fusion.refs_0_, bf16[3,6,18,16,128]{4,3,2,1,0:T(8,128)(2,1)S(1)} %get-tuple-element.27.refs_1_, bf16[27,128,256]{2,1,0:T(8,128)(2,1)S(1)} %get-tuple-element.23.refs_10_.refs_2_), custom_call_target="tpu_custom_call" | custom-call | tf_op jit(solution)/shard_map/pallas_call | solution.py:366
  33.3 2.6 %collective-permute-done.3.refs_2_ = bf16[256,256]{1,0:T(8,128)(2,1)S(1)} collective-permute-done((bf16[256,256]{1,0:T(8,128)(2,1)S(1)}, bf16[256,256]{1,0:T(8,128)(2,1)S(1)}, u32[]{:S(2)}, u32[]{:S(2)}) %collective-permute-start.3) | collective-permute-done | bytes 131104 | tf_op jit(solution)/shard_map/ppermute | solution.py:482
  35.8 0.7 %collective-permute-done.4.refs_3_ = bf16[256,256]{1,0:T(8,128)(2,1)S(1)} collective-permute-done((bf16[256,256]{1,0:T(8,128)(2,1)S(1)}, bf16[256,256]{1,0:T(8,128)(2,1)S(1)}, u32[]{:S(2)}, u32[]{:S(2)}) %collective-permute-start.4) | collective-permute-done | bytes 131104 | tf_op jit(solution)/shard_map/ppermute | solution.py:482
  36.5 3.7 %collective-permute-done.2.refs_1_ = bf16[256,256]{1,0:T(8,128)(2,1)S(1)} collective-permute-done((bf16[256,256]{1,0:T(8,128)(2,1)S(1)}, bf16[256,256]{1,0:T(8,128)(2,1)S(1)}, u32[]{:S(2)}, u32[]{:S(2)}) %collective-permute-start.2) | collective-permute-done | bytes 131104 | tf_op jit(solution)/shard_map/ppermute | solution.py:482
  40.2 0.9 %shard_map.161 = bf16[4,16,4,256]{3,2,1,0:T(4,128)(2,1)} custom-call(bf16[4,64,256]{2,1,0:T(8,128)(2,1)S(1)} %get-tuple-element.24.tile, f32[1,256]{1,0:T(1,128)S(1)} %get-tuple-element.25.bias, bf16[64,64]{1,0:T(8,128)(2,1)S(1)} %get-tuple-element.26.order, f32[256,256]{1,0:T(8,128)S(1)} %shard_map.158.refs_0_, ...), custom_call_target="tpu_custom_call" | custom-call | tf_op jit(solution)/shard_map/pallas_call | solution.py:366
Async XLA Ops:
  2.0 3.4 %collective-permute-start = (f32[72,128]{1,0:T(8,128)S(1)}, f32[72,128]{1,0:T(8,128)S(1)}, u32[]{:S(2)}, u32[]{:S(2)}) collective-permute-start(f32[72,128]{1,0:T(8,128)S(1)} %shard_map.154._.refs_0_.refs_7_), channel_id=1, source_target_pairs={{0,2},{2,0},{1,3},{3,1},{4,6},{6,4},{5,7},{7,5},{8,10},{10,8},{9,1... | collective-permute-start | bytes 110600 | tf_op jit(solution)/shard_map/ppermute | solution.py:432
  6.4 14.5 %all-to-all-start = ((bf16[8,16,512]{2,1,0:T(8,128)(2,1)}), bf16[8,16,512]{2,1,0:T(8,128)(2,1)S(1)}, u32[]{:S(2)}, u32[]{:S(2)}) async-start(bf16[8,16,512]{2,1,0:T(8,128)(2,1)} %shard_map.156), calls=%async_computation | async-start | bytes 262144 | tf_op jit(solution)/shard_map/all_to_all | solution.py:447
  13.2 1.5 %collective-permute-start.1 = (bf16[432,256]{1,0:T(8,128)(2,1)S(1)}, bf16[432,256]{1,0:T(8,128)(2,1)S(1)}, u32[]{:S(2)}, u32[]{:S(2)}) collective-permute-start(bf16[432,256]{1,0:T(8,128)(2,1)S(1)} %get-tuple-element.21.refs_5_), channel_id=1, source_target_pairs={{0,2},{2,0},{1,3},{3,1},{4,6},{6,4},{5,7},{7,5},{8,10},{10,8},{9,1... | collective-permute-start | bytes 663560 | tf_op jit(solution)/shard_map/ppermute | solution.py:440
  27.5 8.3 %collective-permute-start.3 = (bf16[256,256]{1,0:T(8,128)(2,1)S(1)}, bf16[256,256]{1,0:T(8,128)(2,1)S(1)}, u32[]{:S(2)}, u32[]{:S(2)}) collective-permute-start(bf16[256,256]{1,0:T(8,128)(2,1)S(1)} %shard_map.159), channel_id=1, source_target_pairs={{0,12},{4,8},{8,4},{12,0},{1,13},{5,9},{9,5},{13,1},{2,14},{6,10},... | collective-permute-start | bytes 393224 | tf_op jit(solution)/shard_map/ppermute | solution.py:482
  28.0 8.5 %collective-permute-start.4 = (bf16[256,256]{1,0:T(8,128)(2,1)S(1)}, bf16[256,256]{1,0:T(8,128)(2,1)S(1)}, u32[]{:S(2)}, u32[]{:S(2)}) collective-permute-start(bf16[256,256]{1,0:T(8,128)(2,1)S(1)} %shard_map.160), channel_id=1, source_target_pairs={{0,4},{4,0},{8,12},{12,8},{1,5},{5,1},{9,13},{13,9},{2,6},{6,2},{1... | collective-permute-start | bytes 393224 | tf_op jit(solution)/shard_map/ppermute | solution.py:482
  28.6 11.6 %collective-permute-start.2 = (bf16[256,256]{1,0:T(8,128)(2,1)S(1)}, bf16[256,256]{1,0:T(8,128)(2,1)S(1)}, u32[]{:S(2)}, u32[]{:S(2)}) collective-permute-start(bf16[256,256]{1,0:T(8,128)(2,1)S(1)} %get-tuple-element.28), channel_id=1, source_target_pairs={{0,8},{4,12},{8,0},{12,4},{1,9},{5,13},{9,1},{13,5},{2,10},{6,14},... | collective-permute-start | bytes 393224 | tf_op jit(solution)/shard_map/ppermute | solution.py:482

commit v3 on v2

--- a/solution.py
+++ b/solution.py
@@ -400,6 +400,10 @@
     return table
 
 
+def send_order(sections):
+    return list(range(sections // 2, sections)) + list(range(1, sections // 2))
+
+
 def sectioned_shards(
     hidden, modulation, time_embed, head_weight, head_bias, noisy, step_size,
     latent_mean, latent_std, in_weight, in_bias, norm_gain, conv_weight, conv_bias,
@@ -430,14 +434,9 @@
         + [pltpu.SemaphoreType.DMA((3 + 2 * parts,))],
     )(*head_in)
     sums_other = lax.ppermute(sums, "tp", swap)
-    place, head_bias, latent_std, latent_mean, conv, weight_mine, gain, order, conv_bias = staged(
-        sums, jnp.asarray(token_places(height, width), BF16), head_bias.reshape(1, outs),
-        latent_std.reshape(1, lat), latent_mean.reshape(1, lat),
-        conv_weight, in_weight.reshape(taps * lat, half),
-        norm_gain.reshape(sections, 1, deep), jnp.asarray(row_order(height, columns), BF16),
-        conv_bias.reshape(1, half),
-    )
-    weight_other = lax.ppermute(weight_mine, "tp", swap)
+    place, head_bias = staged(
+        sums, jnp.asarray(token_places(height, width), BF16), head_bias.reshape(1, outs)
+    )
     message = call(
         lambda *refs: message_kernel(
             *refs, features=local * halves, cells=cells, channels=lat
@@ -445,12 +444,18 @@
         jax.ShapeDtypeStruct((sections * members, lat, 2 * cells), BF16), vmem(5),
     )(sums, sums_other, head_bias, place, noisy_rows)
     messages = lax.all_to_all(message, ("section", "sp"), 0, 0)
+    latent_std, latent_mean, conv, weight_mine, gain, order, conv_bias = staged(
+        message, latent_std.reshape(1, lat), latent_mean.reshape(1, lat),
+        conv_weight, in_weight.reshape(taps * lat, half),
+        norm_gain.reshape(sections, 1, deep), jnp.asarray(row_order(height, columns), BF16),
+        conv_bias.reshape(1, half),
+    )
+    weight_other = lax.ppermute(weight_mine, "tp", swap)
     block = jnp.where((mine // per_half) == side, 0, per_half) + mine % per_half
     where = jnp.stack([mine, block, lax.axis_index("sp")]).astype(jnp.int32)
 
     size = frames * columns * height
-    sends = list(range(1, sections))
-    sends = sends[sections // 2 - 1 :] + sends[: sections // 2 - 1]
+    sends = send_order(sections)
     partials = {}
     partials[sends[0]], tile, normed = call(
         lambda *refs: norm_kernel(
@@ -506,6 +511,7 @@
             and height % 16 == 0
             and cells % 128 == 0
         )
+
     return fits
 
 
@@ -529,8 +535,9 @@
     fits = sectioned(mesh)
 
     def shards(*args):
-        body = sectioned_shards if fits(args[0], args[3], args[5], args[9], args[12]) else general_shards
-        return body(*args)
+        if not fits(args[0], args[3], args[5], args[9], args[12]):
+            return general_shards(*args)
+        return sectioned_shards(*args)
 
     return jax.shard_map(
         shards,

time: 41.4 us -> 40.7 us (0.983)
  waiting for transfers between devices: 13.7 us -> 11.1 us
  Pallas kernels: 13.6 us -> 15.3 us
    all_to_all x1, waiting for transfers between devices: 6.16 us -> 3.58 us  [sectioned_shards(): messages = lax.all_to_all(message, ('section', 'sp'), 0, 0)]
    pallas_call x8 -> x9, Pallas kernels: 13.6 us -> 15.3 us  [constrained(): run(*[arg if spec is SMEM else pltpu.with_memory_space_constraint(arg, sp...]
  transfers between devices with their start and end apart: 6 -> 6, of which waited for: 5 -> 5; matrix products, arithmetic and copies ran while one was open for 3% -> 3% of each run, Pallas kernels for 7% -> 12%
where the time goes in v3:
time: 40.7 us; the launch traced here: 40.4 us
  Pallas kernels  15.3 us (38%)
  starting transfers between devices  12.1 us (30%)
  waiting for transfers between devices  11.1 us (27%)
  local copies, waits for them, and re-layouts  1.08 us (3%)
  between operations  0.73 us (2%)
    pallas_call x9, Pallas kernels, constrained(): run(*[arg if spec is SMEM else pltpu.with_memory_space_constraint(arg, sp...  15.3 us
    ppermute x3, waiting for transfers between devices, sectioned_shards(): lax.ppermute(partials[k], 'section', [(i, i ^ k) for i in range(sections)])  6.98 us
    all_to_all x1, starting transfers between devices, sectioned_shards(): messages = lax.all_to_all(message, ('section', 'sp'), 0, 0)  6.81 us
    ppermute x3, starting transfers between devices, sectioned_shards(): lax.ppermute(partials[k], 'section', [(i, i ^ k) for i in range(sections)])  4.45 us
    all_to_all x1, waiting for transfers between devices, sectioned_shards(): messages = lax.all_to_all(message, ('section', 'sp'), 0, 0)  3.58 us
    transpose x1, local copies, waits for them, and re-layouts, sectioned_shards(): jnp.transpose(noisy, (3, 0, 2, 1)).reshape(lat, frames * columns * height)  0.96 us
  transfers between devices with their start and end apart: 6, of which 5 were waited for; matrix products, arithmetic and copies ran while one was open for 3% of the time, Pallas kernels for 12%

profile of v3, /device:TPU:0, one launch (start us, length us, event | category | flops | bytes accessed | tf_op | source)
XLA Modules:
  0.0 40.4 jit_solution(14950433491087559887)
XLA Ops:
  0.0 2.0 %shard_map.154._.refs_0_.refs_7_ = f32[72,128]{1,0:T(8,128)S(1)} custom-call(bf16[64,3072]{1,0:T(8,128)(2,1)} %refs_0_.2, f32[2,3072]{1,0:T(2,128)} %refs_1_.2, f32[1,3072]{1,0:T(1,128)} %bitcast.16, bf16[64,3072]{1,0:T(8,128)(2,1)} %bitcast.13, f32[2,128]{1,0:T(2,128)} %bitcast.18), custom_call_target="tpu_custom_call" | custom-call | tf_op jit(solution)/shard_map/pallas_call | solution.py:366
  2.0 0.6 %collective-permute-start = (f32[72,128]{1,0:T(8,128)S(1)}, f32[72,128]{1,0:T(8,128)S(1)}, u32[]{:S(2)}, u32[]{:S(2)}) collective-permute-start(f32[72,128]{1,0:T(8,128)S(1)} %shard_map.154._.refs_0_.refs_7_), channel_id=1, source_target_pairs={{0,2},{2,0},{1,3},{3,1},{4,6},{6,4},{5,7},{7,5},{8,10},{10,8},{9,1... | collective-permute-start | bytes 110600 | tf_op jit(solution)/shard_map/ppermute | solution.py:436
  2.6 1.0 %copy.17 = bf16[16,4,4,16]{3,2,1,0:T(4,128)(2,1)S(1)} copy(bf16[16,4,4,16]{0,2,3,1:T(4,128)(2,1)} %bitcast.15) | data formatting | bytes 16384 | tf_op jit(solution)/shard_map/transpose | solution.py:424
  3.5 0.1 reshape.30.refs_4_
  3.7 0.9 %shard_map.155 = (bf16[64,1024]{1,0:T(8,128)(2,1)S(1)}, f32[1,64]{1,0:T(1,128)S(1)}) custom-call(f32[72,128]{1,0:T(8,128)S(1)} %shard_map.154._.refs_0_.refs_7_, bf16[64,1024]{1,0:T(8,128)(2,1)} %constant.40.clone.refs_0_, f32[1,64]{1,0:T(1,128)} %bitcast.20), custom_call_target="tpu_custom_call" | custom-call | tf_op jit(solution)/shard_map/pallas_call | solution.py:366
  4.6 0.0 collective-permute-done.refs_1_.refs_8_
  4.6 1.0 %shard_map.156._ = bf16[8,16,512]{2,1,0:T(8,128)(2,1)} custom-call(f32[72,128]{1,0:T(8,128)S(1)} %shard_map.154._.refs_0_.refs_7_, f32[72,128]{1,0:T(8,128)S(1)} %collective-permute-done.refs_1_.refs_8_, f32[1,64]{1,0:T(1,128)S(1)} %get-tuple-element.17.refs_2_, bf16[64,1024]{1,0:T(8,128)(2,1)S(1)} %get-tuple-element.18.refs_3_, ...), custom_call_target="tpu_custom_call" | custom-call | tf_op jit(solution)/shard_map/pallas_call | solution.py:366
  5.6 6.8 %all-to-all-start = ((bf16[8,16,512]{2,1,0:T(8,128)(2,1)}), bf16[8,16,512]{2,1,0:T(8,128)(2,1)S(1)}, u32[]{:S(2)}, u32[]{:S(2)}) async-start(bf16[8,16,512]{2,1,0:T(8,128)(2,1)} %shard_map.156._), calls=%async_computation | async-start | bytes 262144 | tf_op jit(solution)/shard_map/all_to_all | solution.py:446
  12.4 2.5 %shard_map.157 = (f32[1,16]{1,0:T(1,128)S(1)}, f32[1,16]{1,0:T(1,128)S(1)}, bf16[27,128,256]{2,1,0:T(8,128)(2,1)S(1)}, bf16[432,256]{1,0:T(8,128)(2,1)S(1)}, f32...) custom-call(bf16[8,16,512]{2,1,0:T(8,128)(2,1)} %shard_map.156._, f32[1,16]{1,0:T(1,128)} %bitcast.21, ...), custom_call_target="tpu_custom_call" | custom-call | tf_op jit(solution)/shard_map/pallas_call | solution.py:366
  14.9 0.3 collective-permute-start.1
  15.9 0.1 pad_add_fusion.refs_0_
  16.0 0.5 %collective-permute-done.1.refs_6_ = bf16[432,256]{1,0:T(8,128)(2,1)S(1)} collective-permute-done((bf16[432,256]{1,0:T(8,128)(2,1)S(1)}, bf16[432,256]{1,0:T(8,128)(2,1)S(1)}, u32[]{:S(2)}, u32[]{:S(2)}) %collective-permute-start.1) | collective-permute-done | bytes 221216 | tf_op jit(solution)/shard_map/ppermute | solution.py:453
  16.5 3.6 %all-to-all-done.refs_2_ = bf16[8,16,512]{2,1,0:T(8,128)(2,1)S(1)} async-done(((bf16[8,16,512]{2,1,0:T(8,128)(2,1)}), bf16[8,16,512]{2,1,0:T(8,128)(2,1)S(1)}, u32[]{:S(2)}, u32[]{:S(2)}) %all-to-all-start) | async-done | bytes 131104 | tf_op jit(solution)/shard_map/all_to_all | solution.py:446
  20.1 4.0 %shard_map.158 = (bf16[256,256]{1,0:T(8,128)(2,1)S(1)}, bf16[4,64,256]{2,1,0:T(8,128)(2,1)S(1)}, bf16[3,6,18,16,128]{4,3,2,1,0:T(8,128)(2,1)S(1)}) custom-call(s32[3]{0:T(128)S(1)} %pad_add_fusion.refs_0_, f32[1]{0:T(128)S(6)} %copy.18.refs_1_, bf16[8,16,512]{2,1,0:T(8,128)(2,1)S(1)} %all-to-all-done.refs_2_, f32[1,16]{1,0:T(1,128)S(1)} %get-tuple-element.19.refs_3_, ...), custom_call_target="tpu_custom_call" | custom-call | tf_op jit(solution)/shard_map/pallas_call | solution.py:366
  24.1 1.3 %shard_map.161 = bf16[256,256]{1,0:T(8,128)(2,1)S(1)} custom-call(s32[3]{0:T(128)S(1)} %pad_add_fusion.refs_0_, bf16[3,6,18,16,128]{4,3,2,1,0:T(8,128)(2,1)S(1)} %get-tuple-element.27.refs_1_, bf16[27,128,256]{2,1,0:T(8,128)(2,1)S(1)} %get-tuple-element.23.refs_10_.refs_2_), custom_call_target="tpu_custom_call" | custom-call | tf_op jit(solution)/shard_map/pallas_call | solution.py:366
  25.4 1.3 %shard_map.160 = bf16[256,256]{1,0:T(8,128)(2,1)S(1)} custom-call(s32[3]{0:T(128)S(1)} %pad_add_fusion.refs_0_, bf16[3,6,18,16,128]{4,3,2,1,0:T(8,128)(2,1)S(1)} %get-tuple-element.27.refs_1_, bf16[27,128,256]{2,1,0:T(8,128)(2,1)S(1)} %get-tuple-element.23.refs_10_.refs_2_), custom_call_target="tpu_custom_call" | custom-call | tf_op jit(solution)/shard_map/pallas_call | solution.py:366
  26.7 0.5 %collective-permute-start.3 = (bf16[256,256]{1,0:T(8,128)(2,1)S(1)}, bf16[256,256]{1,0:T(8,128)(2,1)S(1)}, u32[]{:S(2)}, u32[]{:S(2)}) collective-permute-start(bf16[256,256]{1,0:T(8,128)(2,1)S(1)} %shard_map.160), channel_id=1, source_target_pairs={{0,12},{4,8},{8,4},{12,0},{1,13},{5,9},{9,5},{13,1},{2,14},{6,10},... | collective-permute-start | bytes 393224 | tf_op jit(solution)/shard_map/ppermute | solution.py:487
  27.2 0.6 %collective-permute-start.4 = (bf16[256,256]{1,0:T(8,128)(2,1)S(1)}, bf16[256,256]{1,0:T(8,128)(2,1)S(1)}, u32[]{:S(2)}, u32[]{:S(2)}) collective-permute-start(bf16[256,256]{1,0:T(8,128)(2,1)S(1)} %shard_map.161), channel_id=1, source_target_pairs={{0,4},{4,0},{8,12},{12,8},{1,5},{5,1},{9,13},{13,9},{2,6},{6,2},{1... | collective-permute-start | bytes 393224 | tf_op jit(solution)/shard_map/ppermute | solution.py:487
  27.8 3.3 %collective-permute-start.2 = (bf16[256,256]{1,0:T(8,128)(2,1)S(1)}, bf16[256,256]{1,0:T(8,128)(2,1)S(1)}, u32[]{:S(2)}, u32[]{:S(2)}) collective-permute-start(bf16[256,256]{1,0:T(8,128)(2,1)S(1)} %get-tuple-element.28), channel_id=1, source_target_pairs={{0,8},{4,12},{8,0},{12,4},{1,9},{5,13},{9,1},{13,5},{2,10},{6,14},... | collective-permute-start | bytes 393224 | tf_op jit(solution)/shard_map/ppermute | solution.py:487
  31.2 1.3 %shard_map.159.refs_0_ = f32[256,256]{1,0:T(8,128)S(1)} custom-call(s32[3]{0:T(128)S(1)} %pad_add_fusion.refs_0_, bf16[3,6,18,16,128]{4,3,2,1,0:T(8,128)(2,1)S(1)} %get-tuple-element.27.refs_1_, bf16[27,128,256]{2,1,0:T(8,128)(2,1)S(1)} %get-tuple-element.23.refs_10_.refs_2_), custom_call_target="tpu_custom_call" | custom-call | tf_op jit(solution)/shard_map/pallas_call | solution.py:366
  32.5 2.6 %collective-permute-done.3.refs_2_ = bf16[256,256]{1,0:T(8,128)(2,1)S(1)} collective-permute-done((bf16[256,256]{1,0:T(8,128)(2,1)S(1)}, bf16[256,256]{1,0:T(8,128)(2,1)S(1)}, u32[]{:S(2)}, u32[]{:S(2)}) %collective-permute-start.3) | collective-permute-done | bytes 131104 | tf_op jit(solution)/shard_map/ppermute | solution.py:487
  35.1 1.2 %collective-permute-done.4.refs_3_ = bf16[256,256]{1,0:T(8,128)(2,1)S(1)} collective-permute-done((bf16[256,256]{1,0:T(8,128)(2,1)S(1)}, bf16[256,256]{1,0:T(8,128)(2,1)S(1)}, u32[]{:S(2)}, u32[]{:S(2)}) %collective-permute-start.4) | collective-permute-done | bytes 131104 | tf_op jit(solution)/shard_map/ppermute | solution.py:487
  36.3 3.2 %collective-permute-done.2.refs_1_ = bf16[256,256]{1,0:T(8,128)(2,1)S(1)} collective-permute-done((bf16[256,256]{1,0:T(8,128)(2,1)S(1)}, bf16[256,256]{1,0:T(8,128)(2,1)S(1)}, u32[]{:S(2)}, u32[]{:S(2)}) %collective-permute-start.2) | collective-permute-done | bytes 131104 | tf_op jit(solution)/shard_map/ppermute | solution.py:487
  39.5 0.9 %shard_map.162 = bf16[4,16,4,256]{3,2,1,0:T(4,128)(2,1)} custom-call(bf16[4,64,256]{2,1,0:T(8,128)(2,1)S(1)} %get-tuple-element.24.tile, f32[1,256]{1,0:T(1,128)S(1)} %get-tuple-element.25.bias, bf16[64,64]{1,0:T(8,128)(2,1)S(1)} %get-tuple-element.26.order, f32[256,256]{1,0:T(8,128)S(1)} %shard_map.159.refs_0_, ...), custom_call_target="tpu_custom_call" | custom-call | tf_op jit(solution)/shard_map/pallas_call | solution.py:366
Async XLA Ops:
  2.0 2.6 %collective-permute-start = (f32[72,128]{1,0:T(8,128)S(1)}, f32[72,128]{1,0:T(8,128)S(1)}, u32[]{:S(2)}, u32[]{:S(2)}) collective-permute-start(f32[72,128]{1,0:T(8,128)S(1)} %shard_map.154._.refs_0_.refs_7_), channel_id=1, source_target_pairs={{0,2},{2,0},{1,3},{3,1},{4,6},{6,4},{5,7},{7,5},{8,10},{10,8},{9,1... | collective-permute-start | bytes 110600 | tf_op jit(solution)/shard_map/ppermute | solution.py:436
  5.6 14.4 %all-to-all-start = ((bf16[8,16,512]{2,1,0:T(8,128)(2,1)}), bf16[8,16,512]{2,1,0:T(8,128)(2,1)S(1)}, u32[]{:S(2)}, u32[]{:S(2)}) async-start(bf16[8,16,512]{2,1,0:T(8,128)(2,1)} %shard_map.156._), calls=%async_computation | async-start | bytes 262144 | tf_op jit(solution)/shard_map/all_to_all | solution.py:446
  14.9 1.5 %collective-permute-start.1 = (bf16[432,256]{1,0:T(8,128)(2,1)S(1)}, bf16[432,256]{1,0:T(8,128)(2,1)S(1)}, u32[]{:S(2)}, u32[]{:S(2)}) collective-permute-start(bf16[432,256]{1,0:T(8,128)(2,1)S(1)} %get-tuple-element.21.refs_5_), channel_id=1, source_target_pairs={{0,2},{2,0},{1,3},{3,1},{4,6},{6,4},{5,7},{7,5},{8,10},{10,8},{9,1... | collective-permute-start | bytes 663560 | tf_op jit(solution)/shard_map/ppermute | solution.py:453
  26.7 8.3 %collective-permute-start.3 = (bf16[256,256]{1,0:T(8,128)(2,1)S(1)}, bf16[256,256]{1,0:T(8,128)(2,1)S(1)}, u32[]{:S(2)}, u32[]{:S(2)}) collective-permute-start(bf16[256,256]{1,0:T(8,128)(2,1)S(1)} %shard_map.160), channel_id=1, source_target_pairs={{0,12},{4,8},{8,4},{12,0},{1,13},{5,9},{9,5},{13,1},{2,14},{6,10},... | collective-permute-start | bytes 393224 | tf_op jit(solution)/shard_map/ppermute | solution.py:487
  27.2 9.0 %collective-permute-start.4 = (bf16[256,256]{1,0:T(8,128)(2,1)S(1)}, bf16[256,256]{1,0:T(8,128)(2,1)S(1)}, u32[]{:S(2)}, u32[]{:S(2)}) collective-permute-start(bf16[256,256]{1,0:T(8,128)(2,1)S(1)} %shard_map.161), channel_id=1, source_target_pairs={{0,4},{4,0},{8,12},{12,8},{1,5},{5,1},{9,13},{13,9},{2,6},{6,2},{1... | collective-permute-start | bytes 393224 | tf_op jit(solution)/shard_map/ppermute | solution.py:487
  27.8 11.6 %collective-permute-start.2 = (bf16[256,256]{1,0:T(8,128)(2,1)S(1)}, bf16[256,256]{1,0:T(8,128)(2,1)S(1)}, u32[]{:S(2)}, u32[]{:S(2)}) collective-permute-start(bf16[256,256]{1,0:T(8,128)(2,1)S(1)} %get-tuple-element.28), channel_id=1, source_target_pairs={{0,8},{4,12},{8,0},{12,4},{1,9},{5,13},{9,1},{13,5},{2,10},{6,14},... | collective-permute-start | bytes 393224 | tf_op jit(solution)/shard_map/ppermute | solution.py:487

commit v4 on v3

--- a/solution.py
+++ b/solution.py
@@ -116,8 +116,8 @@
 
 
 def head_kernel(
-    hidden_hbm, modulation_hbm, embed_hbm, weight_hbm, bias_hbm, out,
-    hidden, modulation, time_embed, weight, in_bias, arrived, *, parts
+    hidden_hbm, modulation_hbm, embed_hbm, weight_hbm, bias_hbm, place_hbm, shift_hbm,
+    out, place, head_bias, hidden, modulation, time_embed, weight, in_bias, arrived, *, parts
 ):
     tokens, features = hidden.shape
     outs = weight.shape[0]
@@ -127,6 +127,10 @@
         for i, (source, target) in enumerate(
             ((modulation_hbm, modulation), (embed_hbm, time_embed), (bias_hbm, in_bias))
         )
+    ]
+    later = [
+        pltpu.make_async_copy(source, target, arrived.at[3 + 2 * parts + i])
+        for i, (source, target) in enumerate(((place_hbm, place), (shift_hbm, head_bias)))
     ]
     large = []
     for part in range(parts):
@@ -139,7 +143,7 @@
                 for i, (source, target) in enumerate(((hidden_hbm, hidden), (weight_hbm, weight)))
             ]
         )
-    for copy in small + [copy for pair in large for copy in pair]:
+    for copy in small + [copy for pair in large for copy in pair] + later:
         copy.start()
     for copy in small:
         copy.wait()
@@ -178,13 +182,19 @@
     out[tokens + 1 : tokens + 1 + biases, :] = in_bias[...]
     rest = out.shape[0] - tokens - 1 - biases
     out[tokens + 1 + biases :, :] = jnp.zeros((rest, out.shape[1]), F32)
-
-
-def stage_kernel(_, *refs):
-    count = (len(refs) - 1) // 2
+    for copy in later:
+        copy.wait()
+
+
+def stage_kernel(_, *refs, scalar):
+    arrived, refs = refs[-1], refs[:-1]
+    if scalar:
+        refs[-1][...] = jnp.full(refs[-1].shape, refs[0][0], F32)
+        refs = refs[1:-1]
+    count = len(refs) // 2
     copies = [
-        pltpu.make_async_copy(source, target, refs[-1].at[i])
-        for i, (source, target) in enumerate(zip(refs[:count], refs[count:-1], strict=True))
+        pltpu.make_async_copy(source, target, arrived.at[i])
+        for i, (source, target) in enumerate(zip(refs[:count], refs[count:], strict=True))
     ]
     for copy in copies:
         copy.start()
@@ -235,28 +245,30 @@
 
 def conv_tile(normed, conv, first_column, columns, frames):
     height, deep = normed.shape[3:]
-    half = conv.shape[2]
+    taps, _, half = conv.shape
     size = frames * columns * height
-    total = jnp.zeros((size, half), F32)
-    for a in range(3):
-        for b in range(3):
-            window = jnp.concatenate(
-                [
-                    normed[b, a : a + frames, pl.ds(first_column + e, columns)].reshape(size, deep)
-                    for e in range(3)
-                ],
-                axis=1,
-            )
-            taps = conv[9 * a + 3 * b : 9 * a + 3 * b + 3].reshape(3 * deep, half)
-            total = total + jnp.dot(window, taps, preferred_element_type=F32)
+    total = 0.0
+    for first in range(0, taps, 2):
+        group = range(first, min(first + 2, taps))
+        window = jnp.concatenate(
+            [
+                normed[
+                    t // 3 % 3, t // 9 : t // 9 + frames, pl.ds(first_column + t % 3, columns)
+                ].reshape(size, deep)
+                for t in group
+            ],
+            axis=1,
+        )
+        weight = conv[first : first + len(group)].reshape(len(group) * deep, half)
+        total = total + jnp.dot(window, weight, preferred_element_type=F32)
     return total
 
 
 def norm_kernel(
-    where, step, messages, std, mean, weight_mine, weight_other, sums_mine, sums_other, gain, conv,
+    step, messages, std, mean, weight_mine, weight_other, sums_mine, sums_other, gain, conv,
     partial, tile, normed, rolled, blocks, *, frames, height, width, tokens, k, sections, members
 ):
-    mine, block, member = where[0], where[1], where[2]
+    mine, side, member = (lax.axis_index(axis) for axis in ("section", "tp", "sp"))
     first_frame = member * frames - 2
     cells = height * width
     lat = messages.shape[1]
@@ -265,7 +277,8 @@
     deep = gain.shape[2]
     columns = tile.shape[1] // height
     per_half = half // deep
-    rest = (step[0], std, mean, sections, members, cells)
+    block = jnp.where((mine // per_half) == side, 0, per_half) + mine % per_half
+    rest = (step[:, 0:1], std, mean, sections, members, cells)
     earlier = latents(messages, jnp.maximum(member - 1, 0), *rest)
     earlier = jnp.where(member > 0, earlier, 0.0)
     x = jnp.concatenate([earlier, latents(messages, member, *rest)], axis=1)
@@ -323,8 +336,8 @@
     partial[...] = conv_tile(normed, conv, (mine ^ k) * columns, columns, frames).astype(BF16)
 
 
-def tile_kernel(where, normed, conv, partial, *, columns, frames, k):
-    partial[...] = conv_tile(normed, conv, (where[0] ^ k) * columns, columns, frames).astype(
+def tile_kernel(normed, conv, partial, *, columns, frames, k):
+    partial[...] = conv_tile(normed, conv, (lax.axis_index("section") ^ k) * columns, columns, frames).astype(
         partial.dtype
     )
 
@@ -373,11 +386,16 @@
     return constrained
 
 
-def staged(after, *arrays):
+def staged(after, *arrays, scalar=None):
+    shapes = [jax.ShapeDtypeStruct(x.shape, x.dtype) for x in arrays]
+    first, specs = [after], vmem(1)
+    if scalar is not None:
+        shapes.append(jax.ShapeDtypeStruct((1, 128), F32))
+        first, specs = first + [scalar], specs + [SMEM]
     return call(
-        stage_kernel, [jax.ShapeDtypeStruct(x.shape, x.dtype) for x in arrays],
-        vmem(1) + [HBM] * len(arrays), [pltpu.SemaphoreType.DMA((len(arrays),))],
-    )(after, *arrays)
+        lambda *refs: stage_kernel(*refs, scalar=scalar is not None), shapes,
+        specs + [HBM] * len(arrays), [pltpu.SemaphoreType.DMA((len(arrays),))],
+    )(*first, *arrays)
 
 
 def token_places(height, width):
@@ -401,7 +419,8 @@
 
 
 def send_order(sections):
-    return list(range(sections // 2, sections)) + list(range(1, sections // 2))
+    order = list(range(1, sections))
+    return sorted(order, key=lambda k: (k == sections - 1, -k))
 
 
 def sectioned_shards(
@@ -417,7 +436,6 @@
     outs = head_weight.shape[1]
     deep = conv_weight.shape[1]
     per_half = half // deep
-    mine, side = lax.axis_index("section"), lax.axis_index("tp")
     swap = [(i, i ^ 1) for i in range(halves)]
     taps = in_weight.shape[0]
 
@@ -427,16 +445,16 @@
         hidden, modulation, time_embed.reshape(1, local), head_weight.T,
         in_bias.reshape(per_half, deep),
     )
-    sums = call(
+    kept = (jnp.asarray(token_places(height, width), BF16), head_bias.reshape(1, outs))
+    sums, place, head_bias = call(
         lambda *refs: head_kernel(*refs, parts=parts),
-        jax.ShapeDtypeStruct((tokens + 8, 2 * outs), F32), [HBM] * 5,
+        [jax.ShapeDtypeStruct((tokens + 8, 2 * outs), F32)]
+        + [jax.ShapeDtypeStruct(x.shape, x.dtype) for x in kept],
+        [HBM] * (len(head_in) + len(kept)),
         [pltpu.VMEM(x.shape, x.dtype) for x in head_in]
-        + [pltpu.SemaphoreType.DMA((3 + 2 * parts,))],
-    )(*head_in)
+        + [pltpu.SemaphoreType.DMA((5 + 2 * parts,))],
+    )(*head_in, *kept)
     sums_other = lax.ppermute(sums, "tp", swap)
-    place, head_bias = staged(
-        sums, jnp.asarray(token_places(height, width), BF16), head_bias.reshape(1, outs)
-    )
     message = call(
         lambda *refs: message_kernel(
             *refs, features=local * halves, cells=cells, channels=lat
@@ -444,15 +462,13 @@
         jax.ShapeDtypeStruct((sections * members, lat, 2 * cells), BF16), vmem(5),
     )(sums, sums_other, head_bias, place, noisy_rows)
     messages = lax.all_to_all(message, ("section", "sp"), 0, 0)
-    latent_std, latent_mean, conv, weight_mine, gain, order, conv_bias = staged(
+    latent_std, latent_mean, conv, weight_mine, gain, order, conv_bias, step = staged(
         message, latent_std.reshape(1, lat), latent_mean.reshape(1, lat),
         conv_weight, in_weight.reshape(taps * lat, half),
         norm_gain.reshape(sections, 1, deep), jnp.asarray(row_order(height, columns), BF16),
-        conv_bias.reshape(1, half),
+        conv_bias.reshape(1, half), scalar=step_size,
     )
     weight_other = lax.ppermute(weight_mine, "tp", swap)
-    block = jnp.where((mine // per_half) == side, 0, per_half) + mine % per_half
-    where = jnp.stack([mine, block, lax.axis_index("sp")]).astype(jnp.int32)
 
     size = frames * columns * height
     sends = send_order(sections)
@@ -467,13 +483,13 @@
             jax.ShapeDtypeStruct((frames, columns * height, half), BF16),
             jax.ShapeDtypeStruct((3, frames + 2, width + 2, height, deep), BF16),
         ],
-        [SMEM, SMEM] + vmem(9),
+        vmem(10),
         [
             pltpu.VMEM((9 * lat, 2 * frames * cells), BF16),
             pltpu.VMEM((sections, cells, deep), BF16),
         ],
     )(
-        where, step_size, messages, latent_std, latent_mean, weight_mine, weight_other, sums,
+        step, messages, latent_std, latent_mean, weight_mine, weight_other, sums,
         sums_other, gain, conv,
     )
     received = {}
@@ -481,8 +497,8 @@
         if k not in partials:
             partials[k] = call(
                 lambda *refs: tile_kernel(*refs, columns=columns, frames=frames, k=k),
-                jax.ShapeDtypeStruct((size, half), BF16 if k else F32), [SMEM] + vmem(2),
-            )(where, normed, conv)
+                jax.ShapeDtypeStruct((size, half), BF16 if k else F32), vmem(2),
+            )(normed, conv)
         if k:
             received[k] = lax.ppermute(
                 partials[k], "section", [(i, i ^ k) for i in range(sections)]

time: 40.7 us -> 39 us (0.958)
  Pallas kernels: 15.3 us -> 11.6 us
  waiting for transfers between devices: 11.1 us -> 14.1 us
  starting transfers between devices: 12.1 us -> 11.2 us
    pallas_call x9 -> x8, Pallas kernels: 15.3 us -> 11.6 us  [constrained(): run(*[arg if spec is SMEM else pltpu.with_memory_space_constraint(arg, sp...]
    ppermute x3, waiting for transfers between devices: 6.98 us -> 9.87 us  [sectioned_shards(): lax.ppermute(partials[k], 'section', [(i, i ^ k) for i in range(sections)])]
    ppermute x3, starting transfers between devices: 4.45 us -> 3.55 us  [sectioned_shards(): lax.ppermute(partials[k], 'section', [(i, i ^ k) for i in range(sections)])]
    ppermute x1, waiting for transfers between devices: 0.53 us -> 1.36 us  [sectioned_shards(): weight_other = lax.ppermute(weight_mine, 'tp', swap)]
    all_to_all x1, waiting for transfers between devices: 3.58 us -> 2.85 us  [sectioned_shards(): messages = lax.all_to_all(message, ('section', 'sp'), 0, 0)]
  transfers between devices with their start and end apart: 6 -> 6, of which waited for: 5 -> 5; matrix products, arithmetic and copies ran while one was open for 3% -> 3% of each run, Pallas kernels for 12% -> 8%
where the time goes in v4:
time: 39 us; the launch traced here: 38.6 us
  waiting for transfers between devices  14.1 us (36%)
  Pallas kernels  11.6 us (30%)
  starting transfers between devices  11.2 us (29%)
  local copies, waits for them, and re-layouts  1.08 us (3%)
  between operations  0.72 us (2%)
    pallas_call x8, Pallas kernels, constrained(): run(*[arg if spec is SMEM else pltpu.with_memory_space_constraint(arg, sp...  11.6 us
    ppermute x3, waiting for transfers between devices, sectioned_shards(): lax.ppermute(partials[k], 'section', [(i, i ^ k) for i in range(sections)])  9.87 us
    all_to_all x1, starting transfers between devices, sectioned_shards(): messages = lax.all_to_all(message, ('section', 'sp'), 0, 0)  6.9 us
    ppermute x3, starting transfers between devices, sectioned_shards(): lax.ppermute(partials[k], 'section', [(i, i ^ k) for i in range(sections)])  3.55 us
    all_to_all x1, waiting for transfers between devices, sectioned_shards(): messages = lax.all_to_all(message, ('section', 'sp'), 0, 0)  2.85 us
    ppermute x1, waiting for transfers between devices, sectioned_shards(): weight_other = lax.ppermute(weight_mine, 'tp', swap)  1.36 us
    transpose x1, local copies, waits for them, and re-layouts, sectioned_shards(): jnp.transpose(noisy, (3, 0, 2, 1)).reshape(lat, frames * columns * height)  0.96 us
  transfers between devices with their start and end apart: 6, of which 5 were waited for; matrix products, arithmetic and copies ran while one was open for 3% of the time, Pallas kernels for 8%

profile of v4, /device:TPU:0, one launch (start us, length us, event | category | flops | bytes accessed | tf_op | source)
XLA Modules:
  0.0 38.6 jit_solution(5684922290974851810)
XLA Ops:
  0.0 2.0 %shard_map.154 = (f32[72,128]{1,0:T(8,128)S(1)}, bf16[64,1024]{1,0:T(8,128)(2,1)S(1)}, f32[1,64]{1,0:T(1,128)S(1)}) custom-call(bf16[64,3072]{1,0:T(8,128)(2,1)} %refs_0_.1, f32[2,3072]{1,0:T(2,128)} %refs_1_.2, f32[1,3072]{1,0:T(1,128)} %bitcast.13, bf16[64,3072]{1,0:T(8,128)(2,1)} %bitcast.10, f32[2,128]{1,0:T(2,128)} %bitcast.16, ...), custom_call_target="tpu_custom_call" | custom-call | tf_op jit(solution)/shard_map/pallas_call | solution.py:379
  2.0 0.6 %collective-permute-start = (f32[72,128]{1,0:T(8,128)S(1)}, f32[72,128]{1,0:T(8,128)S(1)}, u32[]{:S(2)}, u32[]{:S(2)}) collective-permute-start(f32[72,128]{1,0:T(8,128)S(1)} %get-tuple-element.19.refs_0_.refs_6_), channel_id=1, source_target_pairs={{0,2},{2,0},{1,3},{3,1},{4,6},{6,4},{5,7},{7,5},{8,10},{10,8},{9,1... | collective-permute-start | bytes 110600 | tf_op jit(solution)/shard_map/ppermute | solution.py:457
  2.6 1.0 %copy.17 = bf16[16,4,4,16]{3,2,1,0:T(4,128)(2,1)S(1)} copy(bf16[16,4,4,16]{0,2,3,1:T(4,128)(2,1)} %bitcast.12) | data formatting | bytes 16384 | tf_op jit(solution)/shard_map/transpose | solution.py:442
  3.5 0.1 reshape.30.refs_4_
  3.7 0.0 collective-permute-done.refs_1_.refs_7_
  3.7 1.0 %shard_map.155.refs_0_ = bf16[8,16,512]{2,1,0:T(8,128)(2,1)} custom-call(f32[72,128]{1,0:T(8,128)S(1)} %get-tuple-element.19.refs_0_.refs_6_, f32[72,128]{1,0:T(8,128)S(1)} %collective-permute-done.refs_1_.refs_7_, f32[1,64]{1,0:T(1,128)S(1)} %get-tuple-element.20.refs_2_, bf16[64,1024]{1,0:T(8,128)(2,1)S(1)} %get-tuple-element.21.refs_3_, ...), custom_call_target="tpu_custom_call" | custom-call | tf_op jit(solution)/shard_map/pallas_call | solution.py:379
  4.7 6.9 %all-to-all-start = ((bf16[8,16,512]{2,1,0:T(8,128)(2,1)}), bf16[8,16,512]{2,1,0:T(8,128)(2,1)S(1)}, u32[]{:S(2)}, u32[]{:S(2)}) async-start(bf16[8,16,512]{2,1,0:T(8,128)(2,1)} %shard_map.155.refs_0_), calls=%async_computation | async-start | bytes 262144 | tf_op jit(solution)/shard_map/all_to_all | solution.py:464
  12.3 2.5 %shard_map.156 = (f32[1,16]{1,0:T(1,128)S(1)}, f32[1,16]{1,0:T(1,128)S(1)}, bf16[27,128,256]{2,1,0:T(8,128)(2,1)S(1)}, bf16[432,256]{1,0:T(8,128)(2,1)S(1)}, f32...) custom-call(bf16[8,16,512]{2,1,0:T(8,128)(2,1)} %shard_map.155.refs_0_, ...), custom_call_target="tpu_custom_call" | custom-call | tf_op jit(solution)/shard_map/pallas_call | solution.py:379
  14.8 0.2 collective-permute-start.1
  14.9 1.4 %collective-permute-done.1.refs_5_ = bf16[432,256]{1,0:T(8,128)(2,1)S(1)} collective-permute-done((bf16[432,256]{1,0:T(8,128)(2,1)S(1)}, bf16[432,256]{1,0:T(8,128)(2,1)S(1)}, u32[]{:S(2)}, u32[]{:S(2)}) %collective-permute-start.1) | collective-permute-done | bytes 221216 | tf_op jit(solution)/shard_map/ppermute | solution.py:471
  16.3 2.9 %all-to-all-done.refs_1_ = bf16[8,16,512]{2,1,0:T(8,128)(2,1)S(1)} async-done(((bf16[8,16,512]{2,1,0:T(8,128)(2,1)}), bf16[8,16,512]{2,1,0:T(8,128)(2,1)S(1)}, u32[]{:S(2)}, u32[]{:S(2)}) %all-to-all-start) | async-done | bytes 131104 | tf_op jit(solution)/shard_map/all_to_all | solution.py:464
  19.2 3.2 %shard_map.157 = (bf16[256,256]{1,0:T(8,128)(2,1)S(1)}, bf16[4,64,256]{2,1,0:T(8,128)(2,1)S(1)}, bf16[3,6,18,16,128]{4,3,2,1,0:T(8,128)(2,1)S(1)}) custom-call(f32[1,128]{1,0:T(1,128)S(1)} %get-tuple-element.22.refs_0_, bf16[8,16,512]{2,1,0:T(8,128)(2,1)S(1)} %all-to-all-done.refs_1_, f32[1,16]{1,0:T(1,128)S(1)} %get-tuple-element.23.refs_2_, ...), custom_call_target="tpu_custom_call" | custom-call | tf_op jit(solution)/shard_map/pallas_call | solution.py:379
  22.4 0.6 %shard_map.160 = bf16[256,256]{1,0:T(8,128)(2,1)S(1)} custom-call(bf16[3,6,18,16,128]{4,3,2,1,0:T(8,128)(2,1)S(1)} %get-tuple-element.31.refs_0_, bf16[27,128,256]{2,1,0:T(8,128)(2,1)S(1)} %get-tuple-element.27.refs_9_.refs_1_), custom_call_target="tpu_custom_call" | custom-call | tf_op jit(solution)/shard_map/pallas_call | solution.py:379
  23.0 0.6 %shard_map.159 = bf16[256,256]{1,0:T(8,128)(2,1)S(1)} custom-call(bf16[3,6,18,16,128]{4,3,2,1,0:T(8,128)(2,1)S(1)} %get-tuple-element.31.refs_0_, bf16[27,128,256]{2,1,0:T(8,128)(2,1)S(1)} %get-tuple-element.27.refs_9_.refs_1_), custom_call_target="tpu_custom_call" | custom-call | tf_op jit(solution)/shard_map/pallas_call | solution.py:379
  23.7 0.1 collective-permute-start.3
  23.8 2.0 %collective-permute-start.4 = (bf16[256,256]{1,0:T(8,128)(2,1)S(1)}, bf16[256,256]{1,0:T(8,128)(2,1)S(1)}, u32[]{:S(2)}, u32[]{:S(2)}) collective-permute-start(bf16[256,256]{1,0:T(8,128)(2,1)S(1)} %shard_map.160), channel_id=1, source_target_pairs={{0,12},{4,8},{8,4},{12,0},{1,13},{5,9},{9,5},{13,1},{2,14},{6,10},... | collective-permute-start | bytes 393224 | tf_op jit(solution)/shard_map/ppermute | solution.py:503
  25.7 1.5 %collective-permute-start.2 = (bf16[256,256]{1,0:T(8,128)(2,1)S(1)}, bf16[256,256]{1,0:T(8,128)(2,1)S(1)}, u32[]{:S(2)}, u32[]{:S(2)}) collective-permute-start(bf16[256,256]{1,0:T(8,128)(2,1)S(1)} %get-tuple-element.32), channel_id=1, source_target_pairs={{0,8},{4,12},{8,0},{12,4},{1,9},{5,13},{9,1},{13,5},{2,10},{6,14},... | collective-permute-start | bytes 393224 | tf_op jit(solution)/shard_map/ppermute | solution.py:503
  27.2 0.6 %shard_map.158.refs_0_ = f32[256,256]{1,0:T(8,128)S(1)} custom-call(bf16[3,6,18,16,128]{4,3,2,1,0:T(8,128)(2,1)S(1)} %get-tuple-element.31.refs_0_, bf16[27,128,256]{2,1,0:T(8,128)(2,1)S(1)} %get-tuple-element.27.refs_9_.refs_1_), custom_call_target="tpu_custom_call" | custom-call | tf_op jit(solution)/shard_map/pallas_call | solution.py:379
  27.9 3.3 %collective-permute-done.3.refs_2_ = bf16[256,256]{1,0:T(8,128)(2,1)S(1)} collective-permute-done((bf16[256,256]{1,0:T(8,128)(2,1)S(1)}, bf16[256,256]{1,0:T(8,128)(2,1)S(1)}, u32[]{:S(2)}, u32[]{:S(2)}) %collective-permute-start.3) | collective-permute-done | bytes 131104 | tf_op jit(solution)/shard_map/ppermute | solution.py:503
  31.2 1.8 %collective-permute-done.4.refs_3_ = bf16[256,256]{1,0:T(8,128)(2,1)S(1)} collective-permute-done((bf16[256,256]{1,0:T(8,128)(2,1)S(1)}, bf16[256,256]{1,0:T(8,128)(2,1)S(1)}, u32[]{:S(2)}, u32[]{:S(2)}) %collective-permute-start.4) | collective-permute-done | bytes 131104 | tf_op jit(solution)/shard_map/ppermute | solution.py:503
  33.0 4.8 %collective-permute-done.2.refs_1_ = bf16[256,256]{1,0:T(8,128)(2,1)S(1)} collective-permute-done((bf16[256,256]{1,0:T(8,128)(2,1)S(1)}, bf16[256,256]{1,0:T(8,128)(2,1)S(1)}, u32[]{:S(2)}, u32[]{:S(2)}) %collective-permute-start.2) | collective-permute-done | bytes 131104 | tf_op jit(solution)/shard_map/ppermute | solution.py:503
  37.7 0.9 %shard_map.161 = bf16[4,16,4,256]{3,2,1,0:T(4,128)(2,1)} custom-call(bf16[4,64,256]{2,1,0:T(8,128)(2,1)S(1)} %get-tuple-element.28.tile, f32[1,256]{1,0:T(1,128)S(1)} %get-tuple-element.29.bias, bf16[64,64]{1,0:T(8,128)(2,1)S(1)} %get-tuple-element.30.order, f32[256,256]{1,0:T(8,128)S(1)} %shard_map.158.refs_0_, ...), custom_call_target="tpu_custom_call" | custom-call | tf_op jit(solution)/shard_map/pallas_call | solution.py:379
Async XLA Ops:
  2.0 1.6 %collective-permute-start = (f32[72,128]{1,0:T(8,128)S(1)}, f32[72,128]{1,0:T(8,128)S(1)}, u32[]{:S(2)}, u32[]{:S(2)}) collective-permute-start(f32[72,128]{1,0:T(8,128)S(1)} %get-tuple-element.19.refs_0_.refs_6_), channel_id=1, source_target_pairs={{0,2},{2,0},{1,3},{3,1},{4,6},{6,4},{5,7},{7,5},{8,10},{10,8},{9,1... | collective-permute-start | bytes 110600 | tf_op jit(solution)/shard_map/ppermute | solution.py:457
  4.7 14.4 %all-to-all-start = ((bf16[8,16,512]{2,1,0:T(8,128)(2,1)}), bf16[8,16,512]{2,1,0:T(8,128)(2,1)S(1)}, u32[]{:S(2)}, u32[]{:S(2)}) async-start(bf16[8,16,512]{2,1,0:T(8,128)(2,1)} %shard_map.155.refs_0_), calls=%async_computation | async-start | bytes 262144 | tf_op jit(solution)/shard_map/all_to_all | solution.py:464
  14.8 1.5 %collective-permute-start.1 = (bf16[432,256]{1,0:T(8,128)(2,1)S(1)}, bf16[432,256]{1,0:T(8,128)(2,1)S(1)}, u32[]{:S(2)}, u32[]{:S(2)}) collective-permute-start(bf16[432,256]{1,0:T(8,128)(2,1)S(1)} %get-tuple-element.25.refs_4_), channel_id=1, source_target_pairs={{0,2},{2,0},{1,3},{3,1},{4,6},{6,4},{5,7},{7,5},{8,10},{10,8},{9,1... | collective-permute-start | bytes 663560 | tf_op jit(solution)/shard_map/ppermute | solution.py:471
  23.7 7.5 %collective-permute-start.3 = (bf16[256,256]{1,0:T(8,128)(2,1)S(1)}, bf16[256,256]{1,0:T(8,128)(2,1)S(1)}, u32[]{:S(2)}, u32[]{:S(2)}) collective-permute-start(bf16[256,256]{1,0:T(8,128)(2,1)S(1)} %shard_map.159), channel_id=1, source_target_pairs={{0,4},{4,0},{8,12},{12,8},{1,5},{5,1},{9,13},{13,9},{2,6},{6,2},{1... | collective-permute-start | bytes 393224 | tf_op jit(solution)/shard_map/ppermute | solution.py:503
  23.8 9.2 %collective-permute-start.4 = (bf16[256,256]{1,0:T(8,128)(2,1)S(1)}, bf16[256,256]{1,0:T(8,128)(2,1)S(1)}, u32[]{:S(2)}, u32[]{:S(2)}) collective-permute-start(bf16[256,256]{1,0:T(8,128)(2,1)S(1)} %shard_map.160), channel_id=1, source_target_pairs={{0,12},{4,8},{8,4},{12,0},{1,13},{5,9},{9,5},{13,1},{2,14},{6,10},... | collective-permute-start | bytes 393224 | tf_op jit(solution)/shard_map/ppermute | solution.py:503
  25.7 12.0 %collective-permute-start.2 = (bf16[256,256]{1,0:T(8,128)(2,1)S(1)}, bf16[256,256]{1,0:T(8,128)(2,1)S(1)}, u32[]{:S(2)}, u32[]{:S(2)}) collective-permute-start(bf16[256,256]{1,0:T(8,128)(2,1)S(1)} %get-tuple-element.32), channel_id=1, source_target_pairs={{0,8},{4,12},{8,0},{12,4},{1,9},{5,13},{9,1},{13,5},{2,10},{6,14},... | collective-permute-start | bytes 393224 | tf_op jit(solution)/shard_map/ppermute | solution.py:503

commit v5 on v4

--- a/solution.py
+++ b/solution.py
@@ -116,8 +116,8 @@
 
 
 def head_kernel(
-    hidden_hbm, modulation_hbm, embed_hbm, weight_hbm, bias_hbm, place_hbm, shift_hbm,
-    out, place, head_bias, hidden, modulation, time_embed, weight, in_bias, arrived, *, parts
+    hidden_hbm, modulation_hbm, embed_hbm, weight_hbm, noisy_hbm, place_hbm, bias_hbm,
+    out, rows, place, bias, hidden, modulation, time_embed, weight, noisy, arrived, *, parts
 ):
     tokens, features = hidden.shape
     outs = weight.shape[0]
@@ -125,12 +125,12 @@
     small = [
         pltpu.make_async_copy(source, target, arrived.at[i])
         for i, (source, target) in enumerate(
-            ((modulation_hbm, modulation), (embed_hbm, time_embed), (bias_hbm, in_bias))
+            ((noisy_hbm, noisy), (modulation_hbm, modulation), (embed_hbm, time_embed))
         )
     ]
     later = [
         pltpu.make_async_copy(source, target, arrived.at[3 + 2 * parts + i])
-        for i, (source, target) in enumerate(((place_hbm, place), (shift_hbm, head_bias)))
+        for i, (source, target) in enumerate(((place_hbm, place), (bias_hbm, bias)))
     ]
     large = []
     for part in range(parts):
@@ -147,6 +147,10 @@
         copy.start()
     for copy in small:
         copy.wait()
+    cells = noisy[...].astype(F32)
+    rows[...] = jnp.concatenate(
+        [cells[f, :, w, :] for f in range(cells.shape[0]) for w in range(cells.shape[2])], axis=0
+    ).T.astype(BF16)
     sums, first, second = 0.0, 0.0, 0.0
     row = lax.broadcasted_iota(jnp.int32, (16, wide), 0)
     for part in range(parts):
@@ -178,28 +182,37 @@
     base = 2 * tokens
     out[tokens : tokens + 1, 0:outs] = sums[base : base + 1] + sums[base + 1 : base + 2]
     out[tokens : tokens + 1, outs : 2 * outs] = sums[base + 2 : base + 3] + sums[base + 3 : base + 4]
-    biases = in_bias.shape[0]
-    out[tokens + 1 : tokens + 1 + biases, :] = in_bias[...]
-    rest = out.shape[0] - tokens - 1 - biases
-    out[tokens + 1 + biases :, :] = jnp.zeros((rest, out.shape[1]), F32)
+    out[tokens + 1 :, :] = jnp.zeros((out.shape[0] - tokens - 1, out.shape[1]), F32)
     for copy in later:
         copy.wait()
 
 
-def stage_kernel(_, *refs, scalar):
-    arrived, refs = refs[-1], refs[:-1]
-    if scalar:
-        refs[-1][...] = jnp.full(refs[-1].shape, refs[0][0], F32)
-        refs = refs[1:-1]
-    count = len(refs) // 2
+def stage_kernel(_, step, weight_hbm, bias_hbm, *refs):
+    bias, arrived, refs = refs[-2], refs[-1], refs[:-2]
+    count = len(refs) // 2 - 1
+    step_row, weight = refs[count : count + 2]
+    taps = weight_hbm.shape[0]
+    pairs = [(weight_hbm, weight.at[0:taps]), (bias_hbm, bias)]
+    pairs += list(zip(refs[:count], refs[count + 2 :], strict=True))
     copies = [
         pltpu.make_async_copy(source, target, arrived.at[i])
-        for i, (source, target) in enumerate(zip(refs[:count], refs[count:], strict=True))
+        for i, (source, target) in enumerate(pairs)
     ]
     for copy in copies:
         copy.start()
-    for copy in copies:
-        copy.wait()
+    step_row[...] = jnp.full(step_row.shape, step[0], F32)
+    copies[1].wait()
+    rest, below = bias[...], weight.shape[0] - taps
+    row = lax.broadcasted_iota(jnp.int32, (below, rest.shape[1]), 0)
+    rows = jnp.zeros(row.shape, F32)
+    for part in range(3):
+        piece = rest.astype(BF16).astype(F32)
+        rows = jnp.where(row == part, piece, rows)
+        rest = rest - piece
+    weight[taps:] = rows.astype(BF16)
+    for i, copy in enumerate(copies):
+        if i != 1:
+            copy.wait()
 
 
 def message_kernel(mine, other, bias, place, noisy, out, *, features, cells, channels):
@@ -265,8 +278,8 @@
 
 
 def norm_kernel(
-    step, messages, std, mean, weight_mine, weight_other, sums_mine, sums_other, gain, conv,
-    partial, tile, normed, rolled, blocks, *, frames, height, width, tokens, k, sections, members
+    step, messages, std, mean, weight_mine, weight_other, gain, conv,
+    partial, tile, normed, rolled, own, *, frames, height, width, k, sections, members
 ):
     mine, side, member = (lax.axis_index(axis) for axis in ("section", "tp", "sp"))
     first_frame = member * frames - 2
@@ -294,33 +307,29 @@
             moved = jnp.where(inside, moved, 0.0)
             first = (3 * b + e) * lat
             rolled[first : first + lat, :] = moved.astype(BF16)
-    bias_rows = [
-        source[tokens + 1 + i : tokens + 2 + i, :]
-        for source in (sums_mine, sums_other)
-        for i in range(per_half)
-    ]
-    gain_row = gain[mine]
+    ones = jnp.ones((weight_mine.shape[0] - 27 * lat, cells), BF16)
+    half_gain = 0.5 * gain[mine]
     edge = lax.broadcasted_iota(jnp.int32, (cells, 1), 0) % height
     zero_column = jnp.zeros((height, deep), BF16)
     for frame in range(frames + 2):
         stacked = jnp.concatenate(
-            [rolled[:, (frame + a) * cells : (frame + a + 1) * cells] for a in range(3)], axis=0
-        )
-        squares = jnp.zeros((cells, deep), F32)
+            [rolled[:, (frame + a) * cells : (frame + a + 1) * cells] for a in range(3)] + [ones],
+            axis=0,
+        )
+        squares, chosen = 0.0, 0.0
         for which, weight in enumerate((weight_mine, weight_other)):
             product = lax.dot_general(
                 stacked, weight[...], (((0,), (0,)), ((), ())), preferred_element_type=F32
             )
             for i in range(per_half):
-                n = which * per_half + i
-                piece = (product[:, i * deep : (i + 1) * deep] + bias_rows[n]).astype(BF16)
-                blocks[n] = piece
-                wide = piece.astype(F32)
-                squares = squares + wide * wide
+                piece = product[:, i * deep : (i + 1) * deep]
+                squares = squares + piece * piece
+                chosen = jnp.where(block == which * per_half + i, piece, chosen)
+            if frame >= 2 and which == 0:
+                own[frame - 2] = product.astype(BF16)
         mean = jnp.sum(squares, axis=1, keepdims=True) / (2 * half)
-        inverse = lax.rsqrt(mean + 1e-06)
-        value = blocks[block].astype(F32) * inverse * gain_row
-        value = value / (1.0 + jnp.exp(-value))
+        value = chosen.astype(BF16).astype(F32) * lax.rsqrt(mean + 1e-06) * half_gain
+        value = value * (1.0 + jnp.tanh(value))
         if frame < 2:
             value = jnp.where(first_frame + frame >= 0, value, 0.0)
         above = jnp.where(edge == 0, 0.0, pltpu.roll(value, 1, axis=0))
@@ -329,10 +338,9 @@
             normed[b, frame, 1 : width + 1] = shifted.astype(BF16).reshape(width, height, deep)
             normed[b, frame, 0] = zero_column
             normed[b, frame, width + 1] = zero_column
-        if frame >= 2:
-            rows = pl.ds(pl.multiple_of(mine * (columns * height), columns * height), columns * height)
-            for i in range(per_half):
-                tile[frame - 2, :, i * deep : (i + 1) * deep] = blocks[i, rows, :]
+    rows = pl.ds(pl.multiple_of(mine * (columns * height), columns * height), columns * height)
+    for frame in range(frames):
+        tile[frame] = own[frame, rows, :]
     partial[...] = conv_tile(normed, conv, (mine ^ k) * columns, columns, frames).astype(BF16)
 
 
@@ -386,16 +394,16 @@
     return constrained
 
 
-def staged(after, *arrays, scalar=None):
-    shapes = [jax.ShapeDtypeStruct(x.shape, x.dtype) for x in arrays]
-    first, specs = [after], vmem(1)
-    if scalar is not None:
-        shapes.append(jax.ShapeDtypeStruct((1, 128), F32))
-        first, specs = first + [scalar], specs + [SMEM]
+def staged(after, step, weight, bias, *arrays):
+    shapes = [
+        jax.ShapeDtypeStruct((1, 128), F32),
+        jax.ShapeDtypeStruct((weight.shape[0] + 16, weight.shape[1]), weight.dtype),
+    ]
+    shapes += [jax.ShapeDtypeStruct(x.shape, x.dtype) for x in arrays]
     return call(
-        lambda *refs: stage_kernel(*refs, scalar=scalar is not None), shapes,
-        specs + [HBM] * len(arrays), [pltpu.SemaphoreType.DMA((len(arrays),))],
-    )(*first, *arrays)
+        stage_kernel, shapes, vmem(1) + [SMEM] + [HBM] * (2 + len(arrays)),
+        [pltpu.VMEM(bias.shape, F32), pltpu.SemaphoreType.DMA((2 + len(arrays),))],
+    )(after, step, weight, bias, *arrays)
 
 
 def token_places(height, width):
@@ -435,20 +443,20 @@
     tokens, local = hidden.shape
     outs = head_weight.shape[1]
     deep = conv_weight.shape[1]
-    per_half = half // deep
     swap = [(i, i ^ 1) for i in range(halves)]
     taps = in_weight.shape[0]
 
-    noisy_rows = jnp.transpose(noisy, (3, 0, 2, 1)).reshape(lat, frames * columns * height)
     parts = 3 if local % (3 * 128) == 0 else 1
     head_in = (
-        hidden, modulation, time_embed.reshape(1, local), head_weight.T,
-        in_bias.reshape(per_half, deep),
+        hidden, modulation, time_embed.reshape(1, local), head_weight.T, noisy,
     )
     kept = (jnp.asarray(token_places(height, width), BF16), head_bias.reshape(1, outs))
-    sums, place, head_bias = call(
+    sums, noisy_rows, place, head_bias = call(
         lambda *refs: head_kernel(*refs, parts=parts),
-        [jax.ShapeDtypeStruct((tokens + 8, 2 * outs), F32)]
+        [
+            jax.ShapeDtypeStruct((tokens + 8, 2 * outs), F32),
+            jax.ShapeDtypeStruct((lat, frames * columns * height), BF16),
+        ]
         + [jax.ShapeDtypeStruct(x.shape, x.dtype) for x in kept],
         [HBM] * (len(head_in) + len(kept)),
         [pltpu.VMEM(x.shape, x.dtype) for x in head_in]
@@ -462,11 +470,11 @@
         jax.ShapeDtypeStruct((sections * members, lat, 2 * cells), BF16), vmem(5),
     )(sums, sums_other, head_bias, place, noisy_rows)
     messages = lax.all_to_all(message, ("section", "sp"), 0, 0)
-    latent_std, latent_mean, conv, weight_mine, gain, order, conv_bias, step = staged(
-        message, latent_std.reshape(1, lat), latent_mean.reshape(1, lat),
-        conv_weight, in_weight.reshape(taps * lat, half),
+    step, weight_mine, latent_std, latent_mean, conv, gain, order, conv_bias = staged(
+        message, step_size, in_weight.reshape(taps * lat, half), in_bias.reshape(1, half),
+        latent_std.reshape(1, lat), latent_mean.reshape(1, lat), conv_weight,
         norm_gain.reshape(sections, 1, deep), jnp.asarray(row_order(height, columns), BF16),
-        conv_bias.reshape(1, half), scalar=step_size,
+        conv_bias.reshape(1, half),
     )
     weight_other = lax.ppermute(weight_mine, "tp", swap)
 
@@ -475,7 +483,7 @@
     partials = {}
     partials[sends[0]], tile, normed = call(
         lambda *refs: norm_kernel(
-            *refs, frames=frames, height=height, width=width, tokens=tokens, k=sends[0],
+            *refs, frames=frames, height=height, width=width, k=sends[0],
             sections=sections, members=members
         ),
         [
@@ -483,14 +491,13 @@
             jax.ShapeDtypeStruct((frames, columns * height, half), BF16),
             jax.ShapeDtypeStruct((3, frames + 2, width + 2, height, deep), BF16),
         ],
-        vmem(10),
+        vmem(8),
         [
             pltpu.VMEM((9 * lat, 2 * frames * cells), BF16),
-            pltpu.VMEM((sections, cells, deep), BF16),
+            pltpu.VMEM((frames, cells, half), BF16),
         ],
     )(
-        step, messages, latent_std, latent_mean, weight_mine, weight_other, sums,
-        sums_other, gain, conv,
+        step, messages, latent_std, latent_mean, weight_mine, weight_other, gain, conv,
     )
     received = {}
     for k in sends + [0]:

time: 39 us -> 38.3 us (0.982)
  local copies, waits for them, and re-layouts: 1.08 us -> 0 us
    all_to_all x1, waiting for transfers between devices: 2.85 us -> 4.59 us  [sectioned_shards(): messages = lax.all_to_all(message, ('section', 'sp'), 0, 0)]
    ppermute x1, waiting for transfers between devices: 1.36 us -> 0.01 us  [sectioned_shards(): weight_other = lax.ppermute(weight_mine, 'tp', swap)]
    transpose x1 -> x0, local copies, waits for them, and re-layouts: 0.96 us -> none  [sectioned_shards(): jnp.transpose(noisy, (3, 0, 2, 1)).reshape(lat, frames * columns * height)]
  transfers between devices with their start and end apart: 6 -> 6, of which waited for: 5 -> 5; matrix products, arithmetic and copies ran while one was open for 3% -> 0% of each run, Pallas kernels for 8% -> 9%
where the time goes in v5:
time: 38.3 us; the launch traced here: 38 us
  waiting for transfers between devices  14.4 us (38%)
  Pallas kernels  11.6 us (30%)
  starting transfers between devices  11.3 us (30%)
  between operations  0.71 us (2%)
    pallas_call x8, Pallas kernels, constrained(): run(*[arg if spec is SMEM else pltpu.with_memory_space_constraint(arg, sp...  11.6 us
    ppermute x3, waiting for transfers between devices, sectioned_shards(): lax.ppermute(partials[k], 'section', [(i, i ^ k) for i in range(sections)])  9.6 us
    all_to_all x1, starting transfers between devices, sectioned_shards(): messages = lax.all_to_all(message, ('section', 'sp'), 0, 0)  7.14 us
    all_to_all x1, waiting for transfers between devices, sectioned_shards(): messages = lax.all_to_all(message, ('section', 'sp'), 0, 0)  4.59 us
    ppermute x3, starting transfers between devices, sectioned_shards(): lax.ppermute(partials[k], 'section', [(i, i ^ k) for i in range(sections)])  3.55 us
  transfers between devices with their start and end apart: 6, of which 5 were waited for; matrix products, arithmetic and copies ran while one was open for 0% of the time, Pallas kernels for 9%

profile of v5, /device:TPU:0, one launch (start us, length us, event | category | flops | bytes accessed | tf_op | source)
XLA Modules:
  0.0 38.0 jit_solution(5630143790613614018)
XLA Ops:
  0.0 2.0 %shard_map.154 = (f32[72,128]{1,0:T(8,128)S(1)}, bf16[16,256]{1,0:T(8,128)(2,1)S(1)}, bf16[64,1024]{1,0:T(8,128)(2,1)S(1)}, f32[1,64]{1,0:T(1,128)S(1)}) custom-call(bf16[64,3072]{1,0:T(8,128)(2,1)} %refs_0_.1, f32[2,3072]{1,0:T(2,128)} %refs_1_.1, f32[1,3072]{1,0:T(1,128)} %bitcast.11, bf16[64,3072]{1,0:T(8,128)(2,1)} %bitcast.9, ...), custom_call_target="tpu_custom_call" | custom-call | tf_op jit(solution)/shard_map/pallas_call | solution.py:387
  2.0 0.6 %collective-permute-start = (f32[72,128]{1,0:T(8,128)S(1)}, f32[72,128]{1,0:T(8,128)S(1)}, u32[]{:S(2)}, u32[]{:S(2)}) collective-permute-start(f32[72,128]{1,0:T(8,128)S(1)} %get-tuple-element.20.refs_0_), channel_id=1, source_target_pairs={{0,2},{2,0},{1,3},{3,1},{4,6},{6,4},{5,7},{7,5},{8,10},{10,8},{9,1... | collective-permute-start | bytes 110600 | tf_op jit(solution)/shard_map/ppermute | solution.py:465
  3.3 0.2 collective-permute-done.refs_1_
  3.5 1.0 %shard_map.155._ = bf16[8,16,512]{2,1,0:T(8,128)(2,1)} custom-call(f32[72,128]{1,0:T(8,128)S(1)} %get-tuple-element.20.refs_0_, f32[72,128]{1,0:T(8,128)S(1)} %collective-permute-done.refs_1_, f32[1,64]{1,0:T(1,128)S(1)} %get-tuple-element.21.refs_2_, bf16[64,1024]{1,0:T(8,128)(2,1)S(1)} %get-tuple-element.22.refs_3_, ...), custom_call_target="tpu_custom_call" | custom-call | tf_op jit(solution)/shard_map/pallas_call | solution.py:387
  4.5 7.1 %all-to-all-start = ((bf16[8,16,512]{2,1,0:T(8,128)(2,1)}), bf16[8,16,512]{2,1,0:T(8,128)(2,1)S(1)}, u32[]{:S(2)}, u32[]{:S(2)}) async-start(bf16[8,16,512]{2,1,0:T(8,128)(2,1)} %shard_map.155._), calls=%async_computation | async-start | bytes 262144 | tf_op jit(solution)/shard_map/all_to_all | solution.py:472
  11.6 2.7 %shard_map.156 = (f32[1,128]{1,0:T(1,128)S(1)}, bf16[448,256]{1,0:T(8,128)(2,1)S(1)}, f32[1,16]{1,0:T(1,128)S(1)}, f32[1,16]{1,0:T(1,128)S(1)}, bf16[27,128,256]...) custom-call(bf16[8,16,512]{2,1,0:T(8,128)(2,1)} %shard_map.155._, ...), custom_call_target="tpu_custom_call" | custom-call | tf_op jit(solution)/shard_map/pallas_call | solution.py:387
  14.3 0.1 collective-permute-start.1
  14.4 4.6 %all-to-all-done.refs_1_ = bf16[8,16,512]{2,1,0:T(8,128)(2,1)S(1)} async-done(((bf16[8,16,512]{2,1,0:T(8,128)(2,1)}), bf16[8,16,512]{2,1,0:T(8,128)(2,1)S(1)}, u32[]{:S(2)}, u32[]{:S(2)}) %all-to-all-start) | async-done | bytes 131104 | tf_op jit(solution)/shard_map/all_to_all | solution.py:472
  19.0 0.0 collective-permute-done.1.refs_5_
  19.0 3.0 %shard_map.157 = (bf16[256,256]{1,0:T(8,128)(2,1)S(1)}, bf16[4,64,256]{2,1,0:T(8,128)(2,1)S(1)}, bf16[3,6,18,16,128]{4,3,2,1,0:T(8,128)(2,1)S(1)}) custom-call(f32[1,128]{1,0:T(1,128)S(1)} %get-tuple-element.24.refs_0_, bf16[8,16,512]{2,1,0:T(8,128)(2,1)S(1)} %all-to-all-done.refs_1_, f32[1,16]{1,0:T(1,128)S(1)} %get-tuple-element.25.refs_2_, ...), custom_call_target="tpu_custom_call" | custom-call | tf_op jit(solution)/shard_map/pallas_call | solution.py:387
  22.0 0.6 %shard_map.160 = bf16[256,256]{1,0:T(8,128)(2,1)S(1)} custom-call(bf16[3,6,18,16,128]{4,3,2,1,0:T(8,128)(2,1)S(1)} %get-tuple-element.33.refs_0_, bf16[27,128,256]{2,1,0:T(8,128)(2,1)S(1)} %get-tuple-element.29.refs_7_.refs_1_), custom_call_target="tpu_custom_call" | custom-call | tf_op jit(solution)/shard_map/pallas_call | solution.py:387
  22.7 0.6 %shard_map.159 = bf16[256,256]{1,0:T(8,128)(2,1)S(1)} custom-call(bf16[3,6,18,16,128]{4,3,2,1,0:T(8,128)(2,1)S(1)} %get-tuple-element.33.refs_0_, bf16[27,128,256]{2,1,0:T(8,128)(2,1)S(1)} %get-tuple-element.29.refs_7_.refs_1_), custom_call_target="tpu_custom_call" | custom-call | tf_op jit(solution)/shard_map/pallas_call | solution.py:387
  23.3 0.1 collective-permute-start.3
  23.4 1.9 %collective-permute-start.4 = (bf16[256,256]{1,0:T(8,128)(2,1)S(1)}, bf16[256,256]{1,0:T(8,128)(2,1)S(1)}, u32[]{:S(2)}, u32[]{:S(2)}) collective-permute-start(bf16[256,256]{1,0:T(8,128)(2,1)S(1)} %shard_map.160), channel_id=1, source_target_pairs={{0,12},{4,8},{8,4},{12,0},{1,13},{5,9},{9,5},{13,1},{2,14},{6,10},... | collective-permute-start | bytes 393224 | tf_op jit(solution)/shard_map/ppermute | solution.py:510
  25.4 1.5 %collective-permute-start.2 = (bf16[256,256]{1,0:T(8,128)(2,1)S(1)}, bf16[256,256]{1,0:T(8,128)(2,1)S(1)}, u32[]{:S(2)}, u32[]{:S(2)}) collective-permute-start(bf16[256,256]{1,0:T(8,128)(2,1)S(1)} %get-tuple-element.34), channel_id=1, source_target_pairs={{0,8},{4,12},{8,0},{12,4},{1,9},{5,13},{9,1},{13,5},{2,10},{6,14},... | collective-permute-start | bytes 393224 | tf_op jit(solution)/shard_map/ppermute | solution.py:510
  26.9 0.6 %shard_map.158.refs_0_ = f32[256,256]{1,0:T(8,128)S(1)} custom-call(bf16[3,6,18,16,128]{4,3,2,1,0:T(8,128)(2,1)S(1)} %get-tuple-element.33.refs_0_, bf16[27,128,256]{2,1,0:T(8,128)(2,1)S(1)} %get-tuple-element.29.refs_7_.refs_1_), custom_call_target="tpu_custom_call" | custom-call | tf_op jit(solution)/shard_map/pallas_call | solution.py:387
  27.5 3.2 %collective-permute-done.3.refs_2_ = bf16[256,256]{1,0:T(8,128)(2,1)S(1)} collective-permute-done((bf16[256,256]{1,0:T(8,128)(2,1)S(1)}, bf16[256,256]{1,0:T(8,128)(2,1)S(1)}, u32[]{:S(2)}, u32[]{:S(2)}) %collective-permute-start.3) | collective-permute-done | bytes 131104 | tf_op jit(solution)/shard_map/ppermute | solution.py:510
  30.7 1.7 %collective-permute-done.4.refs_3_ = bf16[256,256]{1,0:T(8,128)(2,1)S(1)} collective-permute-done((bf16[256,256]{1,0:T(8,128)(2,1)S(1)}, bf16[256,256]{1,0:T(8,128)(2,1)S(1)}, u32[]{:S(2)}, u32[]{:S(2)}) %collective-permute-start.4) | collective-permute-done | bytes 131104 | tf_op jit(solution)/shard_map/ppermute | solution.py:510
  32.4 4.8 %collective-permute-done.2.refs_1_ = bf16[256,256]{1,0:T(8,128)(2,1)S(1)} collective-permute-done((bf16[256,256]{1,0:T(8,128)(2,1)S(1)}, bf16[256,256]{1,0:T(8,128)(2,1)S(1)}, u32[]{:S(2)}, u32[]{:S(2)}) %collective-permute-start.2) | collective-permute-done | bytes 131104 | tf_op jit(solution)/shard_map/ppermute | solution.py:510
  37.2 0.9 %shard_map.161 = bf16[4,16,4,256]{3,2,1,0:T(4,128)(2,1)} custom-call(bf16[4,64,256]{2,1,0:T(8,128)(2,1)S(1)} %get-tuple-element.30.tile, f32[1,256]{1,0:T(1,128)S(1)} %get-tuple-element.31.bias, bf16[64,64]{1,0:T(8,128)(2,1)S(1)} %get-tuple-element.32.order, f32[256,256]{1,0:T(8,128)S(1)} %shard_map.158.refs_0_, ...), custom_call_target="tpu_custom_call" | custom-call | tf_op jit(solution)/shard_map/pallas_call | solution.py:387
Async XLA Ops:
  2.0 1.4 %collective-permute-start = (f32[72,128]{1,0:T(8,128)S(1)}, f32[72,128]{1,0:T(8,128)S(1)}, u32[]{:S(2)}, u32[]{:S(2)}) collective-permute-start(f32[72,128]{1,0:T(8,128)S(1)} %get-tuple-element.20.refs_0_), channel_id=1, source_target_pairs={{0,2},{2,0},{1,3},{3,1},{4,6},{6,4},{5,7},{7,5},{8,10},{10,8},{9,1... | collective-permute-start | bytes 110600 | tf_op jit(solution)/shard_map/ppermute | solution.py:465
  4.5 14.5 %all-to-all-start = ((bf16[8,16,512]{2,1,0:T(8,128)(2,1)}), bf16[8,16,512]{2,1,0:T(8,128)(2,1)S(1)}, u32[]{:S(2)}, u32[]{:S(2)}) async-start(bf16[8,16,512]{2,1,0:T(8,128)(2,1)} %shard_map.155._), calls=%async_computation | async-start | bytes 262144 | tf_op jit(solution)/shard_map/all_to_all | solution.py:472
  14.3 4.7 %collective-permute-start.1 = (bf16[448,256]{1,0:T(8,128)(2,1)S(1)}, bf16[448,256]{1,0:T(8,128)(2,1)S(1)}, u32[]{:S(2)}, u32[]{:S(2)}) collective-permute-start(bf16[448,256]{1,0:T(8,128)(2,1)S(1)} %get-tuple-element.27.refs_4_), channel_id=1, source_target_pairs={{0,2},{2,0},{1,3},{3,1},{4,6},{6,4},{5,7},{7,5},{8,10},{10,8},{9,1... | collective-permute-start | bytes 688136 | tf_op jit(solution)/shard_map/ppermute | solution.py:479
  23.3 7.4 %collective-permute-start.3 = (bf16[256,256]{1,0:T(8,128)(2,1)S(1)}, bf16[256,256]{1,0:T(8,128)(2,1)S(1)}, u32[]{:S(2)}, u32[]{:S(2)}) collective-permute-start(bf16[256,256]{1,0:T(8,128)(2,1)S(1)} %shard_map.159), channel_id=1, source_target_pairs={{0,4},{4,0},{8,12},{12,8},{1,5},{5,1},{9,13},{13,9},{2,6},{6,2},{1... | collective-permute-start | bytes 393224 | tf_op jit(solution)/shard_map/ppermute | solution.py:510
  23.4 9.0 %collective-permute-start.4 = (bf16[256,256]{1,0:T(8,128)(2,1)S(1)}, bf16[256,256]{1,0:T(8,128)(2,1)S(1)}, u32[]{:S(2)}, u32[]{:S(2)}) collective-permute-start(bf16[256,256]{1,0:T(8,128)(2,1)S(1)} %shard_map.160), channel_id=1, source_target_pairs={{0,12},{4,8},{8,4},{12,0},{1,13},{5,9},{9,5},{13,1},{2,14},{6,10},... | collective-permute-start | bytes 393224 | tf_op jit(solution)/shard_map/ppermute | solution.py:510
  25.4 11.8 %collective-permute-start.2 = (bf16[256,256]{1,0:T(8,128)(2,1)S(1)}, bf16[256,256]{1,0:T(8,128)(2,1)S(1)}, u32[]{:S(2)}, u32[]{:S(2)}) collective-permute-start(bf16[256,256]{1,0:T(8,128)(2,1)S(1)} %get-tuple-element.34), channel_id=1, source_target_pairs={{0,8},{4,12},{8,0},{12,4},{1,9},{5,13},{9,1},{13,5},{2,10},{6,14},... | collective-permute-start | bytes 393224 | tf_op jit(solution)/shard_map/ppermute | solution.py:510

commit v6 on v5

--- a/solution.py
+++ b/solution.py
@@ -189,11 +189,11 @@
 
 def stage_kernel(_, step, weight_hbm, bias_hbm, *refs):
     bias, arrived, refs = refs[-2], refs[-1], refs[:-2]
-    count = len(refs) // 2 - 1
-    step_row, weight = refs[count : count + 2]
+    count = (len(refs) - 3) // 2
+    step_row, weight, turned = refs[count : count + 3]
     taps = weight_hbm.shape[0]
     pairs = [(weight_hbm, weight.at[0:taps]), (bias_hbm, bias)]
-    pairs += list(zip(refs[:count], refs[count + 2 :], strict=True))
+    pairs += list(zip(refs[:count], refs[count + 3 :], strict=True))
     copies = [
         pltpu.make_async_copy(source, target, arrived.at[i])
         for i, (source, target) in enumerate(pairs)
@@ -210,9 +210,10 @@
         rows = jnp.where(row == part, piece, rows)
         rest = rest - piece
     weight[taps:] = rows.astype(BF16)
-    for i, copy in enumerate(copies):
-        if i != 1:
-            copy.wait()
+    copies[0].wait()
+    turned[...] = weight[...].T
+    for copy in copies[2:]:
+        copy.wait()
 
 
 def message_kernel(mine, other, bias, place, noisy, out, *, features, cells, channels):
@@ -256,39 +257,45 @@
     return jnp.concatenate(frames, axis=1)
 
 
-def conv_tile(normed, conv, first_column, columns, frames):
+def conv_frames(normed, conv, first_column, columns, frames, a, totals):
     height, deep = normed.shape[3:]
-    taps, _, half = conv.shape
+    half = conv.shape[2]
     size = frames * columns * height
-    total = 0.0
-    for first in range(0, taps, 2):
-        group = range(first, min(first + 2, taps))
+    for i, first in enumerate(range(9 * a, 9 * a + 9, 2)):
+        group = range(first, min(first + 2, 9 * a + 9))
         window = jnp.concatenate(
             [
-                normed[
-                    t // 3 % 3, t // 9 : t // 9 + frames, pl.ds(first_column + t % 3, columns)
-                ].reshape(size, deep)
+                normed[t // 3 % 3, a : a + frames, pl.ds(first_column + t % 3, columns)].reshape(
+                    size, deep
+                )
                 for t in group
             ],
             axis=1,
         )
         weight = conv[first : first + len(group)].reshape(len(group) * deep, half)
-        total = total + jnp.dot(window, weight, preferred_element_type=F32)
-    return total
+        which = (a + i) % 2
+        totals[which] = totals[which] + jnp.dot(window, weight, preferred_element_type=F32)
+
+
+def conv_tile(normed, conv, first_column, columns, frames):
+    totals = [0.0, 0.0]
+    for a in range(3):
+        conv_frames(normed, conv, first_column, columns, frames, a, totals)
+    return totals[0] + totals[1]
 
 
 def norm_kernel(
     step, messages, std, mean, weight_mine, weight_other, gain, conv,
-    partial, tile, normed, rolled, own, *, frames, height, width, k, sections, members
+    partial, normed, rolled, *, frames, height, width, k, sections, members
 ):
     mine, side, member = (lax.axis_index(axis) for axis in ("section", "tp", "sp"))
     first_frame = member * frames - 2
     cells = height * width
     lat = messages.shape[1]
     lanes = 2 * frames * cells
-    half = weight_mine.shape[1]
+    half = weight_mine.shape[0]
     deep = gain.shape[2]
-    columns = tile.shape[1] // height
+    columns = width // sections
     per_half = half // deep
     block = jnp.where((mine // per_half) == side, 0, per_half) + mine % per_half
     rest = (step[:, 0:1], std, mean, sections, members, cells)
@@ -307,28 +314,23 @@
             moved = jnp.where(inside, moved, 0.0)
             first = (3 * b + e) * lat
             rolled[first : first + lat, :] = moved.astype(BF16)
-    ones = jnp.ones((weight_mine.shape[0] - 27 * lat, cells), BF16)
     half_gain = 0.5 * gain[mine]
     edge = lax.broadcasted_iota(jnp.int32, (cells, 1), 0) % height
     zero_column = jnp.zeros((height, deep), BF16)
+    totals = [0.0, 0.0]
     for frame in range(frames + 2):
-        stacked = jnp.concatenate(
-            [rolled[:, (frame + a) * cells : (frame + a + 1) * cells] for a in range(3)] + [ones],
-            axis=0,
-        )
-        squares, chosen = 0.0, 0.0
-        for which, weight in enumerate((weight_mine, weight_other)):
-            product = lax.dot_general(
-                stacked, weight[...], (((0,), (0,)), ((), ())), preferred_element_type=F32
-            )
-            for i in range(per_half):
-                piece = product[:, i * deep : (i + 1) * deep]
-                squares = squares + piece * piece
-                chosen = jnp.where(block == which * per_half + i, piece, chosen)
-            if frame >= 2 and which == 0:
-                own[frame - 2] = product.astype(BF16)
-        mean = jnp.sum(squares, axis=1, keepdims=True) / (2 * half)
-        value = chosen.astype(BF16).astype(F32) * lax.rsqrt(mean + 1e-06) * half_gain
+        stacked = windows(rolled, frame, cells, weight_mine.shape[1])
+        squares, halves = 0.0, []
+        for weight in (weight_mine, weight_other):
+            product = jnp.dot(weight[...], stacked, preferred_element_type=F32)
+            squares = squares + jnp.sum(product * product, axis=0, keepdims=True)
+            halves.append(product)
+        inverse = lax.rsqrt(squares / (2 * half) + 1e-06)
+        chosen = jnp.where(block < per_half, halves[0], halves[1])
+        value = chosen[0:deep]
+        for i in range(1, per_half):
+            value = jnp.where(block % per_half == i, chosen[i * deep : (i + 1) * deep], value)
+        value = (value.astype(BF16).astype(F32) * inverse).T * half_gain
         value = value * (1.0 + jnp.tanh(value))
         if frame < 2:
             value = jnp.where(first_frame + frame >= 0, value, 0.0)
@@ -338,10 +340,10 @@
             normed[b, frame, 1 : width + 1] = shifted.astype(BF16).reshape(width, height, deep)
             normed[b, frame, 0] = zero_column
             normed[b, frame, width + 1] = zero_column
-    rows = pl.ds(pl.multiple_of(mine * (columns * height), columns * height), columns * height)
-    for frame in range(frames):
-        tile[frame] = own[frame, rows, :]
-    partial[...] = conv_tile(normed, conv, (mine ^ k) * columns, columns, frames).astype(BF16)
+        if frame >= frames - 1:
+            first = (mine ^ k) * columns
+            conv_frames(normed, conv, first, columns, frames, frame + 1 - frames, totals)
+    partial[...] = (totals[0] + totals[1]).astype(BF16)
 
 
 def tile_kernel(normed, conv, partial, *, columns, frames, k):
@@ -350,13 +352,38 @@
     )
 
 
-def finish_kernel(tile, bias, order, *refs):
+def windows(rolled, frame, cells, depth):
+    pieces = [rolled[:, (frame + a) * cells : (frame + a + 1) * cells] for a in range(3)]
+    rest = depth - 3 * rolled.shape[0]
+    return jnp.concatenate(pieces + [jnp.ones((rest, cells), BF16)], axis=0)
+
+
+def own_kernel(normed, conv, rolled, weight, bias, total, own, *, columns, frames, cells):
+    mine = lax.axis_index("section")
+    height = normed.shape[3]
+    size = columns * height
+    for frame in range(frames):
+        product = lax.dot_general(
+            windows(rolled, frame + 2, cells, weight.shape[0]), weight[...],
+            (((0,), (0,)), ((), ())), preferred_element_type=F32,
+        )
+        own[frame] = product.astype(BF16)
+    sums = conv_tile(normed, conv, mine * columns, columns, frames)
+    rows = pl.ds(pl.multiple_of(mine * size, size), size)
+    for frame in range(frames):
+        cut = slice(frame * size, (frame + 1) * size)
+        total[cut, :] = sums[cut] + own[frame, rows, :].astype(F32) + bias[...]
+
+
+def finish_kernel(order, first, *refs):
     parts, out = refs[:-1], refs[-1]
-    rows, (height, columns) = tile.shape[1], out.shape[1:3]
-    for frame in range(tile.shape[0]):
-        total = tile[frame].astype(F32) + bias[...]
+    frames, height, columns = out.shape[:3]
+    rows = height * columns
+    for frame in range(frames):
+        cut = slice(frame * rows, (frame + 1) * rows)
+        total = first[cut, :]
         for part in parts:
-            total = total + part[frame * rows : (frame + 1) * rows, :].astype(F32)
+            total = total + part[cut, :].astype(F32)
         placed = jnp.dot(order[...], total.astype(BF16), preferred_element_type=F32)
         out[frame] = placed.reshape(height, columns, -1).astype(BF16)
 
@@ -394,10 +421,15 @@
     return constrained
 
 
+def deep_rows(weight):
+    return (weight.shape[0] + 3 + 127) // 128 * 128
+
+
 def staged(after, step, weight, bias, *arrays):
     shapes = [
         jax.ShapeDtypeStruct((1, 128), F32),
-        jax.ShapeDtypeStruct((weight.shape[0] + 16, weight.shape[1]), weight.dtype),
+        jax.ShapeDtypeStruct((deep_rows(weight), weight.shape[1]), weight.dtype),
+        jax.ShapeDtypeStruct((weight.shape[1], deep_rows(weight)), weight.dtype),
     ]
     shapes += [jax.ShapeDtypeStruct(x.shape, x.dtype) for x in arrays]
     return call(
@@ -446,7 +478,7 @@
     swap = [(i, i ^ 1) for i in range(halves)]
     taps = in_weight.shape[0]
 
-    parts = 3 if local % (3 * 128) == 0 else 1
+    parts = 1
     head_in = (
         hidden, modulation, time_embed.reshape(1, local), head_weight.T, noisy,
     )
@@ -470,7 +502,7 @@
         jax.ShapeDtypeStruct((sections * members, lat, 2 * cells), BF16), vmem(5),
     )(sums, sums_other, head_bias, place, noisy_rows)
     messages = lax.all_to_all(message, ("section", "sp"), 0, 0)
-    step, weight_mine, latent_std, latent_mean, conv, gain, order, conv_bias = staged(
+    step, weight, weight_mine, latent_std, latent_mean, conv, gain, order, conv_bias = staged(
         message, step_size, in_weight.reshape(taps * lat, half), in_bias.reshape(1, half),
         latent_std.reshape(1, lat), latent_mean.reshape(1, lat), conv_weight,
         norm_gain.reshape(sections, 1, deep), jnp.asarray(row_order(height, columns), BF16),
@@ -481,39 +513,35 @@
     size = frames * columns * height
     sends = send_order(sections)
     partials = {}
-    partials[sends[0]], tile, normed = call(
+    partials[sends[0]], normed, rolled = call(
         lambda *refs: norm_kernel(
             *refs, frames=frames, height=height, width=width, k=sends[0],
             sections=sections, members=members
         ),
         [
             jax.ShapeDtypeStruct((size, half), BF16),
-            jax.ShapeDtypeStruct((frames, columns * height, half), BF16),
             jax.ShapeDtypeStruct((3, frames + 2, width + 2, height, deep), BF16),
+            jax.ShapeDtypeStruct((9 * lat, 2 * frames * cells), BF16),
         ],
         vmem(8),
-        [
-            pltpu.VMEM((9 * lat, 2 * frames * cells), BF16),
-            pltpu.VMEM((frames, cells, half), BF16),
-        ],
-    )(
-        step, messages, latent_std, latent_mean, weight_mine, weight_other, gain, conv,
-    )
+    )(step, messages, latent_std, latent_mean, weight_mine, weight_other, gain, conv)
     received = {}
-    for k in sends + [0]:
+    for k in sends:
         if k not in partials:
             partials[k] = call(
                 lambda *refs: tile_kernel(*refs, columns=columns, frames=frames, k=k),
-                jax.ShapeDtypeStruct((size, half), BF16 if k else F32), vmem(2),
+                jax.ShapeDtypeStruct((size, half), BF16), vmem(2),
             )(normed, conv)
-        if k:
-            received[k] = lax.ppermute(
-                partials[k], "section", [(i, i ^ k) for i in range(sections)]
-            )
+        received[k] = lax.ppermute(partials[k], "section", [(i, i ^ k) for i in range(sections)])
+    total = call(
+        lambda *refs: own_kernel(*refs, columns=columns, frames=frames, cells=cells),
+        jax.ShapeDtypeStruct((size, half), F32), vmem(5),
+        [pltpu.VMEM((frames, cells, half), BF16)],
+    )(normed, conv, rolled, weight, conv_bias)
     return call(
         finish_kernel, jax.ShapeDtypeStruct((frames, height, columns, half), BF16),
-        vmem(3 + sections), last=True,
-    )(tile, conv_bias, order, partials[0], *[received[k] for k in sends])
+        vmem(1 + sections), last=True,
+    )(order, total, *[received[k] for k in sends])
 
 
 def sectioned(mesh):

time: 38.3 us -> 38.9 us (1.016)
  blocking collectives: 0 us -> 14.2 us
  starting transfers between devices: 11.3 us -> 4.53 us
  waiting for transfers between devices: 14.4 us -> 9.52 us
  Pallas kernels: 11.6 us -> 9.67 us
    all_to_all x0 -> x1, blocking collectives: none -> 14.2 us  [sectioned_shards(): messages = lax.all_to_all(message, ('section', 'sp'), 0, 0)]
    all_to_all x1 -> x0, starting transfers between devices: 7.14 us -> none  [sectioned_shards(): messages = lax.all_to_all(message, ('section', 'sp'), 0, 0)]
    all_to_all x1 -> x0, waiting for transfers between devices: 4.59 us -> none  [sectioned_shards(): messages = lax.all_to_all(message, ('section', 'sp'), 0, 0)]
    pallas_call x8, Pallas kernels: 11.6 us -> 9.67 us  [constrained(): run(*[arg if spec is SMEM else pltpu.with_memory_space_constraint(arg, sp...]
  transfers between devices with their start and end apart: 6 -> 5, of which waited for: 5 -> 4; matrix products, arithmetic and copies ran while one was open for 0% -> 0% of each run, Pallas kernels for 9% -> 3%
where the time goes in v6:
time: 38.9 us; the launch traced here: 38.7 us
  blocking collectives  14.2 us (37%)
  Pallas kernels  9.67 us (25%)
  waiting for transfers between devices  9.52 us (24%)
  starting transfers between devices  4.53 us (12%)
  between operations  0.71 us (2%)
    all_to_all x1, blocking collectives, sectioned_shards(): messages = lax.all_to_all(message, ('section', 'sp'), 0, 0)  14.2 us
    pallas_call x8, Pallas kernels, constrained(): run(*[arg if spec is SMEM else pltpu.with_memory_space_constraint(arg, sp...  9.67 us
    ppermute x3, waiting for transfers between devices, sectioned_shards(): lax.ppermute(partials[k], 'section', [(i, i ^ k) for i in range(sections)])  9.3 us
    ppermute x3, starting transfers between devices, sectioned_shards(): lax.ppermute(partials[k], 'section', [(i, i ^ k) for i in range(sections)])  3.55 us
  transfers between devices with their start and end apart: 5, of which 4 were waited for; matrix products, arithmetic and copies ran while one was open for 0% of the time, Pallas kernels for 3%

profile of v6, /device:TPU:0, one launch (start us, length us, event | category | flops | bytes accessed | tf_op | source)
XLA Modules:
  0.0 38.7 jit_solution(7833931532884095873)
XLA Ops:
  0.0 1.7 %shard_map.154 = (f32[72,128]{1,0:T(8,128)S(1)}, bf16[16,256]{1,0:T(8,128)(2,1)S(1)}, bf16[64,1024]{1,0:T(8,128)(2,1)S(1)}, f32[1,64]{1,0:T(1,128)S(1)}) custom-call(bf16[64,3072]{1,0:T(8,128)(2,1)} %refs_0_.1, f32[2,3072]{1,0:T(2,128)} %refs_1_.1, f32[1,3072]{1,0:T(1,128)} %bitcast.11, bf16[64,3072]{1,0:T(8,128)(2,1)} %bitcast.9, ...), custom_call_target="tpu_custom_call" | custom-call | tf_op jit(solution)/shard_map/pallas_call | solution.py:414
  1.8 0.6 %collective-permute-start = (f32[72,128]{1,0:T(8,128)S(1)}, f32[72,128]{1,0:T(8,128)S(1)}, u32[]{:S(2)}, u32[]{:S(2)}) collective-permute-start(f32[72,128]{1,0:T(8,128)S(1)} %get-tuple-element.21.refs_0_), channel_id=1, source_target_pairs={{0,2},{2,0},{1,3},{3,1},{4,6},{6,4},{5,7},{7,5},{8,10},{10,8},{9,1... | collective-permute-start | bytes 110600 | tf_op jit(solution)/shard_map/ppermute | solution.py:497
  3.0 0.2 collective-permute-done.refs_1_
  3.2 0.4 shard_map.155._
  3.5 1.7 %shard_map.156 = (f32[1,128]{1,0:T(1,128)S(1)}, bf16[512,256]{1,0:T(8,128)(2,1)S(1)}, bf16[256,512]{1,0:T(8,128)(2,1)S(1)}, f32[1,16]{1,0:T(1,128)S(1)}, f32[1,1...) custom-call(bf16[8,16,512]{2,1,0:T(8,128)(2,1)S(1)} %shard_map.155._, ...), custom_call_target="tpu_custom_call" | custom-call | tf_op jit(solution)/shard_map/pallas_call | solution.py:414
  5.3 0.4 %collective-permute-start.1 = (bf16[256,512]{1,0:T(8,128)(2,1)S(1)}, bf16[256,512]{1,0:T(8,128)(2,1)S(1)}, u32[]{:S(2)}, u32[]{:S(2)}) collective-permute-start(bf16[256,512]{1,0:T(8,128)(2,1)S(1)} %get-tuple-element.29.refs_4_), channel_id=1, source_target_pairs={{0,2},{2,0},{1,3},{3,1},{4,6},{6,4},{5,7},{7,5},{8,10},{10,8},{9,1... | collective-permute-start | bytes 786440 | tf_op jit(solution)/shard_map/ppermute | solution.py:511
  5.7 14.2 %all_to_all.5.refs_1_ = bf16[8,16,512]{2,1,0:T(8,128)(2,1)S(1)} all-to-all(bf16[8,16,512]{2,1,0:T(8,128)(2,1)S(1)} %shard_map.155._), channel_id=1, replica_groups=mesh['groups'=2,'section'=4,'tp'=2,'sp'=2] {'section','sp'}, dimensions={0} | all-to-all | bytes 262144 | tf_op jit(solution)/shard_map/all_to_all | solution.py:504
  19.9 0.0 collective-permute-done.1.refs_5_
  19.9 2.6 %shard_map.157 = (bf16[256,256]{1,0:T(8,128)(2,1)S(1)}, bf16[3,6,18,16,128]{4,3,2,1,0:T(8,128)(2,1)S(1)}, bf16[144,2048]{1,0:T(8,128)(2,1)S(1)}) custom-call(f32[1,128]{1,0:T(1,128)S(1)} %get-tuple-element.26.refs_0_, bf16[8,16,512]{2,1,0:T(8,128)(2,1)S(1)} %all_to_all.5.refs_1_, f32[1,16]{1,0:T(1,128)S(1)} %get-tuple-element.27.refs_2_, ...), custom_call_target="tpu_custom_call" | custom-call | tf_op jit(solution)/shard_map/pallas_call | solution.py:414
  22.6 0.7 %shard_map.160 = bf16[256,256]{1,0:T(8,128)(2,1)S(1)} custom-call(bf16[3,6,18,16,128]{4,3,2,1,0:T(8,128)(2,1)S(1)} %get-tuple-element.32.refs_0_, bf16[27,128,256]{2,1,0:T(8,128)(2,1)S(1)} %get-tuple-element.31.refs_7_.refs_1_), custom_call_target="tpu_custom_call" | custom-call | tf_op jit(solution)/shard_map/pallas_call | solution.py:414
  23.3 0.7 %shard_map.159 = bf16[256,256]{1,0:T(8,128)(2,1)S(1)} custom-call(bf16[3,6,18,16,128]{4,3,2,1,0:T(8,128)(2,1)S(1)} %get-tuple-element.32.refs_0_, bf16[27,128,256]{2,1,0:T(8,128)(2,1)S(1)} %get-tuple-element.31.refs_7_.refs_1_), custom_call_target="tpu_custom_call" | custom-call | tf_op jit(solution)/shard_map/pallas_call | solution.py:414
  23.9 0.1 collective-permute-start.3
  24.0 2.0 %collective-permute-start.4 = (bf16[256,256]{1,0:T(8,128)(2,1)S(1)}, bf16[256,256]{1,0:T(8,128)(2,1)S(1)}, u32[]{:S(2)}, u32[]{:S(2)}) collective-permute-start(bf16[256,256]{1,0:T(8,128)(2,1)S(1)} %shard_map.160), channel_id=1, source_target_pairs={{0,12},{4,8},{8,4},{12,0},{1,13},{5,9},{9,5},{13,1},{2,14},{6,10},... | collective-permute-start | bytes 393224 | tf_op jit(solution)/shard_map/ppermute | solution.py:535
  26.0 1.5 %collective-permute-start.2 = (bf16[256,256]{1,0:T(8,128)(2,1)S(1)}, bf16[256,256]{1,0:T(8,128)(2,1)S(1)}, u32[]{:S(2)}, u32[]{:S(2)}) collective-permute-start(bf16[256,256]{1,0:T(8,128)(2,1)S(1)} %get-tuple-element.36), channel_id=1, source_target_pairs={{0,8},{4,12},{8,0},{12,4},{1,9},{5,13},{9,1},{13,5},{2,10},{6,14},... | collective-permute-start | bytes 393224 | tf_op jit(solution)/shard_map/ppermute | solution.py:535
  27.5 1.0 %shard_map.158.first = f32[256,256]{1,0:T(8,128)S(1)} custom-call(bf16[3,6,18,16,128]{4,3,2,1,0:T(8,128)(2,1)S(1)} %get-tuple-element.32.refs_0_, bf16[27,128,256]{2,1,0:T(8,128)(2,1)S(1)} %get-tuple-element.31.refs_7_.refs_1_, bf16[144,2048]{1,0:T(8,128)(2,1)S(1)} %get-tuple-element.33.refs_2_, bf16[512,256]{1,0:T(8,128)(2,1)S(1)} %get-tuple-element.34.refs_3_, ...), custom_call_target="tpu_custom_call" | custom-call | tf_op jit(solution)/shard_map/pallas_call | solution.py:414
  28.5 2.2 %collective-permute-done.3.refs_1_ = bf16[256,256]{1,0:T(8,128)(2,1)S(1)} collective-permute-done((bf16[256,256]{1,0:T(8,128)(2,1)S(1)}, bf16[256,256]{1,0:T(8,128)(2,1)S(1)}, u32[]{:S(2)}, u32[]{:S(2)}) %collective-permute-start.3) | collective-permute-done | bytes 131104 | tf_op jit(solution)/shard_map/ppermute | solution.py:535
  30.7 2.2 %collective-permute-done.4.refs_2_ = bf16[256,256]{1,0:T(8,128)(2,1)S(1)} collective-permute-done((bf16[256,256]{1,0:T(8,128)(2,1)S(1)}, bf16[256,256]{1,0:T(8,128)(2,1)S(1)}, u32[]{:S(2)}, u32[]{:S(2)}) %collective-permute-start.4) | collective-permute-done | bytes 131104 | tf_op jit(solution)/shard_map/ppermute | solution.py:535
  32.9 4.9 %collective-permute-done.2.refs_0_ = bf16[256,256]{1,0:T(8,128)(2,1)S(1)} collective-permute-done((bf16[256,256]{1,0:T(8,128)(2,1)S(1)}, bf16[256,256]{1,0:T(8,128)(2,1)S(1)}, u32[]{:S(2)}, u32[]{:S(2)}) %collective-permute-start.2) | collective-permute-done | bytes 131104 | tf_op jit(solution)/shard_map/ppermute | solution.py:535
  37.8 0.9 %shard_map.161 = bf16[4,16,4,256]{3,2,1,0:T(4,128)(2,1)} custom-call(bf16[64,64]{1,0:T(8,128)(2,1)S(1)} %get-tuple-element.25.order, f32[256,256]{1,0:T(8,128)S(1)} %shard_map.158.first, bf16[256,256]{1,0:T(8,128)(2,1)S(1)} %collective-permute-done.2.refs_0_, bf16[256,256]{1,0:T(8,128)(2,1)S(1)} %collective-permute-done.3.refs_1_, ...), custom_call_target="tpu_custom_call" | custom-call | tf_op jit(solution)/shard_map/pallas_call | solution.py:414
Async XLA Ops:
  1.8 1.4 %collective-permute-start = (f32[72,128]{1,0:T(8,128)S(1)}, f32[72,128]{1,0:T(8,128)S(1)}, u32[]{:S(2)}, u32[]{:S(2)}) collective-permute-start(f32[72,128]{1,0:T(8,128)S(1)} %get-tuple-element.21.refs_0_), channel_id=1, source_target_pairs={{0,2},{2,0},{1,3},{3,1},{4,6},{6,4},{5,7},{7,5},{8,10},{10,8},{9,1... | collective-permute-start | bytes 110600 | tf_op jit(solution)/shard_map/ppermute | solution.py:497
  5.3 14.6 %collective-permute-start.1 = (bf16[256,512]{1,0:T(8,128)(2,1)S(1)}, bf16[256,512]{1,0:T(8,128)(2,1)S(1)}, u32[]{:S(2)}, u32[]{:S(2)}) collective-permute-start(bf16[256,512]{1,0:T(8,128)(2,1)S(1)} %get-tuple-element.29.refs_4_), channel_id=1, source_target_pairs={{0,2},{2,0},{1,3},{3,1},{4,6},{6,4},{5,7},{7,5},{8,10},{10,8},{9,1... | collective-permute-start | bytes 786440 | tf_op jit(solution)/shard_map/ppermute | solution.py:511
  23.9 6.7 %collective-permute-start.3 = (bf16[256,256]{1,0:T(8,128)(2,1)S(1)}, bf16[256,256]{1,0:T(8,128)(2,1)S(1)}, u32[]{:S(2)}, u32[]{:S(2)}) collective-permute-start(bf16[256,256]{1,0:T(8,128)(2,1)S(1)} %shard_map.159), channel_id=1, source_target_pairs={{0,4},{4,0},{8,12},{12,8},{1,5},{5,1},{9,13},{13,9},{2,6},{6,2},{1... | collective-permute-start | bytes 393224 | tf_op jit(solution)/shard_map/ppermute | solution.py:535
  24.0 8.8 %collective-permute-start.4 = (bf16[256,256]{1,0:T(8,128)(2,1)S(1)}, bf16[256,256]{1,0:T(8,128)(2,1)S(1)}, u32[]{:S(2)}, u32[]{:S(2)}) collective-permute-start(bf16[256,256]{1,0:T(8,128)(2,1)S(1)} %shard_map.160), channel_id=1, source_target_pairs={{0,12},{4,8},{8,4},{12,0},{1,13},{5,9},{9,5},{13,1},{2,14},{6,10},... | collective-permute-start | bytes 393224 | tf_op jit(solution)/shard_map/ppermute | solution.py:535
  26.0 11.8 %collective-permute-start.2 = (bf16[256,256]{1,0:T(8,128)(2,1)S(1)}, bf16[256,256]{1,0:T(8,128)(2,1)S(1)}, u32[]{:S(2)}, u32[]{:S(2)}) collective-permute-start(bf16[256,256]{1,0:T(8,128)(2,1)S(1)} %get-tuple-element.36), channel_id=1, source_target_pairs={{0,8},{4,12},{8,0},{12,4},{1,9},{5,13},{9,1},{13,5},{2,10},{6,14},... | collective-permute-start | bytes 393224 | tf_op jit(solution)/shard_map/ppermute | solution.py:535

commit v7 on v6

--- a/solution.py
+++ b/solution.py
@@ -170,10 +170,12 @@
         extra = jnp.where(row == 1, scale - scale_high, extra)
         extra = jnp.where(row == 2, shift_high, extra)
         extra = jnp.where(row == 3, shift - shift_high, extra).astype(BF16)
-        stacked = jnp.concatenate([high, low, extra], axis=0)
-        sums = sums + lax.dot_general(
-            stacked, weight[:, cut], (((1,), (1,)), ((), ())), preferred_element_type=F32
+        over = (((1,), (1,)), ((), ()))
+        main = lax.dot_general(high, weight[:, cut], over, preferred_element_type=F32)
+        rest = lax.dot_general(
+            jnp.concatenate([low, extra], axis=0), weight[:, cut], over, preferred_element_type=F32
         )
+        sums = sums + jnp.concatenate([main, rest], axis=0)
         first = first + jnp.sum(x, axis=1, keepdims=True)
         second = second + jnp.sum(x * x, axis=1, keepdims=True)
     out[0:tokens, 0:outs] = sums[0:tokens] + sums[tokens : 2 * tokens]
@@ -257,6 +259,12 @@
     return jnp.concatenate(frames, axis=1)
 
 
+def digit(value, base, count):
+    if base & (base - 1) == 0 and count & (count - 1) == 0:
+        return (value >> (base.bit_length() - 1)) & (count - 1)
+    return value // base % count
+
+
 def conv_frames(normed, conv, first_column, columns, frames, a, totals):
     height, deep = normed.shape[3:]
     half = conv.shape[2]
@@ -303,19 +311,20 @@
     earlier = jnp.where(member > 0, earlier, 0.0)
     x = jnp.concatenate([earlier, latents(messages, member, *rest)], axis=1)
     position = lax.broadcasted_iota(jnp.int32, (1, lanes), 1)
-    at_row = position % height
-    at_column = (position // height) % width
+    at_row, at_column = digit(position, 1, height), digit(position, height, width)
+    in_row = {0: at_row > 0, 2: at_row < height - 1}
+    in_column = {0: at_column > 0, 2: at_column < width - 1}
     for b in range(3):
         for e in range(3):
             offset = (e - 1) * height + (b - 1)
             moved = x if offset == 0 else pltpu.roll(x, (-offset) % lanes, axis=1)
-            row, column = at_row + (b - 1), at_column + (e - 1)
-            inside = (row >= 0) & (row < height) & (column >= 0) & (column < width)
-            moved = jnp.where(inside, moved, 0.0)
+            masks = [kind[i] for kind, i in ((in_row, b), (in_column, e)) if i != 1]
+            if masks:
+                moved = jnp.where(masks[0] if len(masks) == 1 else masks[0] & masks[1], moved, 0.0)
             first = (3 * b + e) * lat
             rolled[first : first + lat, :] = moved.astype(BF16)
     half_gain = 0.5 * gain[mine]
-    edge = lax.broadcasted_iota(jnp.int32, (cells, 1), 0) % height
+    edge = digit(lax.broadcasted_iota(jnp.int32, (cells, 1), 0), 1, height)
     zero_column = jnp.zeros((height, deep), BF16)
     totals = [0.0, 0.0]
     for frame in range(frames + 2):
@@ -422,7 +431,7 @@
 
 
 def deep_rows(weight):
-    return (weight.shape[0] + 3 + 127) // 128 * 128
+    return (weight.shape[0] + 3 + 15) // 16 * 16
 
 
 def staged(after, step, weight, bias, *arrays):

time: 38.9 us -> 37.6 us (0.967)
  blocking collectives: 14.2 us -> 0 us
  starting transfers between devices: 4.53 us -> 11.3 us
  waiting for transfers between devices: 9.52 us -> 14.1 us
  Pallas kernels: 9.67 us -> 11.2 us
    all_to_all x1 -> x0, blocking collectives: 14.2 us -> none  [sectioned_shards(): messages = lax.all_to_all(message, ('section', 'sp'), 0, 0)]
    all_to_all x0 -> x1, starting transfers between devices: none -> 7.14 us  [sectioned_shards(): messages = lax.all_to_all(message, ('section', 'sp'), 0, 0)]
    all_to_all x0 -> x1, waiting for transfers between devices: none -> 4.59 us  [sectioned_shards(): messages = lax.all_to_all(message, ('section', 'sp'), 0, 0)]
    pallas_call x8, Pallas kernels: 9.67 us -> 11.2 us  [constrained(): run(*[arg if spec is SMEM else pltpu.with_memory_space_constraint(arg, sp...]
  transfers between devices with their start and end apart: 5 -> 6, of which waited for: 4 -> 5; matrix products, arithmetic and copies ran while one was open for 0% -> 0% of each run, Pallas kernels for 3% -> 10%
where the time goes in v7:
time: 37.6 us; the launch traced here: 37.3 us
  waiting for transfers between devices  14.1 us (38%)
  starting transfers between devices  11.3 us (30%)
  Pallas kernels  11.2 us (30%)
  between operations  0.71 us (2%)
    pallas_call x8, Pallas kernels, constrained(): run(*[arg if spec is SMEM else pltpu.with_memory_space_constraint(arg, sp...  11.2 us
    ppermute x3, waiting for transfers between devices, sectioned_shards(): lax.ppermute(partials[k], 'section', [(i, i ^ k) for i in range(sections)])  9.26 us
    all_to_all x1, starting transfers between devices, sectioned_shards(): messages = lax.all_to_all(message, ('section', 'sp'), 0, 0)  7.14 us
    all_to_all x1, waiting for transfers between devices, sectioned_shards(): messages = lax.all_to_all(message, ('section', 'sp'), 0, 0)  4.59 us
    ppermute x3, starting transfers between devices, sectioned_shards(): lax.ppermute(partials[k], 'section', [(i, i ^ k) for i in range(sections)])  3.55 us
  transfers between devices with their start and end apart: 6, of which 5 were waited for; matrix products, arithmetic and copies ran while one was open for 0% of the time, Pallas kernels for 10%

profile of v7, /device:TPU:0, one launch (start us, length us, event | category | flops | bytes accessed | tf_op | source)
XLA Modules:
  0.0 37.3 jit_solution(7641456000230386325)
XLA Ops:
  0.0 1.8 %shard_map.154 = (f32[72,128]{1,0:T(8,128)S(1)}, bf16[16,256]{1,0:T(8,128)(2,1)S(1)}, bf16[64,1024]{1,0:T(8,128)(2,1)S(1)}, f32[1,64]{1,0:T(1,128)S(1)}) custom-call(bf16[64,3072]{1,0:T(8,128)(2,1)} %refs_0_.1, f32[2,3072]{1,0:T(2,128)} %refs_1_.1, f32[1,3072]{1,0:T(1,128)} %bitcast.11, bf16[64,3072]{1,0:T(8,128)(2,1)} %bitcast.9, ...), custom_call_target="tpu_custom_call" | custom-call | tf_op jit(solution)/shard_map/pallas_call | solution.py:423
  1.8 0.6 %collective-permute-start = (f32[72,128]{1,0:T(8,128)S(1)}, f32[72,128]{1,0:T(8,128)S(1)}, u32[]{:S(2)}, u32[]{:S(2)}) collective-permute-start(f32[72,128]{1,0:T(8,128)S(1)} %get-tuple-element.21.refs_0_), channel_id=1, source_target_pairs={{0,2},{2,0},{1,3},{3,1},{4,6},{6,4},{5,7},{7,5},{8,10},{10,8},{9,1... | collective-permute-start | bytes 110600 | tf_op jit(solution)/shard_map/ppermute | solution.py:506
  3.0 0.2 collective-permute-done.refs_1_
  3.2 1.0 %shard_map.155._ = bf16[8,16,512]{2,1,0:T(8,128)(2,1)} custom-call(f32[72,128]{1,0:T(8,128)S(1)} %get-tuple-element.21.refs_0_, f32[72,128]{1,0:T(8,128)S(1)} %collective-permute-done.refs_1_, f32[1,64]{1,0:T(1,128)S(1)} %get-tuple-element.22.refs_2_, bf16[64,1024]{1,0:T(8,128)(2,1)S(1)} %get-tuple-element.23.refs_3_, ...), custom_call_target="tpu_custom_call" | custom-call | tf_op jit(solution)/shard_map/pallas_call | solution.py:423
  4.2 7.1 %all-to-all-start = ((bf16[8,16,512]{2,1,0:T(8,128)(2,1)}), bf16[8,16,512]{2,1,0:T(8,128)(2,1)S(1)}, u32[]{:S(2)}, u32[]{:S(2)}) async-start(bf16[8,16,512]{2,1,0:T(8,128)(2,1)} %shard_map.155._), calls=%async_computation | async-start | bytes 262144 | tf_op jit(solution)/shard_map/all_to_all | solution.py:513
  11.4 2.7 %shard_map.156 = (f32[1,128]{1,0:T(1,128)S(1)}, bf16[448,256]{1,0:T(8,128)(2,1)S(1)}, bf16[256,448]{1,0:T(8,128)(2,1)S(1)}, f32[1,16]{1,0:T(1,128)S(1)}, f32[1,1...) custom-call(bf16[8,16,512]{2,1,0:T(8,128)(2,1)} %shard_map.155._, ...), custom_call_target="tpu_custom_call" | custom-call | tf_op jit(solution)/shard_map/pallas_call | solution.py:423
  14.0 0.1 collective-permute-start.1
  14.1 4.6 %all-to-all-done.refs_1_ = bf16[8,16,512]{2,1,0:T(8,128)(2,1)S(1)} async-done(((bf16[8,16,512]{2,1,0:T(8,128)(2,1)}), bf16[8,16,512]{2,1,0:T(8,128)(2,1)S(1)}, u32[]{:S(2)}, u32[]{:S(2)}) %all-to-all-start) | async-done | bytes 131104 | tf_op jit(solution)/shard_map/all_to_all | solution.py:513
  18.7 0.0 collective-permute-done.1.refs_5_
  18.7 2.5 %shard_map.157 = (bf16[256,256]{1,0:T(8,128)(2,1)S(1)}, bf16[3,6,18,16,128]{4,3,2,1,0:T(8,128)(2,1)S(1)}, bf16[144,2048]{1,0:T(8,128)(2,1)S(1)}) custom-call(f32[1,128]{1,0:T(1,128)S(1)} %get-tuple-element.26.refs_0_, bf16[8,16,512]{2,1,0:T(8,128)(2,1)S(1)} %all-to-all-done.refs_1_, f32[1,16]{1,0:T(1,128)S(1)} %get-tuple-element.27.refs_2_, ...), custom_call_target="tpu_custom_call" | custom-call | tf_op jit(solution)/shard_map/pallas_call | solution.py:423
  21.3 0.7 %shard_map.160 = bf16[256,256]{1,0:T(8,128)(2,1)S(1)} custom-call(bf16[3,6,18,16,128]{4,3,2,1,0:T(8,128)(2,1)S(1)} %get-tuple-element.32.refs_0_, bf16[27,128,256]{2,1,0:T(8,128)(2,1)S(1)} %get-tuple-element.31.refs_7_.refs_1_), custom_call_target="tpu_custom_call" | custom-call | tf_op jit(solution)/shard_map/pallas_call | solution.py:423
  21.9 0.7 %shard_map.159 = bf16[256,256]{1,0:T(8,128)(2,1)S(1)} custom-call(bf16[3,6,18,16,128]{4,3,2,1,0:T(8,128)(2,1)S(1)} %get-tuple-element.32.refs_0_, bf16[27,128,256]{2,1,0:T(8,128)(2,1)S(1)} %get-tuple-element.31.refs_7_.refs_1_), custom_call_target="tpu_custom_call" | custom-call | tf_op jit(solution)/shard_map/pallas_call | solution.py:423
  22.6 0.1 collective-permute-start.3
  22.7 2.0 %collective-permute-start.4 = (bf16[256,256]{1,0:T(8,128)(2,1)S(1)}, bf16[256,256]{1,0:T(8,128)(2,1)S(1)}, u32[]{:S(2)}, u32[]{:S(2)}) collective-permute-start(bf16[256,256]{1,0:T(8,128)(2,1)S(1)} %shard_map.160), channel_id=1, source_target_pairs={{0,12},{4,8},{8,4},{12,0},{1,13},{5,9},{9,5},{13,1},{2,14},{6,10},... | collective-permute-start | bytes 393224 | tf_op jit(solution)/shard_map/ppermute | solution.py:544
  24.6 1.5 %collective-permute-start.2 = (bf16[256,256]{1,0:T(8,128)(2,1)S(1)}, bf16[256,256]{1,0:T(8,128)(2,1)S(1)}, u32[]{:S(2)}, u32[]{:S(2)}) collective-permute-start(bf16[256,256]{1,0:T(8,128)(2,1)S(1)} %get-tuple-element.36), channel_id=1, source_target_pairs={{0,8},{4,12},{8,0},{12,4},{1,9},{5,13},{9,1},{13,5},{2,10},{6,14},... | collective-permute-start | bytes 393224 | tf_op jit(solution)/shard_map/ppermute | solution.py:544
  26.2 1.0 %shard_map.158.first = f32[256,256]{1,0:T(8,128)S(1)} custom-call(bf16[3,6,18,16,128]{4,3,2,1,0:T(8,128)(2,1)S(1)} %get-tuple-element.32.refs_0_, bf16[27,128,256]{2,1,0:T(8,128)(2,1)S(1)} %get-tuple-element.31.refs_7_.refs_1_, bf16[144,2048]{1,0:T(8,128)(2,1)S(1)} %get-tuple-element.33.refs_2_, bf16[448,256]{1,0:T(8,128)(2,1)S(1)} %get-tuple-element.34.refs_3_, ...), custom_call_target="tpu_custom_call" | custom-call | tf_op jit(solution)/shard_map/pallas_call | solution.py:423
  27.2 3.0 %collective-permute-done.3.refs_1_ = bf16[256,256]{1,0:T(8,128)(2,1)S(1)} collective-permute-done((bf16[256,256]{1,0:T(8,128)(2,1)S(1)}, bf16[256,256]{1,0:T(8,128)(2,1)S(1)}, u32[]{:S(2)}, u32[]{:S(2)}) %collective-permute-start.3) | collective-permute-done | bytes 131104 | tf_op jit(solution)/shard_map/ppermute | solution.py:544
  30.2 1.5 %collective-permute-done.4.refs_2_ = bf16[256,256]{1,0:T(8,128)(2,1)S(1)} collective-permute-done((bf16[256,256]{1,0:T(8,128)(2,1)S(1)}, bf16[256,256]{1,0:T(8,128)(2,1)S(1)}, u32[]{:S(2)}, u32[]{:S(2)}) %collective-permute-start.4) | collective-permute-done | bytes 131104 | tf_op jit(solution)/shard_map/ppermute | solution.py:544
  31.7 4.7 %collective-permute-done.2.refs_0_ = bf16[256,256]{1,0:T(8,128)(2,1)S(1)} collective-permute-done((bf16[256,256]{1,0:T(8,128)(2,1)S(1)}, bf16[256,256]{1,0:T(8,128)(2,1)S(1)}, u32[]{:S(2)}, u32[]{:S(2)}) %collective-permute-start.2) | collective-permute-done | bytes 131104 | tf_op jit(solution)/shard_map/ppermute | solution.py:544
  36.4 0.9 %shard_map.161 = bf16[4,16,4,256]{3,2,1,0:T(4,128)(2,1)} custom-call(bf16[64,64]{1,0:T(8,128)(2,1)S(1)} %get-tuple-element.25.order, f32[256,256]{1,0:T(8,128)S(1)} %shard_map.158.first, bf16[256,256]{1,0:T(8,128)(2,1)S(1)} %collective-permute-done.2.refs_0_, bf16[256,256]{1,0:T(8,128)(2,1)S(1)} %collective-permute-done.3.refs_1_, ...), custom_call_target="tpu_custom_call" | custom-call | tf_op jit(solution)/shard_map/pallas_call | solution.py:423
Async XLA Ops:
  1.8 1.4 %collective-permute-start = (f32[72,128]{1,0:T(8,128)S(1)}, f32[72,128]{1,0:T(8,128)S(1)}, u32[]{:S(2)}, u32[]{:S(2)}) collective-permute-start(f32[72,128]{1,0:T(8,128)S(1)} %get-tuple-element.21.refs_0_), channel_id=1, source_target_pairs={{0,2},{2,0},{1,3},{3,1},{4,6},{6,4},{5,7},{7,5},{8,10},{10,8},{9,1... | collective-permute-start | bytes 110600 | tf_op jit(solution)/shard_map/ppermute | solution.py:506
  4.2 14.5 %all-to-all-start = ((bf16[8,16,512]{2,1,0:T(8,128)(2,1)}), bf16[8,16,512]{2,1,0:T(8,128)(2,1)S(1)}, u32[]{:S(2)}, u32[]{:S(2)}) async-start(bf16[8,16,512]{2,1,0:T(8,128)(2,1)} %shard_map.155._), calls=%async_computation | async-start | bytes 262144 | tf_op jit(solution)/shard_map/all_to_all | solution.py:513
  14.0 4.7 %collective-permute-start.1 = (bf16[256,448]{1,0:T(8,128)(2,1)S(1)}, bf16[256,448]{1,0:T(8,128)(2,1)S(1)}, u32[]{:S(2)}, u32[]{:S(2)}) collective-permute-start(bf16[256,448]{1,0:T(8,128)(2,1)S(1)} %get-tuple-element.29.refs_4_), channel_id=1, source_target_pairs={{0,2},{2,0},{1,3},{3,1},{4,6},{6,4},{5,7},{7,5},{8,10},{10,8},{9,1... | collective-permute-start | bytes 688136 | tf_op jit(solution)/shard_map/ppermute | solution.py:520
  22.6 7.6 %collective-permute-start.3 = (bf16[256,256]{1,0:T(8,128)(2,1)S(1)}, bf16[256,256]{1,0:T(8,128)(2,1)S(1)}, u32[]{:S(2)}, u32[]{:S(2)}) collective-permute-start(bf16[256,256]{1,0:T(8,128)(2,1)S(1)} %shard_map.159), channel_id=1, source_target_pairs={{0,4},{4,0},{8,12},{12,8},{1,5},{5,1},{9,13},{13,9},{2,6},{6,2},{1... | collective-permute-start | bytes 393224 | tf_op jit(solution)/shard_map/ppermute | solution.py:544
  22.7 9.0 %collective-permute-start.4 = (bf16[256,256]{1,0:T(8,128)(2,1)S(1)}, bf16[256,256]{1,0:T(8,128)(2,1)S(1)}, u32[]{:S(2)}, u32[]{:S(2)}) collective-permute-start(bf16[256,256]{1,0:T(8,128)(2,1)S(1)} %shard_map.160), channel_id=1, source_target_pairs={{0,12},{4,8},{8,4},{12,0},{1,13},{5,9},{9,5},{13,1},{2,14},{6,10},... | collective-permute-start | bytes 393224 | tf_op jit(solution)/shard_map/ppermute | solution.py:544
  24.6 11.8 %collective-permute-start.2 = (bf16[256,256]{1,0:T(8,128)(2,1)S(1)}, bf16[256,256]{1,0:T(8,128)(2,1)S(1)}, u32[]{:S(2)}, u32[]{:S(2)}) collective-permute-start(bf16[256,256]{1,0:T(8,128)(2,1)S(1)} %get-tuple-element.36), channel_id=1, source_target_pairs={{0,8},{4,12},{8,0},{12,4},{1,9},{5,13},{9,1},{13,5},{2,10},{6,14},... | collective-permute-start | bytes 393224 | tf_op jit(solution)/shard_map/ppermute | solution.py:544
